TPU v7x, 512 devices: a whole 4x4x16 slice. The times are simulated.
512 devices in a mesh: dom: 64 (over z, x), sub: 8 (over y, core).
Axes of the slice: x: 4, y: 4, z: 16, core: 2. Of those that a mesh axis runs over, the one named last changes fastest.
Arguments:
- jac_blocks: bfloat16 [6144, 6, 128, 128], P(('dom', 'sub')), may hold values from -0.06717514 to 0.06717514
- block_cols: int32 [6144, 6], P(('dom', 'sub')), may hold values from 0 to 19, as said below
- precond: float32 [6144, 36, 128], P(('dom', 'sub')), may hold values from -0.3 to 0.3
- right_side: float32 [6144, 48, 128], P(('dom', 'sub')), may hold values from -6 to 6
- halo_rows: int32 [2048, 2], P(('dom', 'sub')), may hold values from 0 to 11
- surface_tile: int32 [4096], P(('dom', 'sub')), may hold values from 0 to 11
- surface_block: int32 [4096], P(('dom', 'sub')), may hold values from 0 to 31
- surface_count: int32 [512], P(('dom', 'sub')), may hold values from 0 to 8, as said below
- surface_residual_derivative: float32 [4096, 18, 128], P(('dom', 'sub')), may hold values from -6 to 6
- lattice_bernstein_weights: bfloat16 [4096, 128, 128], P(('dom', 'sub')), may hold values from 0 to 0.03125
Outputs:
- adjoint: float32 [6144, 48, 128], P(('dom', 'sub'))
- design_grad: float32 [2, 32, 24, 128], P(None, 'sub')
Inputs may be any that keep to these rules, and one draw needn't show every extreme that they name: `block_cols`: entries below 12 name the partition's own tiles; entry 12 + k * 2 + h names halo tile h of neighbour k. `surface_count`: slots at and beyond the count are empty; some partition has all 8 slots live.
All inputs are finite; a program needn't handle non-finite values.
Results may differ from a plain program's by a relative error of at most 0.0055.
Values may be sent and summed in bfloat16 or wider, within the bound.
No kernel may reach another device: no remote copies, remote signals or barrier semaphores. Data moves between devices by JAX's collectives and lax.ppermute only.
A program may use at most 64 MiB of HBM per device.

v0:
```python
import math

import jax
import jax.numpy as jnp
from jax import lax
from jax.sharding import PartitionSpec as P

NOBJ = 8
NVAR = 6
FB_DEV = 4
OUTER = 2
INNER = 5


OFFSETS = (1, -1, 2, -2)
RELAXATION = 0.7


def from_behind(value, axis, steps):
    count = lax.axis_size(axis)
    pairs = [(source, (source + steps) % count) for source in range(count)]
    return lax.ppermute(value, axis, pairs)


def variable_mix(blending_factor, residual):
    tile_count = residual.shape[0]
    cell_count = residual.shape[-1]
    residual_split = residual.reshape(tile_count, NOBJ, NVAR, cell_count)
    mixing_split = blending_factor.reshape(tile_count, NVAR, NVAR, cell_count)
    mixed = jnp.sum(mixing_split[:, None, :, :, :] * residual_split[:, :, None, :, :], axis=3)
    return mixed.reshape(tile_count, NOBJ * NVAR, cell_count)


def design_partial(
    adjoint,
    surface_tile,
    surface_block,
    surface_count,
    surface_residual_derivative,
    lattice_bernstein_weights,
):
    slot_count = surface_tile.shape[0]
    cell_count = adjoint.shape[-1]
    block_total = FB_DEV * lax.axis_size("sub")
    selected = adjoint[surface_tile]
    weights_split = surface_residual_derivative.reshape(slot_count, 1, NVAR, 3, cell_count)
    sensitivity = jnp.sum(
        selected.reshape(slot_count, NOBJ, NVAR, 1, cell_count) * weights_split, axis=2
    )
    alive = (jnp.arange(slot_count, dtype=jnp.int32) < surface_count[0]).astype(jnp.float32)
    rounded = (
        (sensitivity * alive[:, None, None, None])
        .reshape(slot_count, NOBJ * 3, cell_count)
        .astype(jnp.bfloat16)
    )
    projected = jnp.einsum(
        "uoc,upc->uop", rounded, lattice_bernstein_weights, preferred_element_type=jnp.float32
    )
    selector = (surface_block[:, None] == jnp.arange(block_total, dtype=jnp.int32)[None, :]).astype(
        jnp.float32
    )
    return jnp.einsum("ub,uop->bop", selector, projected, precision=lax.Precision.HIGHEST)


def per_device(
    jac_blocks,
    block_cols,
    precond,
    right_side,
    halo_rows,
    surface_tile,
    surface_block,
    surface_count,
    surface_residual_derivative,
    lattice_bernstein_weights,
):
    slot_count = surface_tile.shape[0]
    scaling = math.sqrt(FB_DEV / (slot_count * lax.axis_size("dom")))
    adjoint = jnp.zeros_like(right_side)
    gradients = []
    for outer_index in range(OUTER):
        for sweep_index in range(INNER):
            rounded = adjoint.astype(jnp.bfloat16)
            halo_tiles = []
            for position, offset in enumerate(OFFSETS):
                neighbour = from_behind(rounded, "dom", offset)
                halo_tiles.append(neighbour[halo_rows[position]])
            extended = jnp.concatenate([rounded] + halo_tiles, axis=0)
            picked = extended[block_cols]
            coupled = adjoint + jnp.einsum(
                "tbor,tbrc->toc", picked, jac_blocks, preferred_element_type=jnp.float32
            )
            residual = right_side - coupled
            adjoint = adjoint + RELAXATION * residual + variable_mix(precond, residual)
        partial_sum = design_partial(
            adjoint,
            surface_tile,
            surface_block,
            surface_count,
            surface_residual_derivative,
            lattice_bernstein_weights,
        )
        summed = lax.psum(partial_sum, ("dom", "sub"))
        fraction_part = lax.dynamic_slice_in_dim(summed, lax.axis_index("sub") * FB_DEV, FB_DEV, 0)
        gradients.append(fraction_part * scaling)
    return (adjoint, jnp.stack(gradients, axis=0))


def solution(mesh):
    in_specs = (
        P(("dom", "sub"), None, None, None),
        P(("dom", "sub"), None),
        P(("dom", "sub"), None, None),
        P(("dom", "sub"), None, None),
        P(("dom", "sub"), None),
        P(("dom", "sub")),
        P(("dom", "sub")),
        P(("dom", "sub")),
        P(("dom", "sub"), None, None),
        P(("dom", "sub"), None, None),
    )
    out_specs = (P(("dom", "sub"), None, None), P(None, "sub", None, None))
    return jax.shard_map(
        per_device, mesh=mesh, in_specs=in_specs, out_specs=out_specs, check_vma=False
    )
```

profile of v0, /device:TPU:2, one launch (start us, length us, event | category | flops | bytes accessed | tf_op | source)
XLA Modules:
  0.0 867.9 jit_solution(3967326572669578691)
XLA Ops:
  7.3 3.5 collective-permute-start
  10.8 6.3 collective-permute-start.1
  17.1 1.9 collective-permute-start.2
  19.1 9.1 %collective-permute-start.3 = (bf16[12,48,128]{2,1,0:T(8,128)(2,1)S(1)}, bf16[12,48,128]{2,1,0:T(8,128)(2,1)S(1)}, u32[]{:S(2)}, u32[]{:S(2)}) collective-permute-start(bf16[12,48,128]{2,1,0:T(8,128)(2,1)S(1)} %broadcast_in_dim.6), channel_id=1, source_target_pairs={{0,496},{8,504},{16,0},{24,8},{32,16},{40,24},{48,32},{56,40},{64,... | collective-permute-start | bytes 442376 | tf_op jit(solution)/shard_map/ppermute | solution.py:22
  44.3 2.5 collective-permute-start.4
  46.8 6.1 collective-permute-start.5
  52.9 1.9 collective-permute-start.6
  54.8 7.5 collective-permute-start.7
  62.4 2.2 gather_fusion.5
  65.9 2.1 gather_fusion.6
  69.3 2.1 gather_fusion.7
  72.8 2.1 gather_fusion.8
  76.2 2.6 gather_fusion.9
  78.8 2.5 fusion.17
  86.8 1.9 constant_dynamic-update-slice_fusion.14
  88.7 3.2 collective-permute-start.8
  91.9 6.1 collective-permute-start.9
  98.0 1.9 collective-permute-start.10
  99.9 7.5 collective-permute-start.11
  115.0 2.6 gather_fusion.14
  117.6 2.4 fusion.15
  125.6 1.9 constant_dynamic-update-slice_fusion.19
  127.5 3.2 collective-permute-start.12
  130.7 6.1 collective-permute-start.13
  136.8 1.9 collective-permute-start.14
  138.7 7.5 collective-permute-start.15
  154.0 2.4 fusion.13
  162.0 1.9 constant_dynamic-update-slice_fusion.24
  163.8 3.2 collective-permute-start.16
  167.0 6.1 collective-permute-start.17
  173.1 1.9 collective-permute-start.18
  175.1 7.5 collective-permute-start.19
  190.4 2.5 fusion.11
  194.9 1.9 constant_dynamic-update-slice_fusion.29
  196.8 3.1 collective-permute-start.20
  199.8 6.1 collective-permute-start.21
  205.9 1.9 collective-permute-start.22
  207.9 7.5 collective-permute-start.23
  229.6 1.9 constant_dynamic-update-slice_fusion.34
  231.4 3.1 collective-permute-start.24
  234.5 6.1 collective-permute-start.25
  240.6 1.9 collective-permute-start.26
  242.5 7.7 collective-permute-start.27
  258.0 1.8 fusion.7
  262.7 1.7 reshape.180
  264.5 2.0 constant_dynamic-update-slice_fusion.39
  266.4 3.1 collective-permute-start.28
  269.5 6.1 collective-permute-start.29
  275.6 1.9 collective-permute-start.30
  277.5 7.5 collective-permute-start.31
  292.8 1.8 fusion.5
  297.5 1.7 reshape.181
  299.3 2.0 constant_dynamic-update-slice_fusion.44
  301.3 3.1 collective-permute-start.32
  304.3 6.1 collective-permute-start.33
  311.6 1.9 collective-permute-start.34
  313.5 7.5 collective-permute-start.35
  328.8 1.8 fusion.3
  335.3 2.0 constant_dynamic-update-slice_fusion.49
  337.2 3.1 collective-permute-start.36
  341.6 6.1 collective-permute-start.37
  352.9 1.9 collective-permute-start.38
  354.8 7.5 collective-permute-start.39
  380.8 478.6 %all-reduce.3.cloned.1.call-done = (f32[32,24,128]{2,0,1:T(8,128)}, f32[32,24,128]{2,0,1:T(8,128)}) async-done(((f32[32,24,128]{2,0,1:T(8,128)}, f32[32,24,128]{2,0,1:T(8,128)}), (f32[32,24,128]{2,0,1:T(8,128)}, f32[32,24,128]{2,0,1:T(8,128)})) %all-reduce.3.cloned.1.call-update) | async-done | bytes 786448 | tf_op jit(solution)/shard_map/psum | solution.py:103
  (248 shorter events, 137.6 us)
Async XLA Ops:
  7.2 30.8 %copy-start = (bf16[12,6,128,128]{3,2,1,0:T(8,128)(2,1)S(1)}, bf16[12,6,128,128]{3,2,1,0:T(8,128)(2,1)}, u32[]{:S(2)}) copy-start(bf16[12,6,128,128]{3,2,1,0:T(8,128)(2,1)} %param.10) | copy-start | bytes 7077892
  7.2 30.7 %copy-start.1 = (f32[12,48,128]{2,1,0:T(8,128)S(1)}, f32[12,48,128]{2,1,0:T(8,128)}, u32[]{:S(2)}) copy-start(f32[12,48,128]{2,1,0:T(8,128)} %param.13) | copy-start | bytes 884740
  7.2 852.2 %all-reduce.3.cloned.1.call-start = ((), (), s32[]{:S(2)}) async-start(), calls=%async_computation | async-start | bytes 1572864 | tf_op jit(solution)/shard_map/psum | solution.py:103
  7.3 23.9 %collective-permute-start = (bf16[12,48,128]{2,1,0:T(8,128)(2,1)S(1)}, bf16[12,48,128]{2,1,0:T(8,128)(2,1)}, u32[]{:S(2)}, u32[]{:S(2)}) collective-permute-start(bf16[12,48,128]{2,1,0:T(8,128)(2,1)S(1)} %broadcast_in_dim.6), channel_id=1, source_target_pairs={{0,8},{8,16},{16,24},{24,32},{32,40},{40,48},{48,56},{56,64},{64,7... | collective-permute-start | bytes 442376 | tf_op jit(solution)/shard_map/ppermute | solution.py:22
  10.8 21.9 %collective-permute-start.1 = (bf16[12,48,128]{2,1,0:T(8,128)(2,1)S(1)}, bf16[12,48,128]{2,1,0:T(8,128)(2,1)}, u32[]{:S(2)}, u32[]{:S(2)}) collective-permute-start(bf16[12,48,128]{2,1,0:T(8,128)(2,1)S(1)} %broadcast_in_dim.6), channel_id=1, source_target_pairs={{0,504},{8,0},{16,8},{24,16},{32,24},{40,32},{48,40},{56,48},{64,5... | collective-permute-start | bytes 442376 | tf_op jit(solution)/shard_map/ppermute | solution.py:22
  17.1 17.1 %collective-permute-start.2 = (bf16[12,48,128]{2,1,0:T(8,128)(2,1)S(1)}, bf16[12,48,128]{2,1,0:T(8,128)(2,1)}, u32[]{:S(2)}, u32[]{:S(2)}) collective-permute-start(bf16[12,48,128]{2,1,0:T(8,128)(2,1)S(1)} %broadcast_in_dim.6), channel_id=1, source_target_pairs={{0,16},{8,24},{16,32},{24,40},{32,48},{40,56},{48,64},{56,72},{64,... | collective-permute-start | bytes 442376 | tf_op jit(solution)/shard_map/ppermute | solution.py:22
  19.1 16.6 %collective-permute-start.3 = (bf16[12,48,128]{2,1,0:T(8,128)(2,1)S(1)}, bf16[12,48,128]{2,1,0:T(8,128)(2,1)S(1)}, u32[]{:S(2)}, u32[]{:S(2)}) collective-permute-start(bf16[12,48,128]{2,1,0:T(8,128)(2,1)S(1)} %broadcast_in_dim.6), channel_id=1, source_target_pairs={{0,496},{8,504},{16,0},{24,8},{32,16},{40,24},{48,32},{56,40},{64,... | collective-permute-start | bytes 442376 | tf_op jit(solution)/shard_map/ppermute | solution.py:22
  29.3 10.4 %copy-start.12 = (s32[1024]{0:T(1024)}, s32[1024]{0:T(1024)S(1)}, u32[]{:S(2)}) copy-start(s32[1024]{0:T(1024)S(1)} %pad_clamp_fusion.5) | copy-start | bytes 12292
  44.3 18.1 %collective-permute-start.4 = (bf16[12,48,128]{2,1,0:T(8,128)(2,1)}, bf16[12,48,128]{2,1,0:T(8,128)(2,1)}, u32[]{:S(2)}, u32[]{:S(2)}) collective-permute-start(bf16[12,48,128]{2,1,0:T(8,128)(2,1)} %get-tuple-element.41), channel_id=1, source_target_pairs={{0,8},{8,16},{16,24},{24,32},{32,40},{40,48},{48,56},{56,64},{64,7... | collective-permute-start | bytes 442376 | tf_op jit(solution)/shard_map/ppermute | solution.py:22
  46.8 19.1 %collective-permute-start.5 = (bf16[12,48,128]{2,1,0:T(8,128)(2,1)}, bf16[12,48,128]{2,1,0:T(8,128)(2,1)}, u32[]{:S(2)}, u32[]{:S(2)}) collective-permute-start(bf16[12,48,128]{2,1,0:T(8,128)(2,1)} %get-tuple-element.41), channel_id=1, source_target_pairs={{0,504},{8,0},{16,8},{24,16},{32,24},{40,32},{48,40},{56,48},{64,5... | collective-permute-start | bytes 442376 | tf_op jit(solution)/shard_map/ppermute | solution.py:22
  52.9 16.4 %collective-permute-start.6 = (bf16[12,48,128]{2,1,0:T(8,128)(2,1)}, bf16[12,48,128]{2,1,0:T(8,128)(2,1)}, u32[]{:S(2)}, u32[]{:S(2)}) collective-permute-start(bf16[12,48,128]{2,1,0:T(8,128)(2,1)} %get-tuple-element.41), channel_id=1, source_target_pairs={{0,16},{8,24},{16,32},{24,40},{32,48},{40,56},{48,64},{56,72},{64,... | collective-permute-start | bytes 442376 | tf_op jit(solution)/shard_map/ppermute | solution.py:22
  54.8 17.9 %collective-permute-start.7 = (bf16[12,48,128]{2,1,0:T(8,128)(2,1)}, bf16[12,48,128]{2,1,0:T(8,128)(2,1)}, u32[]{:S(2)}, u32[]{:S(2)}) collective-permute-start(bf16[12,48,128]{2,1,0:T(8,128)(2,1)} %get-tuple-element.41), channel_id=1, source_target_pairs={{0,496},{8,504},{16,0},{24,8},{32,16},{40,24},{48,32},{56,40},{64,... | collective-permute-start | bytes 442376 | tf_op jit(solution)/shard_map/ppermute | solution.py:22
  88.7 28.9 %copy-start.2 = (f32[12,48,128]{2,1,0:T(8,128)S(1)}, f32[12,48,128]{2,1,0:T(8,128)}, u32[]{:S(2)}) copy-start(f32[12,48,128]{2,1,0:T(8,128)} %get-tuple-element.39) | copy-start | bytes 884740
  88.7 18.8 %collective-permute-start.8 = (bf16[12,48,128]{2,1,0:T(8,128)(2,1)}, bf16[12,48,128]{2,1,0:T(8,128)(2,1)}, u32[]{:S(2)}, u32[]{:S(2)}) collective-permute-start(bf16[12,48,128]{2,1,0:T(8,128)(2,1)} %get-tuple-element.38), channel_id=1, source_target_pairs={{0,8},{8,16},{16,24},{24,32},{32,40},{40,48},{48,56},{56,64},{64,7... | collective-permute-start | bytes 442376 | tf_op jit(solution)/shard_map/ppermute | solution.py:22
  91.9 17.8 %collective-permute-start.9 = (bf16[12,48,128]{2,1,0:T(8,128)(2,1)}, bf16[12,48,128]{2,1,0:T(8,128)(2,1)}, u32[]{:S(2)}, u32[]{:S(2)}) collective-permute-start(bf16[12,48,128]{2,1,0:T(8,128)(2,1)} %get-tuple-element.38), channel_id=1, source_target_pairs={{0,504},{8,0},{16,8},{24,16},{32,24},{40,32},{48,40},{56,48},{64,5... | collective-permute-start | bytes 442376 | tf_op jit(solution)/shard_map/ppermute | solution.py:22
  98.0 13.8 %collective-permute-start.10 = (bf16[12,48,128]{2,1,0:T(8,128)(2,1)}, bf16[12,48,128]{2,1,0:T(8,128)(2,1)}, u32[]{:S(2)}, u32[]{:S(2)}) collective-permute-start(bf16[12,48,128]{2,1,0:T(8,128)(2,1)} %get-tuple-element.38), channel_id=1, source_target_pairs={{0,16},{8,24},{16,32},{24,40},{32,48},{40,56},{48,64},{56,72},{64,... | collective-permute-start | bytes 442376 | tf_op jit(solution)/shard_map/ppermute | solution.py:22
  99.9 13.9 %collective-permute-start.11 = (bf16[12,48,128]{2,1,0:T(8,128)(2,1)}, bf16[12,48,128]{2,1,0:T(8,128)(2,1)S(1)}, u32[]{:S(2)}, u32[]{:S(2)}) collective-permute-start(bf16[12,48,128]{2,1,0:T(8,128)(2,1)} %get-tuple-element.38), channel_id=1, source_target_pairs={{0,496},{8,504},{16,0},{24,8},{32,16},{40,24},{48,32},{56,40},{64,... | collective-permute-start | bytes 442376 | tf_op jit(solution)/shard_map/ppermute | solution.py:22
  127.5 26.5 %copy-start.4 = (f32[12,48,128]{2,1,0:T(8,128)S(1)}, f32[12,48,128]{2,1,0:T(8,128)}, u32[]{:S(2)}) copy-start(f32[12,48,128]{2,1,0:T(8,128)} %get-tuple-element.36) | copy-start | bytes 884740
  127.5 18.8 %collective-permute-start.12 = (bf16[12,48,128]{2,1,0:T(8,128)(2,1)}, bf16[12,48,128]{2,1,0:T(8,128)(2,1)}, u32[]{:S(2)}, u32[]{:S(2)}) collective-permute-start(bf16[12,48,128]{2,1,0:T(8,128)(2,1)} %get-tuple-element.35), channel_id=1, source_target_pairs={{0,8},{8,16},{16,24},{24,32},{32,40},{40,48},{48,56},{56,64},{64,7... | collective-permute-start | bytes 442376 | tf_op jit(solution)/shard_map/ppermute | solution.py:22
  130.7 17.2 %collective-permute-start.13 = (bf16[12,48,128]{2,1,0:T(8,128)(2,1)}, bf16[12,48,128]{2,1,0:T(8,128)(2,1)}, u32[]{:S(2)}, u32[]{:S(2)}) collective-permute-start(bf16[12,48,128]{2,1,0:T(8,128)(2,1)} %get-tuple-element.35), channel_id=1, source_target_pairs={{0,504},{8,0},{16,8},{24,16},{32,24},{40,32},{48,40},{56,48},{64,5... | collective-permute-start | bytes 442376 | tf_op jit(solution)/shard_map/ppermute | solution.py:22
  136.8 12.6 %collective-permute-start.14 = (bf16[12,48,128]{2,1,0:T(8,128)(2,1)}, bf16[12,48,128]{2,1,0:T(8,128)(2,1)}, u32[]{:S(2)}, u32[]{:S(2)}) collective-permute-start(bf16[12,48,128]{2,1,0:T(8,128)(2,1)} %get-tuple-element.35), channel_id=1, source_target_pairs={{0,16},{8,24},{16,32},{24,40},{32,48},{40,56},{48,64},{56,72},{64,... | collective-permute-start | bytes 442376 | tf_op jit(solution)/shard_map/ppermute | solution.py:22
  138.7 12.2 %collective-permute-start.15 = (bf16[12,48,128]{2,1,0:T(8,128)(2,1)}, bf16[12,48,128]{2,1,0:T(8,128)(2,1)}, u32[]{:S(2)}, u32[]{:S(2)}) collective-permute-start(bf16[12,48,128]{2,1,0:T(8,128)(2,1)} %get-tuple-element.35), channel_id=1, source_target_pairs={{0,496},{8,504},{16,0},{24,8},{32,16},{40,24},{48,32},{56,40},{64,... | collective-permute-start | bytes 442376 | tf_op jit(solution)/shard_map/ppermute | solution.py:22
  163.8 26.5 %copy-start.5 = (f32[12,48,128]{2,1,0:T(8,128)S(1)}, f32[12,48,128]{2,1,0:T(8,128)}, u32[]{:S(2)}) copy-start(f32[12,48,128]{2,1,0:T(8,128)} %get-tuple-element.33) | copy-start | bytes 884740
  163.8 18.8 %collective-permute-start.16 = (bf16[12,48,128]{2,1,0:T(8,128)(2,1)}, bf16[12,48,128]{2,1,0:T(8,128)(2,1)}, u32[]{:S(2)}, u32[]{:S(2)}) collective-permute-start(bf16[12,48,128]{2,1,0:T(8,128)(2,1)} %get-tuple-element.32), channel_id=1, source_target_pairs={{0,8},{8,16},{16,24},{24,32},{32,40},{40,48},{48,56},{56,64},{64,7... | collective-permute-start | bytes 442376 | tf_op jit(solution)/shard_map/ppermute | solution.py:22
  167.0 17.2 %collective-permute-start.17 = (bf16[12,48,128]{2,1,0:T(8,128)(2,1)}, bf16[12,48,128]{2,1,0:T(8,128)(2,1)}, u32[]{:S(2)}, u32[]{:S(2)}) collective-permute-start(bf16[12,48,128]{2,1,0:T(8,128)(2,1)} %get-tuple-element.32), channel_id=1, source_target_pairs={{0,504},{8,0},{16,8},{24,16},{32,24},{40,32},{48,40},{56,48},{64,5... | collective-permute-start | bytes 442376 | tf_op jit(solution)/shard_map/ppermute | solution.py:22
  173.1 12.6 %collective-permute-start.18 = (bf16[12,48,128]{2,1,0:T(8,128)(2,1)}, bf16[12,48,128]{2,1,0:T(8,128)(2,1)}, u32[]{:S(2)}, u32[]{:S(2)}) collective-permute-start(bf16[12,48,128]{2,1,0:T(8,128)(2,1)} %get-tuple-element.32), channel_id=1, source_target_pairs={{0,16},{8,24},{16,32},{24,40},{32,48},{40,56},{48,64},{56,72},{64,... | collective-permute-start | bytes 442376 | tf_op jit(solution)/shard_map/ppermute | solution.py:22
  175.1 12.2 %collective-permute-start.19 = (bf16[12,48,128]{2,1,0:T(8,128)(2,1)}, bf16[12,48,128]{2,1,0:T(8,128)(2,1)}, u32[]{:S(2)}, u32[]{:S(2)}) collective-permute-start(bf16[12,48,128]{2,1,0:T(8,128)(2,1)} %get-tuple-element.32), channel_id=1, source_target_pairs={{0,496},{8,504},{16,0},{24,8},{32,16},{40,24},{48,32},{56,40},{64,... | collective-permute-start | bytes 442376 | tf_op jit(solution)/shard_map/ppermute | solution.py:22
  196.8 18.6 %collective-permute-start.20 = (bf16[12,48,128]{2,1,0:T(8,128)(2,1)}, bf16[12,48,128]{2,1,0:T(8,128)(2,1)}, u32[]{:S(2)}, u32[]{:S(2)}) collective-permute-start(bf16[12,48,128]{2,1,0:T(8,128)(2,1)} %get-tuple-element.29), channel_id=1, source_target_pairs={{0,8},{8,16},{16,24},{24,32},{32,40},{40,48},{48,56},{56,64},{64,7... | collective-permute-start | bytes 442376 | tf_op jit(solution)/shard_map/ppermute | solution.py:22
  199.8 17.2 %collective-permute-start.21 = (bf16[12,48,128]{2,1,0:T(8,128)(2,1)}, bf16[12,48,128]{2,1,0:T(8,128)(2,1)}, u32[]{:S(2)}, u32[]{:S(2)}) collective-permute-start(bf16[12,48,128]{2,1,0:T(8,128)(2,1)} %get-tuple-element.29), channel_id=1, source_target_pairs={{0,504},{8,0},{16,8},{24,16},{32,24},{40,32},{48,40},{56,48},{64,5... | collective-permute-start | bytes 442376 | tf_op jit(solution)/shard_map/ppermute | solution.py:22
  205.9 12.6 %collective-permute-start.22 = (bf16[12,48,128]{2,1,0:T(8,128)(2,1)}, bf16[12,48,128]{2,1,0:T(8,128)(2,1)}, u32[]{:S(2)}, u32[]{:S(2)}) collective-permute-start(bf16[12,48,128]{2,1,0:T(8,128)(2,1)} %get-tuple-element.29), channel_id=1, source_target_pairs={{0,16},{8,24},{16,32},{24,40},{32,48},{40,56},{48,64},{56,72},{64,... | collective-permute-start | bytes 442376 | tf_op jit(solution)/shard_map/ppermute | solution.py:22
  207.9 12.2 %collective-permute-start.23 = (bf16[12,48,128]{2,1,0:T(8,128)(2,1)}, bf16[12,48,128]{2,1,0:T(8,128)(2,1)}, u32[]{:S(2)}, u32[]{:S(2)}) collective-permute-start(bf16[12,48,128]{2,1,0:T(8,128)(2,1)} %get-tuple-element.29), channel_id=1, source_target_pairs={{0,496},{8,504},{16,0},{24,8},{32,16},{40,24},{48,32},{56,40},{64,... | collective-permute-start | bytes 442376 | tf_op jit(solution)/shard_map/ppermute | solution.py:22
  224.9 2.9 copy-start.9
  231.4 18.8 %collective-permute-start.24 = (bf16[12,48,128]{2,1,0:T(8,128)(2,1)}, bf16[12,48,128]{2,1,0:T(8,128)(2,1)}, u32[]{:S(2)}, u32[]{:S(2)}) collective-permute-start(bf16[12,48,128]{2,1,0:T(8,128)(2,1)} %get-tuple-element.26), channel_id=1, source_target_pairs={{0,8},{8,16},{16,24},{24,32},{32,40},{40,48},{48,56},{56,64},{64,7... | collective-permute-start | bytes 442376 | tf_op jit(solution)/shard_map/ppermute | solution.py:22
  234.5 17.4 %collective-permute-start.25 = (bf16[12,48,128]{2,1,0:T(8,128)(2,1)}, bf16[12,48,128]{2,1,0:T(8,128)(2,1)}, u32[]{:S(2)}, u32[]{:S(2)}) collective-permute-start(bf16[12,48,128]{2,1,0:T(8,128)(2,1)} %get-tuple-element.26), channel_id=1, source_target_pairs={{0,504},{8,0},{16,8},{24,16},{32,24},{40,32},{48,40},{56,48},{64,5... | collective-permute-start | bytes 442376 | tf_op jit(solution)/shard_map/ppermute | solution.py:22
  240.6 12.8 %collective-permute-start.26 = (bf16[12,48,128]{2,1,0:T(8,128)(2,1)}, bf16[12,48,128]{2,1,0:T(8,128)(2,1)}, u32[]{:S(2)}, u32[]{:S(2)}) collective-permute-start(bf16[12,48,128]{2,1,0:T(8,128)(2,1)} %get-tuple-element.26), channel_id=1, source_target_pairs={{0,16},{8,24},{16,32},{24,40},{32,48},{40,56},{48,64},{56,72},{64,... | collective-permute-start | bytes 442376 | tf_op jit(solution)/shard_map/ppermute | solution.py:22
  242.5 12.3 %collective-permute-start.27 = (bf16[12,48,128]{2,1,0:T(8,128)(2,1)}, bf16[12,48,128]{2,1,0:T(8,128)(2,1)}, u32[]{:S(2)}, u32[]{:S(2)}) collective-permute-start(bf16[12,48,128]{2,1,0:T(8,128)(2,1)} %get-tuple-element.26), channel_id=1, source_target_pairs={{0,496},{8,504},{16,0},{24,8},{32,16},{40,24},{48,32},{56,40},{64,... | collective-permute-start | bytes 442376 | tf_op jit(solution)/shard_map/ppermute | solution.py:22
  259.8 2.9 copy-start.6
  266.4 18.6 %collective-permute-start.28 = (bf16[12,48,128]{2,1,0:T(8,128)(2,1)}, bf16[12,48,128]{2,1,0:T(8,128)(2,1)}, u32[]{:S(2)}, u32[]{:S(2)}) collective-permute-start(bf16[12,48,128]{2,1,0:T(8,128)(2,1)} %get-tuple-element.23), channel_id=1, source_target_pairs={{0,8},{8,16},{16,24},{24,32},{32,40},{40,48},{48,56},{56,64},{64,7... | collective-permute-start | bytes 442376 | tf_op jit(solution)/shard_map/ppermute | solution.py:22
  269.5 17.2 %collective-permute-start.29 = (bf16[12,48,128]{2,1,0:T(8,128)(2,1)}, bf16[12,48,128]{2,1,0:T(8,128)(2,1)}, u32[]{:S(2)}, u32[]{:S(2)}) collective-permute-start(bf16[12,48,128]{2,1,0:T(8,128)(2,1)} %get-tuple-element.23), channel_id=1, source_target_pairs={{0,504},{8,0},{16,8},{24,16},{32,24},{40,32},{48,40},{56,48},{64,5... | collective-permute-start | bytes 442376 | tf_op jit(solution)/shard_map/ppermute | solution.py:22
  275.6 12.6 %collective-permute-start.30 = (bf16[12,48,128]{2,1,0:T(8,128)(2,1)}, bf16[12,48,128]{2,1,0:T(8,128)(2,1)}, u32[]{:S(2)}, u32[]{:S(2)}) collective-permute-start(bf16[12,48,128]{2,1,0:T(8,128)(2,1)} %get-tuple-element.23), channel_id=1, source_target_pairs={{0,16},{8,24},{16,32},{24,40},{32,48},{40,56},{48,64},{56,72},{64,... | collective-permute-start | bytes 442376 | tf_op jit(solution)/shard_map/ppermute | solution.py:22
  277.5 12.2 %collective-permute-start.31 = (bf16[12,48,128]{2,1,0:T(8,128)(2,1)}, bf16[12,48,128]{2,1,0:T(8,128)(2,1)}, u32[]{:S(2)}, u32[]{:S(2)}) collective-permute-start(bf16[12,48,128]{2,1,0:T(8,128)(2,1)} %get-tuple-element.23), channel_id=1, source_target_pairs={{0,496},{8,504},{16,0},{24,8},{32,16},{40,24},{48,32},{56,40},{64,... | collective-permute-start | bytes 442376 | tf_op jit(solution)/shard_map/ppermute | solution.py:22
  294.6 2.9 copy-start.7
  301.3 19.8 %collective-permute-start.32 = (bf16[12,48,128]{2,1,0:T(8,128)(2,1)}, bf16[12,48,128]{2,1,0:T(8,128)(2,1)}, u32[]{:S(2)}, u32[]{:S(2)}) collective-permute-start(bf16[12,48,128]{2,1,0:T(8,128)(2,1)} %get-tuple-element.20), channel_id=1, source_target_pairs={{0,8},{8,16},{16,24},{24,32},{32,40},{40,48},{48,56},{56,64},{64,7... | collective-permute-start | bytes 442376 | tf_op jit(solution)/shard_map/ppermute | solution.py:22
  304.3 18.4 %collective-permute-start.33 = (bf16[12,48,128]{2,1,0:T(8,128)(2,1)}, bf16[12,48,128]{2,1,0:T(8,128)(2,1)}, u32[]{:S(2)}, u32[]{:S(2)}) collective-permute-start(bf16[12,48,128]{2,1,0:T(8,128)(2,1)} %get-tuple-element.20), channel_id=1, source_target_pairs={{0,504},{8,0},{16,8},{24,16},{32,24},{40,32},{48,40},{56,48},{64,5... | collective-permute-start | bytes 442376 | tf_op jit(solution)/shard_map/ppermute | solution.py:22
  311.6 12.6 %collective-permute-start.34 = (bf16[12,48,128]{2,1,0:T(8,128)(2,1)}, bf16[12,48,128]{2,1,0:T(8,128)(2,1)}, u32[]{:S(2)}, u32[]{:S(2)}) collective-permute-start(bf16[12,48,128]{2,1,0:T(8,128)(2,1)} %get-tuple-element.20), channel_id=1, source_target_pairs={{0,16},{8,24},{16,32},{24,40},{32,48},{40,56},{48,64},{56,72},{64,... | collective-permute-start | bytes 442376 | tf_op jit(solution)/shard_map/ppermute | solution.py:22
  313.5 12.2 %collective-permute-start.35 = (bf16[12,48,128]{2,1,0:T(8,128)(2,1)}, bf16[12,48,128]{2,1,0:T(8,128)(2,1)}, u32[]{:S(2)}, u32[]{:S(2)}) collective-permute-start(bf16[12,48,128]{2,1,0:T(8,128)(2,1)} %get-tuple-element.20), channel_id=1, source_target_pairs={{0,496},{8,504},{16,0},{24,8},{32,16},{40,24},{48,32},{56,40},{64,... | collective-permute-start | bytes 442376 | tf_op jit(solution)/shard_map/ppermute | solution.py:22
  330.6 2.9 copy-start.8
  337.2 25.1 %collective-permute-start.36 = (bf16[12,48,128]{2,1,0:T(8,128)(2,1)}, bf16[12,48,128]{2,1,0:T(8,128)(2,1)}, u32[]{:S(2)}, u32[]{:S(2)}) collective-permute-start(bf16[12,48,128]{2,1,0:T(8,128)(2,1)} %get-tuple-element.17), channel_id=1, source_target_pairs={{0,8},{8,16},{16,24},{24,32},{32,40},{40,48},{48,56},{56,64},{64,7... | collective-permute-start | bytes 442376 | tf_op jit(solution)/shard_map/ppermute | solution.py:22
  341.0 21.3 %copy-start.13 = (s32[1024]{0:T(1024)}, s32[1024]{0:T(1024)S(1)}, u32[]{:S(2)}) copy-start(s32[1024]{0:T(1024)S(1)} %pad_clamp_fusion) | copy-start | bytes 12292
  341.6 22.3 %collective-permute-start.37 = (bf16[12,48,128]{2,1,0:T(8,128)(2,1)}, bf16[12,48,128]{2,1,0:T(8,128)(2,1)}, u32[]{:S(2)}, u32[]{:S(2)}) collective-permute-start(bf16[12,48,128]{2,1,0:T(8,128)(2,1)} %get-tuple-element.17), channel_id=1, source_target_pairs={{0,504},{8,0},{16,8},{24,16},{32,24},{40,32},{48,40},{56,48},{64,5... | collective-permute-start | bytes 442376 | tf_op jit(solution)/shard_map/ppermute | solution.py:22
  351.1 19.0 %copy-start.3 = (f32[12,48,128]{2,1,0:T(8,128)S(1)}, f32[12,48,128]{2,1,0:T(8,128)}, u32[]{:S(2)}) copy-start(f32[12,48,128]{2,1,0:T(8,128)} %get-tuple-element.18) | copy-start | bytes 884740
  352.9 12.6 %collective-permute-start.38 = (bf16[12,48,128]{2,1,0:T(8,128)(2,1)}, bf16[12,48,128]{2,1,0:T(8,128)(2,1)}, u32[]{:S(2)}, u32[]{:S(2)}) collective-permute-start(bf16[12,48,128]{2,1,0:T(8,128)(2,1)} %get-tuple-element.17), channel_id=1, source_target_pairs={{0,16},{8,24},{16,32},{24,40},{32,48},{40,56},{48,64},{56,72},{64,... | collective-permute-start | bytes 442376 | tf_op jit(solution)/shard_map/ppermute | solution.py:22
  354.8 12.2 %collective-permute-start.39 = (bf16[12,48,128]{2,1,0:T(8,128)(2,1)}, bf16[12,48,128]{2,1,0:T(8,128)(2,1)}, u32[]{:S(2)}, u32[]{:S(2)}) collective-permute-start(bf16[12,48,128]{2,1,0:T(8,128)(2,1)} %get-tuple-element.17), channel_id=1, source_target_pairs={{0,496},{8,504},{16,0},{24,8},{32,16},{40,24},{48,32},{56,40},{64,... | collective-permute-start | bytes 442376 | tf_op jit(solution)/shard_map/ppermute | solution.py:22
  373.8 3.9 copy-start.15
  374.7 3.2 copy-start.10
  374.7 3.7 copy-start.14
  375.7 5.0 copy-start.11
Sparse Core Ops, SparseCore 0:
  380.9 478.4 all-reduce.2
where the time goes:
time: 872 us; the launch traced here: 868 us
  waiting for transfers between devices  479 us (55%)
  starting transfers between devices  188 us (22%)
  local copies, waits for them, and re-layouts  138 us (16%)
  other arithmetic  24 us (3%)
  matrix products  23.2 us (3%)
  between operations  15.8 us (2%)
    psum x1, waiting for transfers between devices, per_device(): summed = lax.psum(partial_sum, ('dom', 'sub'))  479 us
    ppermute x40, starting transfers between devices, from_behind(): return lax.ppermute(value, axis, pairs)  188 us
    gather x40, local copies, waits for them, and re-layouts, per_device(): halo_tiles.append(neighbour[halo_rows[position]])  60.5 us
    mul x21, local copies, waits for them, and re-layouts, variable_mix(): mixing_split[:, None, :, :, :] * residual_split[:, :, None, :, :]  21.8 us
    dot_general x10, matrix products, per_device(): jnp.einsum('tbor,tbrc->toc', picked, jac_blocks, preferred_element_type=j...  20.3 us
    gather x10, local copies, waits for them, and re-layouts, per_device(): picked = extended[block_cols]  18.4 us
  transfers between devices with their start and end apart: 41, of which 1 were waited for; matrix products, arithmetic and copies ran while one was open for 7% of the time, Pallas kernels for 0%

commit v1 on v0

v1 whole, which is shorter than its diff:
```python
import functools
import math

import jax
import jax.numpy as jnp
from jax import lax
from jax.experimental import pallas as pl
from jax.experimental.pallas import tpu as pltpu
from jax.sharding import PartitionSpec as P

NOBJ = 8
NVAR = 6
NDIR = 3
FB_DEV = 4
OUTER = 2
INNER = 5
HALO = 2
LINE = 4

OFFSETS = (1, -1, 2, -2)
RELAXATION = 0.7
VMEM = pltpu.MemorySpace.VMEM
SMEM = pltpu.MemorySpace.SMEM
GRANT = pltpu.CompilerParams(vmem_limit_bytes=16 * 1024 * 1024)


def from_behind(value, axis, steps):
    count = lax.axis_size(axis)
    pairs = [(source, (source + steps) % count) for source in range(count)]
    return lax.ppermute(value, axis, pairs)


def relaxed(current, residual, mixing_ref, tile):
    rows = [residual[w * NOBJ : (w + 1) * NOBJ, :] for w in range(NVAR)]
    pieces = []
    for v in range(NVAR):
        total = RELAXATION * rows[v]
        for w in range(NVAR):
            k = v * NVAR + w
            total = total + mixing_ref[tile, k : k + 1, :] * rows[w]
        pieces.append(total)
    update = jnp.concatenate(pieces, axis=0)
    return update if current is None else current + update


def first_kernel(rows_ref, target_ref, mixing_ref, sorted_ref, state_ref, rounded_ref, *payload_refs):
    tiles = target_ref.shape[0]
    for tile in range(tiles):
        target = jnp.concatenate(
            [target_ref[tile, pl.ds(v, NOBJ, stride=NVAR), :] for v in range(NVAR)], axis=0
        )
        sorted_ref[tile] = target
        state = relaxed(None, target, mixing_ref, tile)
        state_ref[tile] = state
        rounded = state.astype(jnp.bfloat16)
        rounded_ref[tile] = rounded
        for payload_ref in payload_refs:
            payload_ref[tile] = rounded
    shape = payload_refs[0].shape[1:]
    half = lax.broadcasted_iota(jnp.int32, shape, 0) < shape[0] // HALO
    for k, payload_ref in enumerate(payload_refs):
        first = rows_ref[k * HALO].astype(jnp.float32)
        second = rows_ref[k * HALO + 1].astype(jnp.float32)
        payload_ref[tiles] = jnp.where(half, first, second).astype(jnp.bfloat16)


def update_tiles(cols_ref, state_ref, extended_ref, target_ref, mixing_ref, blocks_ref, store):
    block_count = blocks_ref.shape[1]
    cells = blocks_ref.shape[3]
    for tile in range(state_ref.shape[0]):
        picked = jnp.concatenate(
            [extended_ref[cols_ref[tile * block_count + b]] for b in range(block_count)], axis=1
        )
        product = jnp.dot(
            picked,
            blocks_ref[tile].reshape(block_count * cells, cells),
            preferred_element_type=jnp.float32,
        )
        current = state_ref[tile]
        residual = target_ref[tile] - (current + product)
        store(tile, relaxed(current, residual, mixing_ref, tile))


def pack(place, needs, rounded_ref, own_ref, layer_ref):
    rows = rounded_ref.shape[1]

    def wanted(offset, h):
        index = jnp.int32(0)
        for k, o in enumerate(OFFSETS):
            index = jnp.where(offset == o, needs[k * HALO + h], index)
        return index

    for h in range(HALO):
        span = slice(h * rows, (h + 1) * rows)
        for peer in range(LINE):
            own_ref[peer, span, :] = rounded_ref[wanted(peer - place, h)]
        for side in range(2):
            there = jnp.where(place < 2, side - 2, side + LINE)
            layer_ref[side, span, :] = rounded_ref[wanted(there - place, h)]


def second_kernel(
    place_ref,
    cols_ref,
    rows_ref,
    state_ref,
    rounded_ref,
    from0_ref,
    from1_ref,
    from2_ref,
    from3_ref,
    target_ref,
    mixing_ref,
    blocks_ref,
    new_ref,
    new_rounded_ref,
    own_ref,
    layer_ref,
    needs_ref,
    extended_ref,
):
    tiles = state_ref.shape[0]
    sources = (from0_ref, from1_ref, from2_ref, from3_ref)
    needs = [None] * (len(OFFSETS) * HALO)
    for k, source_ref in enumerate(sources):
        for h in range(HALO):
            entry = k * HALO + h
            extended_ref[tiles + entry] = source_ref[rows_ref[entry]]
            named = source_ref[tiles, h * 24 : h * 24 + 8, :].astype(jnp.float32)
            told = OFFSETS.index(-OFFSETS[k])
            needs[told * HALO + h] = jnp.max(named).astype(jnp.int32)
    for entry, need in enumerate(needs):
        needs_ref[entry] = need
    for tile in range(tiles):
        extended_ref[tile] = rounded_ref[tile]

    def store(tile, state):
        new_ref[tile] = state
        new_rounded_ref[tile] = state.astype(jnp.bfloat16)

    update_tiles(cols_ref, state_ref, extended_ref, target_ref, mixing_ref, blocks_ref, store)
    pack(place_ref[0], needs, new_rounded_ref, own_ref, layer_ref)


def sweep_kernel(
    last,
    place_ref,
    cols_ref,
    needs_ref,
    state_ref,
    rounded_ref,
    halo_ref,
    target_ref,
    mixing_ref,
    blocks_ref,
    new_ref,
    *rest,
):
    tiles = state_ref.shape[0]
    rows = state_ref.shape[1]
    extended_ref = rest[-1]
    place = place_ref[0]
    for k, offset in enumerate(OFFSETS):
        source = place - offset
        relayed = jnp.where((source < 0) | (source >= LINE), 1, 0)
        peer = source & (LINE - 1)
        for h in range(HALO):
            start = pl.multiple_of((relayed * HALO + h) * rows, 16)
            extended_ref[tiles + k * HALO + h] = halo_ref[peer, pl.ds(start, rows), :]
    for tile in range(tiles):
        extended_ref[tile] = rounded_ref[tile]

    def store(tile, state):
        new_ref[tile] = state
        if last:
            for v in range(NVAR):
                part = state[v * NOBJ : (v + 1) * NOBJ, :]
                rest[0][tile, pl.ds(v, NOBJ, stride=NVAR), :] = part
        else:
            rest[0][tile] = state.astype(jnp.bfloat16)

    update_tiles(cols_ref, state_ref, extended_ref, target_ref, mixing_ref, blocks_ref, store)
    if not last:
        needs = [needs_ref[entry] for entry in range(len(OFFSETS) * HALO)]
        pack(place, needs, rest[0], rest[1], rest[2])


def design_kernel(
    tile_ref, block_ref, count_ref, state_ref, derivative_ref, weights_ref, out_ref, sum_ref
):
    owners = sum_ref.shape[0] // 2
    rows = NOBJ * NDIR
    sum_ref[...] = jnp.zeros(sum_ref.shape, jnp.float32)
    for slot in range(weights_ref.shape[0]):
        tile = tile_ref[slot]
        selected = state_ref[tile]
        pieces = []
        for k in range(NDIR):
            total = None
            for v in range(NVAR):
                row = v * NDIR + k
                term = (
                    selected[v * NOBJ : (v + 1) * NOBJ, :]
                    * derivative_ref[slot, row : row + 1, :]
                )
                total = term if total is None else total + term
            pieces.append(total)
        sensitivity = jnp.concatenate(pieces, axis=0)
        alive = slot < count_ref[0]
        sensitivity = jnp.where(alive, sensitivity, 0.0)
        coarse = sensitivity.astype(jnp.bfloat16)
        fine = sensitivity - coarse.astype(jnp.float32)
        halves = lax.dot_general(
            jnp.concatenate([coarse.astype(jnp.float32), fine], axis=0).astype(jnp.bfloat16),
            weights_ref[slot],
            (((1,), (1,)), ((), ())),
            preferred_element_type=jnp.float32,
        )
        projected = halves[:rows] + halves[rows:]
        block = block_ref[slot]
        within = block % FB_DEV
        chunk = (within // 2) * owners + block // FB_DEV
        start = pl.multiple_of((within % 2) * rows, 8)
        sum_ref[chunk, pl.ds(start, rows), :] = sum_ref[chunk, pl.ds(start, rows), :] + projected
    for chunk in range(sum_ref.shape[0]):
        out_ref[chunk] = sum_ref[chunk].astype(jnp.bfloat16)


def vmem(count):
    return [pl.BlockSpec(memory_space=VMEM)] * count


def smem(count):
    return [pl.BlockSpec(memory_space=SMEM)] * count


def first_sweep(rows, target, mixing):
    shape = jax.ShapeDtypeStruct(target.shape, jnp.float32)
    rounded = jax.ShapeDtypeStruct(target.shape, jnp.bfloat16)
    payload = jax.ShapeDtypeStruct((target.shape[0] + 1,) + target.shape[1:], jnp.bfloat16)
    return pl.pallas_call(
        first_kernel,
        out_shape=(shape, shape, rounded) + (payload,) * len(OFFSETS),
        in_specs=smem(1) + vmem(2),
        out_specs=tuple(vmem(3 + len(OFFSETS))),
        compiler_params=GRANT,
        name="first_sweep",
    )(rows, target, mixing)


def sweep_shapes(state):
    chunk = (HALO * state.shape[1], state.shape[2])
    return (
        jax.ShapeDtypeStruct(state.shape, jnp.float32),
        jax.ShapeDtypeStruct(state.shape, jnp.bfloat16),
        jax.ShapeDtypeStruct((LINE,) + chunk, jnp.bfloat16),
        jax.ShapeDtypeStruct((2,) + chunk, jnp.bfloat16),
    )


def extended_scratch(state):
    tiles = state.shape[0] + len(OFFSETS) * HALO
    return [pltpu.VMEM((tiles,) + state.shape[1:], jnp.bfloat16)]


def second_sweep(place, cols, rows, state, rounded, sources, target, mixing, blocks):
    needs = jax.ShapeDtypeStruct((len(OFFSETS) * HALO,), jnp.int32)
    return pl.pallas_call(
        second_kernel,
        out_shape=sweep_shapes(state) + (needs,),
        in_specs=smem(3) + vmem(9),
        out_specs=tuple(vmem(4) + smem(1)),
        scratch_shapes=extended_scratch(state),
        compiler_params=GRANT,
        name="second_sweep",
    )(place, cols, rows, state, rounded, *sources, target, mixing, blocks)


def sweep(place, cols, needs, state, rounded, halo, target, mixing, blocks, last):
    shapes = sweep_shapes(state)
    out_shape = (shapes[0], shapes[0]) if last else shapes
    return pl.pallas_call(
        functools.partial(sweep_kernel, last),
        out_shape=out_shape,
        in_specs=smem(3) + vmem(6),
        out_specs=tuple(vmem(len(out_shape))),
        scratch_shapes=extended_scratch(state),
        compiler_params=GRANT,
        name="last_sweep" if last else "sweep",
    )(place, cols, needs, state, rounded, halo, target, mixing, blocks)


def exchange(own, layer):
    count = lax.axis_size("dom")
    steps = [LINE if source % LINE >= 2 else -LINE for source in range(count)]
    pairs = [(source, (source + step) % count) for source, step in enumerate(steps)]
    relayed = lax.ppermute(layer, "dom", pairs)
    chunks = jnp.concatenate([own, jnp.concatenate([relayed, relayed], axis=0)], axis=1)
    lines = [[start + x for x in range(LINE)] for start in range(0, count, LINE)]
    return lax.all_to_all(chunks, "dom", 0, 0, axis_index_groups=lines)


def design_partial(tile, block, count, state, derivative, weights, owners):
    chunk = (2 * owners, 2 * NOBJ * NDIR, weights.shape[1])
    return pl.pallas_call(
        design_kernel,
        out_shape=jax.ShapeDtypeStruct(chunk, jnp.bfloat16),
        in_specs=smem(3) + vmem(3),
        out_specs=pl.BlockSpec(memory_space=VMEM),
        scratch_shapes=[pltpu.VMEM(chunk, jnp.float32)],
        compiler_params=GRANT,
        name="design_partial",
    )(tile, block, count, state, derivative, weights)


def reduce_design(first, second, scaling):
    dom, sub = lax.axis_size("dom"), lax.axis_size("sub")
    columns = LINE
    layers = dom // columns
    plane = columns * sub
    chunks = jnp.concatenate([first, second], axis=0)
    planes = [[layer * plane + i for i in range(plane)] for layer in range(layers)]
    spread = lax.all_to_all(chunks, ("dom", "sub"), 0, 0, axis_index_groups=planes)
    mine = jnp.sum(spread.astype(jnp.float32), axis=0).astype(jnp.bfloat16)
    stacks = [[layer * columns + x for layer in range(layers)] for x in range(columns)]
    copies = jnp.broadcast_to(mine[None], (layers,) + mine.shape)
    stacked = lax.all_to_all(copies, "dom", 0, 0, axis_index_groups=stacks)
    total = jnp.sum(stacked.astype(jnp.float32), axis=0) * scaling
    lines = [[layer * columns + x for x in range(columns)] for layer in range(layers)]
    copies = jnp.broadcast_to(total[None], (columns,) + total.shape)
    gathered = lax.all_to_all(copies, "dom", 0, 0, axis_index_groups=lines)
    split = gathered.reshape(OUTER, FB_DEV, NDIR, NOBJ, gathered.shape[-1])
    return split.swapaxes(2, 3).reshape(OUTER, FB_DEV, NOBJ * NDIR, gathered.shape[-1])


def per_device(
    jac_blocks,
    block_cols,
    precond,
    right_side,
    halo_rows,
    surface_tile,
    surface_block,
    surface_count,
    surface_residual_derivative,
    lattice_bernstein_weights,
):
    slot_count = surface_tile.shape[0]
    scaling = math.sqrt(FB_DEV / (slot_count * lax.axis_size("dom")))
    cols = block_cols.reshape(-1)
    rows = halo_rows.reshape(-1)
    place = (lax.axis_index("dom") % LINE).astype(jnp.int32).reshape(1)
    target, state, rounded, *payloads = first_sweep(rows, right_side, precond)
    partials = []
    adjoint = None
    for outer_index in range(OUTER):
        for sweep_index in range(INNER):
            number = outer_index * INNER + sweep_index
            last = number == OUTER * INNER - 1
            if number == 0:
                continue
            if number == 1:
                sources = [
                    from_behind(payloads[OFFSETS.index(-offset)], "dom", offset)
                    for offset in OFFSETS
                ]
                state, rounded, own, layer, needs = second_sweep(
                    place, cols, rows, state, rounded, sources, target, precond, jac_blocks
                )
                continue
            halo = exchange(own, layer)
            result = sweep(
                place, cols, needs, state, rounded, halo, target, precond, jac_blocks, last
            )
            if last:
                state, adjoint = result
            else:
                state, rounded, own, layer = result
        partials.append(
            design_partial(
                surface_tile,
                surface_block,
                surface_count,
                state,
                surface_residual_derivative,
                lattice_bernstein_weights,
                lax.axis_size("sub"),
            )
        )
    return (adjoint, reduce_design(partials[0], partials[1], scaling))


def solution(mesh):
    in_specs = (
        P(("dom", "sub"), None, None, None),
        P(("dom", "sub"), None),
        P(("dom", "sub"), None, None),
        P(("dom", "sub"), None, None),
        P(("dom", "sub"), None),
        P(("dom", "sub")),
        P(("dom", "sub")),
        P(("dom", "sub")),
        P(("dom", "sub"), None, None),
        P(("dom", "sub"), None, None),
    )
    out_specs = (P(("dom", "sub"), None, None), P(None, "sub", None, None))
    return jax.shard_map(
        per_device, mesh=mesh, in_specs=in_specs, out_specs=out_specs, check_vma=False
    )
```

time: 872 us -> 241 us (0.28)
  the two profiles are of different devices: /device:TPU:2 before, /device:TPU:32 now
where the time goes in v1:
time: 241 us; the launch traced here: 240 us
  blocking collectives  116 us (48%)
  starting transfers between devices  67 us (28%)
  local copies, waits for them, and re-layouts  20.5 us (9%)
  waiting for transfers between devices  19.4 us (8%)
  Pallas kernels  14.7 us (6%)
    all_to_all x7, blocking collectives, exchange(): return lax.all_to_all(chunks, 'dom', 0, 0, axis_index_groups=lines)  62.7 us
    ppermute x8, starting transfers between devices, exchange(): relayed = lax.ppermute(layer, 'dom', pairs)  46.8 us
    all_to_all x1, blocking collectives, reduce_design(): stacked = lax.all_to_all(copies, 'dom', 0, 0, axis_index_groups=stacks)  29.4 us
    unnamed x58, local copies, waits for them, and re-layouts  20.3 us
    ppermute x4, starting transfers between devices, from_behind(): return lax.ppermute(value, axis, pairs)  16.2 us
    all_to_all x1, blocking collectives, reduce_design(): lax.all_to_all(chunks, ('dom', 'sub'), 0, 0, axis_index_groups=planes)  15.6 us
    ppermute x8, waiting for transfers between devices, exchange(): relayed = lax.ppermute(layer, 'dom', pairs)  14.3 us
    pallas_call x8, Pallas kernels, sweep(): pl.pallas_call(functools.partial(sweep_kernel, last), out_shape=out_shape...  10.5 us
  transfers between devices with their start and end apart: 13, of which 11 were waited for; matrix products, arithmetic and copies ran while one was open for 1% of the time, Pallas kernels for 0%

profile of v1, /device:TPU:32, one launch (start us, length us, event | category | flops | bytes accessed | tf_op | source)
XLA Modules:
  0.0 240.2 jit_solution(12646169421733981468)
XLA Ops:
  0.6 0.8 copy.23
  1.5 0.9 copy-done.2
  2.4 1.0 copy-done.8
  3.4 0.7 first_sweep.1
  4.7 3.4 %collective-permute-start = (bf16[13,48,128]{2,1,0:T(8,128)(2,1)S(1)}, bf16[13,48,128]{2,1,0:T(8,128)(2,1)S(1)}, u32[]{:S(2)}, u32[]{:S(2)}) collective-permute-start(bf16[13,48,128]{2,1,0:T(8,128)(2,1)S(1)} %get-tuple-element.46), channel_id=1, source_target_pairs={{0,8},{8,16},{16,24},{24,32},{32,40},{40,48},{48,56},{56,64},{64,7... | collective-permute-start | bytes 479240 | tf_op jit(solution)/shard_map/ppermute | solution.py:30
  8.1 4.6 %collective-permute-start.1 = (bf16[13,48,128]{2,1,0:T(8,128)(2,1)S(1)}, bf16[13,48,128]{2,1,0:T(8,128)(2,1)S(1)}, u32[]{:S(2)}, u32[]{:S(2)}) collective-permute-start(bf16[13,48,128]{2,1,0:T(8,128)(2,1)S(1)} %get-tuple-element.47), channel_id=1, source_target_pairs={{0,504},{8,0},{16,8},{24,16},{32,24},{40,32},{48,40},{56,48},{64,5... | collective-permute-start | bytes 479240 | tf_op jit(solution)/shard_map/ppermute | solution.py:30
  12.7 2.8 %collective-permute-start.2 = (bf16[13,48,128]{2,1,0:T(8,128)(2,1)S(1)}, bf16[13,48,128]{2,1,0:T(8,128)(2,1)S(1)}, u32[]{:S(2)}, u32[]{:S(2)}) collective-permute-start(bf16[13,48,128]{2,1,0:T(8,128)(2,1)S(1)} %get-tuple-element.48), channel_id=1, source_target_pairs={{0,16},{8,24},{16,32},{24,40},{32,48},{40,56},{48,64},{56,72},{64,... | collective-permute-start | bytes 479240 | tf_op jit(solution)/shard_map/ppermute | solution.py:30
  15.5 5.4 %collective-permute-start.3 = (bf16[13,48,128]{2,1,0:T(8,128)(2,1)S(1)}, bf16[13,48,128]{2,1,0:T(8,128)(2,1)S(1)}, u32[]{:S(2)}, u32[]{:S(2)}) collective-permute-start(bf16[13,48,128]{2,1,0:T(8,128)(2,1)S(1)} %get-tuple-element.49), channel_id=1, source_target_pairs={{0,496},{8,504},{16,0},{24,8},{32,16},{40,24},{48,32},{56,40},{64,... | collective-permute-start | bytes 479240 | tf_op jit(solution)/shard_map/ppermute | solution.py:30
  21.0 0.8 copy.22
  22.4 0.7 copy-done.11
  23.1 2.7 %collective-permute-done.3.from3_ref = bf16[13,48,128]{2,1,0:T(8,128)(2,1)S(1)} collective-permute-done((bf16[13,48,128]{2,1,0:T(8,128)(2,1)S(1)}, bf16[13,48,128]{2,1,0:T(8,128)(2,1)S(1)}, u32[]{:S(2)}, u32[]{:S(2)}) %collective-permute-start.3) | collective-permute-done | bytes 159776 | tf_op jit(solution)/shard_map/ppermute | solution.py:30
  26.4 1.7 copy-done
  28.0 0.9 copy-done.3
  29.0 0.9 copy-done.12
  29.9 0.9 copy-done.14
  30.8 0.9 copy-done.16
  31.7 1.8 second_sweep.1
  33.6 10.9 %collective-permute-start.4 = (bf16[2,96,128]{2,1,0:T(8,128)(2,1)S(1)}, bf16[2,96,128]{2,1,0:T(8,128)(2,1)S(1)}, u32[]{:S(2)}, u32[]{:S(2)}) collective-permute-start(bf16[2,96,128]{2,1,0:T(8,128)(2,1)S(1)} %get-tuple-element.55), channel_id=1, source_target_pairs={{0,480},{8,488},{16,48},{24,56},{32,0},{40,8},{48,80},{56,88},{64,... | collective-permute-start | bytes 147464 | tf_op jit(solution)/shard_map/ppermute | solution.py:297
  44.5 1.7 collective-permute-done.4
  46.2 8.7 %all_to_all.55.halo_ref = bf16[4,192,128]{2,1,0:T(8,128)(2,1)S(1)} all-to-all(bf16[4,192,128]{2,1,0:T(8,128)(2,1)S(1)} %maximum_maximum_fusion), channel_id=1, replica_groups={{0,8,16,24},{32,40,48,56},{64,72,80,88},{96,104,112,120},{128,136,144,1..., dimensions={0} | all-to-all | bytes 393216 | tf_op jit(solution)/shard_map/all_to_all | solution.py:300
  54.9 1.2 sweep.7
  56.1 5.5 %collective-permute-start.5 = (bf16[2,96,128]{2,1,0:T(8,128)(2,1)S(1)}, bf16[2,96,128]{2,1,0:T(8,128)(2,1)S(1)}, u32[]{:S(2)}, u32[]{:S(2)}) collective-permute-start(bf16[2,96,128]{2,1,0:T(8,128)(2,1)S(1)} %get-tuple-element.59), channel_id=1, source_target_pairs={{0,480},{8,488},{16,48},{24,56},{32,0},{40,8},{48,80},{56,88},{64,... | collective-permute-start | bytes 147464 | tf_op jit(solution)/shard_map/ppermute | solution.py:297
  61.7 1.7 collective-permute-done.5
  63.4 8.9 %all_to_all.56.halo_ref = bf16[4,192,128]{2,1,0:T(8,128)(2,1)S(1)} all-to-all(bf16[4,192,128]{2,1,0:T(8,128)(2,1)S(1)} %maximum_maximum_fusion.1), channel_id=1, replica_groups={{0,8,16,24},{32,40,48,56},{64,72,80,88},{96,104,112,120},{128,136,144,1..., dimensions={0} | all-to-all | bytes 393216 | tf_op jit(solution)/shard_map/all_to_all | solution.py:300
  72.3 1.2 sweep.8
  73.5 5.1 %collective-permute-start.6 = (bf16[2,96,128]{2,1,0:T(8,128)(2,1)S(1)}, bf16[2,96,128]{2,1,0:T(8,128)(2,1)S(1)}, u32[]{:S(2)}, u32[]{:S(2)}) collective-permute-start(bf16[2,96,128]{2,1,0:T(8,128)(2,1)S(1)} %get-tuple-element.63), channel_id=1, source_target_pairs={{0,480},{8,488},{16,48},{24,56},{32,0},{40,8},{48,80},{56,88},{64,... | collective-permute-start | bytes 147464 | tf_op jit(solution)/shard_map/ppermute | solution.py:297
  78.6 1.7 collective-permute-done.6
  80.4 8.9 %all_to_all.57.halo_ref = bf16[4,192,128]{2,1,0:T(8,128)(2,1)S(1)} all-to-all(bf16[4,192,128]{2,1,0:T(8,128)(2,1)S(1)} %maximum_maximum_fusion.2), channel_id=1, replica_groups={{0,8,16,24},{32,40,48,56},{64,72,80,88},{96,104,112,120},{128,136,144,1..., dimensions={0} | all-to-all | bytes 393216 | tf_op jit(solution)/shard_map/all_to_all | solution.py:300
  89.3 1.2 sweep.9
  90.5 5.1 %collective-permute-start.7 = (bf16[2,96,128]{2,1,0:T(8,128)(2,1)S(1)}, bf16[2,96,128]{2,1,0:T(8,128)(2,1)S(1)}, u32[]{:S(2)}, u32[]{:S(2)}) collective-permute-start(bf16[2,96,128]{2,1,0:T(8,128)(2,1)S(1)} %get-tuple-element.67), channel_id=1, source_target_pairs={{0,480},{8,488},{16,48},{24,56},{32,0},{40,8},{48,80},{56,88},{64,... | collective-permute-start | bytes 147464 | tf_op jit(solution)/shard_map/ppermute | solution.py:297
  95.6 1.7 collective-permute-done.7
  97.4 8.9 %all_to_all.58.halo_ref = bf16[4,192,128]{2,1,0:T(8,128)(2,1)S(1)} all-to-all(bf16[4,192,128]{2,1,0:T(8,128)(2,1)S(1)} %maximum_maximum_fusion.3), channel_id=1, replica_groups={{0,8,16,24},{32,40,48,56},{64,72,80,88},{96,104,112,120},{128,136,144,1..., dimensions={0} | all-to-all | bytes 393216 | tf_op jit(solution)/shard_map/all_to_all | solution.py:300
  106.3 1.2 sweep.10
  107.4 5.1 %collective-permute-start.8 = (bf16[2,96,128]{2,1,0:T(8,128)(2,1)S(1)}, bf16[2,96,128]{2,1,0:T(8,128)(2,1)S(1)}, u32[]{:S(2)}, u32[]{:S(2)}) collective-permute-start(bf16[2,96,128]{2,1,0:T(8,128)(2,1)S(1)} %get-tuple-element.71), channel_id=1, source_target_pairs={{0,480},{8,488},{16,48},{24,56},{32,0},{40,8},{48,80},{56,88},{64,... | collective-permute-start | bytes 147464 | tf_op jit(solution)/shard_map/ppermute | solution.py:297
  112.6 1.7 collective-permute-done.8
  114.3 8.9 %all_to_all.59.halo_ref = bf16[4,192,128]{2,1,0:T(8,128)(2,1)S(1)} all-to-all(bf16[4,192,128]{2,1,0:T(8,128)(2,1)S(1)} %maximum_maximum_fusion.4), channel_id=1, replica_groups={{0,8,16,24},{32,40,48,56},{64,72,80,88},{96,104,112,120},{128,136,144,1..., dimensions={0} | all-to-all | bytes 393216 | tf_op jit(solution)/shard_map/all_to_all | solution.py:300
  123.2 1.2 sweep.11
  124.4 5.1 %collective-permute-start.9 = (bf16[2,96,128]{2,1,0:T(8,128)(2,1)S(1)}, bf16[2,96,128]{2,1,0:T(8,128)(2,1)S(1)}, u32[]{:S(2)}, u32[]{:S(2)}) collective-permute-start(bf16[2,96,128]{2,1,0:T(8,128)(2,1)S(1)} %get-tuple-element.75), channel_id=1, source_target_pairs={{0,480},{8,488},{16,48},{24,56},{32,0},{40,8},{48,80},{56,88},{64,... | collective-permute-start | bytes 147464 | tf_op jit(solution)/shard_map/ppermute | solution.py:297
  129.5 1.8 collective-permute-done.9
  131.4 9.4 %all_to_all.60.halo_ref = bf16[4,192,128]{2,1,0:T(8,128)(2,1)S(1)} all-to-all(bf16[4,192,128]{2,1,0:T(8,128)(2,1)S(1)} %maximum_maximum_fusion.5), channel_id=1, replica_groups={{0,8,16,24},{32,40,48,56},{64,72,80,88},{96,104,112,120},{128,136,144,1..., dimensions={0} | all-to-all | bytes 393216 | tf_op jit(solution)/shard_map/all_to_all | solution.py:300
  140.7 1.2 sweep.12
  141.9 5.1 %collective-permute-start.10 = (bf16[2,96,128]{2,1,0:T(8,128)(2,1)S(1)}, bf16[2,96,128]{2,1,0:T(8,128)(2,1)S(1)}, u32[]{:S(2)}, u32[]{:S(2)}) collective-permute-start(bf16[2,96,128]{2,1,0:T(8,128)(2,1)S(1)} %get-tuple-element.79), channel_id=1, source_target_pairs={{0,480},{8,488},{16,48},{24,56},{32,0},{40,8},{48,80},{56,88},{64,... | collective-permute-start | bytes 147464 | tf_op jit(solution)/shard_map/ppermute | solution.py:297
  147.0 2.1 collective-permute-done.10
  149.1 9.0 %all_to_all.61.halo_ref = bf16[4,192,128]{2,1,0:T(8,128)(2,1)S(1)} all-to-all(bf16[4,192,128]{2,1,0:T(8,128)(2,1)S(1)} %maximum_maximum_fusion.6), channel_id=1, replica_groups={{0,8,16,24},{32,40,48,56},{64,72,80,88},{96,104,112,120},{128,136,144,1..., dimensions={0} | all-to-all | bytes 393216 | tf_op jit(solution)/shard_map/all_to_all | solution.py:300
  158.2 1.2 sweep.13
  159.4 0.7 copy-done.9
  160.1 0.7 copy-done.17
  160.8 4.7 %collective-permute-start.11 = (bf16[2,96,128]{2,1,0:T(8,128)(2,1)S(1)}, bf16[2,96,128]{2,1,0:T(8,128)(2,1)S(1)}, u32[]{:S(2)}, u32[]{:S(2)}) collective-permute-start(bf16[2,96,128]{2,1,0:T(8,128)(2,1)S(1)} %get-tuple-element.83), channel_id=1, source_target_pairs={{0,480},{8,488},{16,48},{24,56},{32,0},{40,8},{48,80},{56,88},{64,... | collective-permute-start | bytes 147464 | tf_op jit(solution)/shard_map/ppermute | solution.py:297
  165.5 1.7 collective-permute-done.11
  167.2 0.7 maximum_maximum_fusion.7
  167.9 4.0 %all-to-all-start.7 = ((bf16[4,192,128]{2,1,0:T(8,128)(2,1)}), bf16[4,192,128]{2,1,0:T(8,128)(2,1)}, u32[]{:S(2)}, u32[]{:S(2)}) async-start(bf16[4,192,128]{2,1,0:T(8,128)(2,1)} %maximum_maximum_fusion.7), calls=%async_computation.7 | async-start | bytes 393216 | tf_op jit(solution)/shard_map/all_to_all | solution.py:300
  171.9 0.9 copy.24.derivative_ref
  174.8 0.9 design_partial.2
  175.7 0.7 copy-done.6
  176.3 2.0 all-to-all-done.7.halo_ref
  178.3 1.0 copy-done.10
  179.3 0.9 copy-done.18
  180.2 0.7 copy-done.20
  180.9 0.7 copy-done.22
  181.5 2.3 last_sweep.1
  185.1 0.9 design_partial.3
  186.1 15.6 %all_to_all.62 = bf16[32,48,128]{2,1,0:T(8,128)(2,1)S(1)} all-to-all(bf16[32,48,128]{2,1,0:T(8,128)(2,1)S(1)} %pad_maximum_fusion), channel_id=1, replica_groups={{0,1,2,3,4,5,6,7,8,9,10,11,12,13,14,15,16,17,18,19,20,21,22,23,24,25,26..., dimensions={0} | all-to-all | bytes 786432 | tf_op jit(solution)/shard_map/all_to_all | solution.py:323
  201.8 29.4 %all_to_all.63 = bf16[16,48,128]{2,1,0:T(8,128)(2,1)S(1)} all-to-all(bf16[16,48,128]{2,1,0:T(8,128)(2,1)S(1)} %broadcast_in_dim.4), channel_id=1, replica_groups={{0,32,64,96,128,160,192,224,256,288,320,352,384,416,448,480},{8,40,72,1..., dimensions={0} | all-to-all | bytes 393216 | tf_op jit(solution)/shard_map/all_to_all | solution.py:327
  231.2 8.2 %all_to_all.64 = f32[4,48,128]{2,1,0:T(8,128)S(1)} all-to-all(f32[4,48,128]{2,1,0:T(8,128)S(1)} %broadcast_in_dim.5), channel_id=1, replica_groups={{0,8,16,24},{32,40,48,56},{64,72,80,88},{96,104,112,120},{128,136,144,1..., dimensions={0} | all-to-all | bytes 196608 | tf_op jit(solution)/shard_map/all_to_all | solution.py:331
  (59 shorter events, 5.7 us)
Async XLA Ops:
  1.5 0.9 copy-start.2
  2.4 1.0 copy-start.8
  4.1 0.7 copy-start.15
  4.7 17.1 %collective-permute-start = (bf16[13,48,128]{2,1,0:T(8,128)(2,1)S(1)}, bf16[13,48,128]{2,1,0:T(8,128)(2,1)S(1)}, u32[]{:S(2)}, u32[]{:S(2)}) collective-permute-start(bf16[13,48,128]{2,1,0:T(8,128)(2,1)S(1)} %get-tuple-element.46), channel_id=1, source_target_pairs={{0,8},{8,16},{16,24},{24,32},{32,40},{40,48},{48,56},{56,64},{64,7... | collective-permute-start | bytes 479240 | tf_op jit(solution)/shard_map/ppermute | solution.py:30
  8.1 13.7 %collective-permute-start.1 = (bf16[13,48,128]{2,1,0:T(8,128)(2,1)S(1)}, bf16[13,48,128]{2,1,0:T(8,128)(2,1)S(1)}, u32[]{:S(2)}, u32[]{:S(2)}) collective-permute-start(bf16[13,48,128]{2,1,0:T(8,128)(2,1)S(1)} %get-tuple-element.47), channel_id=1, source_target_pairs={{0,504},{8,0},{16,8},{24,16},{32,24},{40,32},{48,40},{56,48},{64,5... | collective-permute-start | bytes 479240 | tf_op jit(solution)/shard_map/ppermute | solution.py:30
  12.7 9.7 %collective-permute-start.2 = (bf16[13,48,128]{2,1,0:T(8,128)(2,1)S(1)}, bf16[13,48,128]{2,1,0:T(8,128)(2,1)S(1)}, u32[]{:S(2)}, u32[]{:S(2)}) collective-permute-start(bf16[13,48,128]{2,1,0:T(8,128)(2,1)S(1)} %get-tuple-element.48), channel_id=1, source_target_pairs={{0,16},{8,24},{16,32},{24,40},{32,48},{40,56},{48,64},{56,72},{64,... | collective-permute-start | bytes 479240 | tf_op jit(solution)/shard_map/ppermute | solution.py:30
  15.5 10.2 %collective-permute-start.3 = (bf16[13,48,128]{2,1,0:T(8,128)(2,1)S(1)}, bf16[13,48,128]{2,1,0:T(8,128)(2,1)S(1)}, u32[]{:S(2)}, u32[]{:S(2)}) collective-permute-start(bf16[13,48,128]{2,1,0:T(8,128)(2,1)S(1)} %get-tuple-element.49), channel_id=1, source_target_pairs={{0,496},{8,504},{16,0},{24,8},{32,16},{40,24},{48,32},{56,40},{64,... | collective-permute-start | bytes 479240 | tf_op jit(solution)/shard_map/ppermute | solution.py:30
  21.8 136.3 %copy-start.19 = (s32[72]{0:T(128)}, s32[72]{0:T(128)S(1)}, u32[]{:S(2)}) copy-start(s32[72]{0:T(128)S(1)} %reshape.24.cols_ref) | copy-start | bytes 868
  22.4 0.7 copy-start.11
  25.7 0.7 copy-start.13
  26.4 1.7 copy-start
  28.0 0.9 copy-start.3
  29.0 0.9 copy-start.12
  29.9 0.9 copy-start.14
  30.8 0.9 copy-start.16
  31.7 23.2 %copy-start.1 = (bf16[12,6,128,128]{3,2,1,0:T(8,128)(2,1)S(1)}, bf16[12,6,128,128]{3,2,1,0:T(8,128)(2,1)}, u32[]{:S(2)}) copy-start(bf16[12,6,128,128]{3,2,1,0:T(8,128)(2,1)} %blocks_ref.17) | copy-start | bytes 7077892
  31.7 23.2 %copy-start.4 = (f32[12,36,128]{2,1,0:T(8,128)S(1)}, f32[12,36,128]{2,1,0:T(8,128)}, u32[]{:S(2)}) copy-start(f32[12,36,128]{2,1,0:T(8,128)} %mixing_ref.19) | copy-start | bytes 663556
  33.6 124.6 %copy-start.21 = (s32[8]{0:T(128)}, s32[8]{0:T(128)S(1)}, u32[]{:S(2)}) copy-start(s32[8]{0:T(128)S(1)} %get-tuple-element.51.needs_ref) | copy-start | bytes 100
  33.6 12.6 %collective-permute-start.4 = (bf16[2,96,128]{2,1,0:T(8,128)(2,1)S(1)}, bf16[2,96,128]{2,1,0:T(8,128)(2,1)S(1)}, u32[]{:S(2)}, u32[]{:S(2)}) collective-permute-start(bf16[2,96,128]{2,1,0:T(8,128)(2,1)S(1)} %get-tuple-element.55), channel_id=1, source_target_pairs={{0,480},{8,488},{16,48},{24,56},{32,0},{40,8},{48,80},{56,88},{64,... | collective-permute-start | bytes 147464 | tf_op jit(solution)/shard_map/ppermute | solution.py:297
  56.1 7.3 %collective-permute-start.5 = (bf16[2,96,128]{2,1,0:T(8,128)(2,1)S(1)}, bf16[2,96,128]{2,1,0:T(8,128)(2,1)S(1)}, u32[]{:S(2)}, u32[]{:S(2)}) collective-permute-start(bf16[2,96,128]{2,1,0:T(8,128)(2,1)S(1)} %get-tuple-element.59), channel_id=1, source_target_pairs={{0,480},{8,488},{16,48},{24,56},{32,0},{40,8},{48,80},{56,88},{64,... | collective-permute-start | bytes 147464 | tf_op jit(solution)/shard_map/ppermute | solution.py:297
  73.5 6.9 %collective-permute-start.6 = (bf16[2,96,128]{2,1,0:T(8,128)(2,1)S(1)}, bf16[2,96,128]{2,1,0:T(8,128)(2,1)S(1)}, u32[]{:S(2)}, u32[]{:S(2)}) collective-permute-start(bf16[2,96,128]{2,1,0:T(8,128)(2,1)S(1)} %get-tuple-element.63), channel_id=1, source_target_pairs={{0,480},{8,488},{16,48},{24,56},{32,0},{40,8},{48,80},{56,88},{64,... | collective-permute-start | bytes 147464 | tf_op jit(solution)/shard_map/ppermute | solution.py:297
  90.5 6.9 %collective-permute-start.7 = (bf16[2,96,128]{2,1,0:T(8,128)(2,1)S(1)}, bf16[2,96,128]{2,1,0:T(8,128)(2,1)S(1)}, u32[]{:S(2)}, u32[]{:S(2)}) collective-permute-start(bf16[2,96,128]{2,1,0:T(8,128)(2,1)S(1)} %get-tuple-element.67), channel_id=1, source_target_pairs={{0,480},{8,488},{16,48},{24,56},{32,0},{40,8},{48,80},{56,88},{64,... | collective-permute-start | bytes 147464 | tf_op jit(solution)/shard_map/ppermute | solution.py:297
  107.4 6.9 %collective-permute-start.8 = (bf16[2,96,128]{2,1,0:T(8,128)(2,1)S(1)}, bf16[2,96,128]{2,1,0:T(8,128)(2,1)S(1)}, u32[]{:S(2)}, u32[]{:S(2)}) collective-permute-start(bf16[2,96,128]{2,1,0:T(8,128)(2,1)S(1)} %get-tuple-element.71), channel_id=1, source_target_pairs={{0,480},{8,488},{16,48},{24,56},{32,0},{40,8},{48,80},{56,88},{64,... | collective-permute-start | bytes 147464 | tf_op jit(solution)/shard_map/ppermute | solution.py:297
  124.4 6.9 %collective-permute-start.9 = (bf16[2,96,128]{2,1,0:T(8,128)(2,1)S(1)}, bf16[2,96,128]{2,1,0:T(8,128)(2,1)S(1)}, u32[]{:S(2)}, u32[]{:S(2)}) collective-permute-start(bf16[2,96,128]{2,1,0:T(8,128)(2,1)S(1)} %get-tuple-element.75), channel_id=1, source_target_pairs={{0,480},{8,488},{16,48},{24,56},{32,0},{40,8},{48,80},{56,88},{64,... | collective-permute-start | bytes 147464 | tf_op jit(solution)/shard_map/ppermute | solution.py:297
  141.9 7.2 %collective-permute-start.10 = (bf16[2,96,128]{2,1,0:T(8,128)(2,1)S(1)}, bf16[2,96,128]{2,1,0:T(8,128)(2,1)S(1)}, u32[]{:S(2)}, u32[]{:S(2)}) collective-permute-start(bf16[2,96,128]{2,1,0:T(8,128)(2,1)S(1)} %get-tuple-element.79), channel_id=1, source_target_pairs={{0,480},{8,488},{16,48},{24,56},{32,0},{40,8},{48,80},{56,88},{64,... | collective-permute-start | bytes 147464 | tf_op jit(solution)/shard_map/ppermute | solution.py:297
  149.1 24.4 %copy-start.5 = (bf16[8,128,128]{2,1,0:T(8,128)(2,1)S(1)}, bf16[8,128,128]{2,1,0:T(8,128)(2,1)}, u32[]{:S(2)}) copy-start(bf16[8,128,128]{2,1,0:T(8,128)(2,1)} %weights_ref.3) | copy-start | bytes 786436
  159.4 0.7 copy-start.9
  160.1 0.7 copy-start.17
  160.8 6.5 %collective-permute-start.11 = (bf16[2,96,128]{2,1,0:T(8,128)(2,1)S(1)}, bf16[2,96,128]{2,1,0:T(8,128)(2,1)S(1)}, u32[]{:S(2)}, u32[]{:S(2)}) collective-permute-start(bf16[2,96,128]{2,1,0:T(8,128)(2,1)S(1)} %get-tuple-element.83), channel_id=1, source_target_pairs={{0,480},{8,488},{16,48},{24,56},{32,0},{40,8},{48,80},{56,88},{64,... | collective-permute-start | bytes 147464 | tf_op jit(solution)/shard_map/ppermute | solution.py:297
  167.9 10.4 %all-to-all-start.7 = ((bf16[4,192,128]{2,1,0:T(8,128)(2,1)}), bf16[4,192,128]{2,1,0:T(8,128)(2,1)}, u32[]{:S(2)}, u32[]{:S(2)}) async-start(bf16[4,192,128]{2,1,0:T(8,128)(2,1)} %maximum_maximum_fusion.7), calls=%async_computation.7 | async-start | bytes 393216 | tf_op jit(solution)/shard_map/all_to_all | solution.py:300
  173.5 0.7 copy-start.23
  174.1 0.7 copy-start.25
  175.7 0.7 copy-start.6
  178.3 7.7 %copy-start.7 = (bf16[16,48,128]{2,1,0:T(8,128)(2,1)S(1)}, bf16[16,48,128]{2,1,0:T(8,128)(2,1)}, u32[]{:S(2)}) copy-start(bf16[16,48,128]{2,1,0:T(8,128)(2,1)} %copy-done.6) | copy-start | bytes 589828
  178.3 1.0 copy-start.10
  179.3 0.9 copy-start.18
  180.2 0.7 copy-start.20
  180.9 0.7 copy-start.22
  183.8 0.7 copy-start.24
  184.5 0.7 copy-start.26

commit v2 on v1

v2 whole, which is shorter than its diff:
```python
import functools
import math

import jax
import jax.numpy as jnp
from jax import lax
from jax.experimental import pallas as pl
from jax.experimental.pallas import tpu as pltpu
from jax.sharding import PartitionSpec as P

NOBJ = 8
NVAR = 6
NDIR = 3
FB_DEV = 4
OUTER = 2
INNER = 5
HALO = 2
LINE = 4

OFFSETS = (1, -1, 2, -2)
NEEDS = len(OFFSETS) * HALO
COLS = 32
PLACE = COLS - 1
PART = 3
RELAXATION = 0.7
VMEM = pltpu.MemorySpace.VMEM
SMEM = pltpu.MemorySpace.SMEM
HBM = pltpu.MemorySpace.HBM
GRANT = pltpu.CompilerParams(vmem_limit_bytes=16 * 1024 * 1024)


def specs(*kinds):
    return [pl.BlockSpec(memory_space=kind) for kind in kinds]


def from_behind(value, axis, steps):
    count = lax.axis_size(axis)
    pairs = [(source, (source + steps) % count) for source in range(count)]
    return lax.ppermute(value, axis, pairs)


def relaxed(current, residual, mixing_ref, tile):
    rows = [residual[w * NOBJ : (w + 1) * NOBJ, :] for w in range(NVAR)]
    pieces = []
    for v in range(NVAR):
        total = RELAXATION * rows[v]
        for w in range(NVAR):
            k = v * NVAR + w
            total = total + mixing_ref[tile, k : k + 1, :] * rows[w]
        pieces.append(total)
    update = jnp.concatenate(pieces, axis=0)
    return update if current is None else current + update


def first_kernel(
    rows_hbm,
    target_hbm,
    mixing_hbm,
    sorted_ref,
    state_ref,
    payload_ref,
    rows_ref,
    target_ref,
    mixing_ref,
    sems,
):
    pairs = ((target_hbm, target_ref), (mixing_hbm, mixing_ref), (rows_hbm, rows_ref))
    copies = [pltpu.make_async_copy(*pair, sems.at[i]) for i, pair in enumerate(pairs)]
    for copy in copies:
        copy.start()
    for copy in copies:
        copy.wait()
    tiles = target_ref.shape[0]
    for tile in range(tiles):
        target = jnp.concatenate(
            [target_ref[tile, pl.ds(v, NOBJ, stride=NVAR), :] for v in range(NVAR)], axis=0
        )
        sorted_ref[tile] = target
        state = relaxed(None, target, mixing_ref, tile)
        state_ref[tile] = state
        payload_ref[tile] = state.astype(jnp.bfloat16)
    row = lax.broadcasted_iota(jnp.int32, payload_ref.shape[1:], 0)
    told = jnp.zeros(payload_ref.shape[1:], jnp.float32)
    for k in range(len(OFFSETS)):
        for h in range(HALO):
            told = jnp.where(row == k * HALO + h, rows_ref[h, k].astype(jnp.float32), told)
    payload_ref[tiles] = told.astype(jnp.bfloat16)


def update_tiles(
    table_ref, state_ref, extended_ref, target_ref, mixing_ref, blocks_ref, store, before=None
):
    block_count = blocks_ref.shape[1]
    cells = blocks_ref.shape[3]
    for tile in range(state_ref.shape[0]):
        if before is not None:
            before(tile)
        first = COLS + tile * block_count
        picked = jnp.concatenate(
            [extended_ref[table_ref[first + b]] for b in range(block_count)], axis=1
        )
        product = jnp.dot(
            picked,
            blocks_ref[tile].reshape(block_count * cells, cells),
            preferred_element_type=jnp.float32,
        )
        current = state_ref[tile]
        residual = target_ref[tile] - (current + product)
        store(tile, relaxed(current, residual, mixing_ref, tile))


def pack(place, needs, rounded_ref, own_ref, layer_ref):
    rows = rounded_ref.shape[1]

    def wanted(offset, h):
        index = jnp.int32(0)
        for k, o in enumerate(OFFSETS):
            index = jnp.where(offset == o, needs[k * HALO + h], index)
        return index

    for h in range(HALO):
        span = slice(h * rows, (h + 1) * rows)
        for peer in range(LINE):
            own_ref[peer, span, :] = rounded_ref[wanted(peer - place, h)]
        for side in range(2):
            there = jnp.where(place < 2, side - 2, side + LINE)
            layer_ref[side, span, :] = rounded_ref[wanted(there - place, h)]


def second_kernel(
    cols_hbm,
    rows_hbm,
    tile_hbm,
    block_hbm,
    mixing_hbm,
    blocks_hbm,
    count_ref,
    place_ref,
    state_ref,
    rounded_ref,
    from0_ref,
    from1_ref,
    from2_ref,
    from3_ref,
    target_ref,
    new_ref,
    new_rounded_ref,
    own_ref,
    layer_ref,
    table_ref,
    cols_ref,
    rows_ref,
    tile_ref,
    block_ref,
    mixing_ref,
    blocks_ref,
    extended_ref,
    told_ref,
    sems,
):
    tiles = state_ref.shape[0]
    small = (
        (rows_hbm, rows_ref),
        (cols_hbm, cols_ref),
        (tile_hbm, tile_ref),
        (block_hbm, block_ref),
    )
    number = iter(range(sems.shape[0]))
    first = [pltpu.make_async_copy(*pair, sems.at[next(number)]) for pair in small]
    large = [pltpu.make_async_copy(mixing_hbm, mixing_ref, sems.at[next(number)])]
    parts = []
    for start in range(0, tiles, PART):
        span = pl.ds(start, PART)
        parts.append(
            pltpu.make_async_copy(
                blocks_hbm.at[span], blocks_ref.at[span], sems.at[next(number)]
            )
        )
    for copy in first + large + parts:
        copy.start()
    for tile in range(tiles):
        extended_ref[tile] = rounded_ref[tile]
    for copy in first:
        copy.wait()
    sources = (from0_ref, from1_ref, from2_ref, from3_ref)
    copies = []
    for k, source_ref in enumerate(sources):
        for h in range(HALO):
            copies.append(
                pltpu.make_async_copy(
                    source_ref.at[rows_ref[h, k]],
                    extended_ref.at[tiles + k * HALO + h],
                    sems.at[next(number)],
                )
            )
        copies.append(
            pltpu.make_async_copy(source_ref.at[tiles], told_ref.at[k], sems.at[next(number)])
        )
    for copy in copies:
        copy.start()
    block_count = blocks_ref.shape[1]
    for tile in range(tiles):
        for b in range(block_count):
            table_ref[COLS + tile * block_count + b] = cols_ref[b, tile]
    slots = tile_ref.shape[0]
    for slot in range(slots):
        table_ref[NEEDS + slot] = tile_ref[slot]
        table_ref[NEEDS + slots + slot] = block_ref[slot]
    table_ref[NEEDS + 2 * slots] = count_ref[0]
    place = place_ref[0]
    table_ref[PLACE] = place
    for copy in copies:
        copy.wait()
    needs = [None] * NEEDS
    for k in range(len(sources)):
        named = told_ref[k].astype(jnp.float32)
        row = lax.broadcasted_iota(jnp.int32, named.shape, 0)
        told = OFFSETS.index(-OFFSETS[k])
        for h in range(HALO):
            entry = told * HALO + h
            needs[entry] = jnp.max(jnp.where(row == entry, named, 0.0)).astype(jnp.int32)
    for entry, need in enumerate(needs):
        table_ref[entry] = need
    for copy in large:
        copy.wait()

    def before(tile):
        if tile % PART == 0:
            parts[tile // PART].wait()

    def store(tile, state):
        new_ref[tile] = state
        new_rounded_ref[tile] = state.astype(jnp.bfloat16)

    update_tiles(
        table_ref, state_ref, extended_ref, target_ref, mixing_ref, blocks_ref, store, before
    )
    pack(place, needs, new_rounded_ref, own_ref, layer_ref)


def design_sum(table_ref, state_ref, derivative_ref, weights_ref, sum_ref):
    owners = sum_ref.shape[0] // FB_DEV
    rows = NOBJ * NDIR
    slots = weights_ref.shape[0]
    sum_ref[...] = jnp.zeros(sum_ref.shape, jnp.float32)
    for slot in range(slots):
        selected = state_ref[table_ref[NEEDS + slot]]
        pieces = []
        for k in range(NDIR):
            total = None
            for v in range(NVAR):
                term = (
                    selected[v * NOBJ : (v + 1) * NOBJ, :]
                    * derivative_ref[v * NDIR + k, slot : slot + 1, :]
                )
                total = term if total is None else total + term
            pieces.append(total)
        alive = slot < table_ref[NEEDS + 2 * slots]
        sensitivity = jnp.where(alive, jnp.concatenate(pieces, axis=0), 0.0)
        coarse = sensitivity.astype(jnp.bfloat16).astype(jnp.float32)
        halves = lax.dot_general(
            jnp.concatenate([coarse, sensitivity - coarse], axis=0).astype(jnp.bfloat16),
            weights_ref[slot],
            (((1,), (1,)), ((), ())),
            preferred_element_type=jnp.float32,
        )
        block = table_ref[NEEDS + slots + slot]
        chunk = (block % FB_DEV) * owners + block // FB_DEV
        sum_ref[chunk] = sum_ref[chunk] + (halves[:rows] + halves[rows:])


def sweep_kernel(kind, *refs):
    table_ref, state_ref, rounded_ref, halo_ref, target_ref, mixing_ref, blocks_ref = refs[:7]
    refs = list(refs[7:])
    copies = []
    if kind != "middle":
        derivative_hbm, weights_hbm = refs[:2]
        refs = refs[2:]
        sems = refs.pop()
        sum_ref, weights_ref, derivative_ref = refs.pop(), refs.pop(), refs.pop()
        copies.append(pltpu.make_async_copy(derivative_hbm, derivative_ref, sems.at[0]))
        copies.append(pltpu.make_async_copy(weights_hbm, weights_ref, sems.at[1]))
    extended_ref = refs.pop()
    if kind == "last":
        earlier_hbm, adjoint_hbm, chunks_ref = refs[:3]
        new_ref, adjoint_ref = refs[3:]
        half = sum_ref.shape[0]
        copies.append(
            pltpu.make_async_copy(earlier_hbm, chunks_ref.at[pl.ds(0, half)], sems.at[2])
        )
    elif kind == "design":
        partial_hbm, new_ref, new_rounded_ref, own_ref, layer_ref, partial_ref = refs
    else:
        new_ref, new_rounded_ref, own_ref, layer_ref = refs
    for copy in copies:
        copy.start()
    tiles = state_ref.shape[0]
    rows = state_ref.shape[1]
    place = table_ref[PLACE]
    for k, offset in enumerate(OFFSETS):
        source = place - offset
        relayed = jnp.where((source < 0) | (source >= LINE), 1, 0)
        peer = source & (LINE - 1)
        for h in range(HALO):
            start = pl.multiple_of((relayed * HALO + h) * rows, 16)
            extended_ref[tiles + k * HALO + h] = halo_ref[peer, pl.ds(start, rows), :]
    for tile in range(tiles):
        extended_ref[tile] = rounded_ref[tile]

    def store(tile, state):
        new_ref[tile] = state
        if kind == "last":
            for v in range(NVAR):
                part = state[v * NOBJ : (v + 1) * NOBJ, :]
                adjoint_ref[tile, pl.ds(v, NOBJ, stride=NVAR), :] = part
        else:
            new_rounded_ref[tile] = state.astype(jnp.bfloat16)

    update_tiles(table_ref, state_ref, extended_ref, target_ref, mixing_ref, blocks_ref, store)
    if kind == "last":
        written = pltpu.make_async_copy(adjoint_ref, adjoint_hbm, sems.at[3])
        written.start()
    if kind != "middle":
        for copy in copies:
            copy.wait()
        design_sum(table_ref, new_ref, derivative_ref, weights_ref, sum_ref)
    if kind == "design":
        partial_ref[...] = sum_ref[...].astype(jnp.bfloat16)
        written = pltpu.make_async_copy(partial_ref, partial_hbm, sems.at[2])
        written.start()
    if kind == "last":
        chunks_ref[pl.ds(half, half)] = sum_ref[...].astype(jnp.bfloat16)
    else:
        needs = [table_ref[entry] for entry in range(NEEDS)]
        pack(place, needs, new_rounded_ref, own_ref, layer_ref)
    if kind != "middle":
        written.wait()


def in_hbm(value):
    return pltpu.with_memory_space_constraint(value, HBM)


def first_sweep(rows, target, mixing):
    shape = jax.ShapeDtypeStruct(target.shape, jnp.float32)
    payload = jax.ShapeDtypeStruct((target.shape[0] + 1,) + target.shape[1:], jnp.bfloat16)
    return pl.pallas_call(
        first_kernel,
        out_shape=(shape, shape, payload),
        in_specs=specs(HBM, HBM, HBM),
        out_specs=tuple(specs(VMEM, VMEM, VMEM)),
        scratch_shapes=[
            pltpu.SMEM(rows.shape, rows.dtype),
            pltpu.VMEM(target.shape, target.dtype),
            pltpu.VMEM(mixing.shape, mixing.dtype),
            pltpu.SemaphoreType.DMA((3,)),
        ],
        compiler_params=GRANT,
        name="first_sweep",
    )(in_hbm(rows), in_hbm(target), in_hbm(mixing))


def sweep_shapes(state):
    chunk = (HALO * state.shape[1], state.shape[2])
    return (
        jax.ShapeDtypeStruct(state.shape, jnp.float32),
        jax.ShapeDtypeStruct(state.shape, jnp.bfloat16),
        jax.ShapeDtypeStruct((LINE,) + chunk, jnp.bfloat16),
        jax.ShapeDtypeStruct((2,) + chunk, jnp.bfloat16),
    )


def extended_scratch(state):
    return pltpu.VMEM((state.shape[0] + NEEDS,) + state.shape[1:], jnp.bfloat16)


def second_sweep(place, cols, rows, indices, state, payload, sources, target, mixing, blocks):
    table = jax.ShapeDtypeStruct((COLS + cols.size,), jnp.int32)
    small = (cols, rows) + indices[:2]
    kept = [in_hbm(value) for value in small + (mixing, blocks)]
    own = [pltpu.SMEM(value.shape, value.dtype) for value in small]
    own += [pltpu.VMEM(value.shape, value.dtype) for value in (mixing, blocks)]
    tiles = state.shape[0]
    copies = len(own) - 1 + tiles // PART + NEEDS + len(OFFSETS)
    return pl.pallas_call(
        second_kernel,
        out_shape=sweep_shapes(state) + (table,),
        in_specs=specs(*[HBM] * 6, SMEM, SMEM, VMEM, VMEM, *[pl.ANY] * 4, VMEM),
        out_specs=tuple(specs(VMEM, VMEM, VMEM, VMEM, SMEM)),
        scratch_shapes=own
        + [
            extended_scratch(state),
            pltpu.VMEM((len(OFFSETS),) + state.shape[1:], jnp.bfloat16),
            pltpu.SemaphoreType.DMA((copies,)),
        ],
        compiler_params=GRANT,
        name="second_sweep",
    )(*kept, indices[2], place, state, payload, *sources, target)


def sweep(kind, table, state, rounded, halo, target, mixing, blocks, design=()):
    shapes = sweep_shapes(state)
    scratch = [extended_scratch(state)]
    in_specs = specs(SMEM, VMEM, VMEM, VMEM, VMEM, VMEM, VMEM)
    out_specs = specs(VMEM, VMEM, VMEM, VMEM)
    if kind != "middle":
        derivative, weights = design[:2]
        design = [in_hbm(value) for value in design]
        sums = (FB_DEV * lax.axis_size("sub"), NOBJ * NDIR, weights.shape[1])
        extra = [
            pltpu.VMEM(derivative.shape, derivative.dtype),
            pltpu.VMEM(weights.shape, weights.dtype),
            pltpu.VMEM(sums, jnp.float32),
            pltpu.SemaphoreType.DMA((4,)),
        ]
        in_specs += specs(HBM, HBM)
    if kind == "last":
        in_specs += specs(HBM)
        chunks = jax.ShapeDtypeStruct((OUTER * sums[0],) + sums[1:], jnp.bfloat16)
        shapes = (shapes[0], chunks)
        out_specs = specs(HBM, VMEM)
        full = pltpu.VMEM(state.shape, jnp.float32)
        scratch = [full, full] + scratch + extra
    elif kind == "design":
        shapes = (HBM(sums, jnp.bfloat16),) + shapes
        out_specs = specs(HBM) + out_specs
        scratch = [pltpu.VMEM(sums, jnp.bfloat16)] + scratch + extra
    return pl.pallas_call(
        functools.partial(sweep_kernel, kind),
        out_shape=shapes,
        in_specs=in_specs,
        out_specs=tuple(out_specs),
        scratch_shapes=scratch,
        compiler_params=GRANT,
        name="sweep_" + kind,
    )(table, state, rounded, halo, target, mixing, blocks, *design)


def exchange(own, layer):
    count = lax.axis_size("dom")
    steps = [LINE if source % LINE >= 2 else -LINE for source in range(count)]
    pairs = [(source, (source + step) % count) for source, step in enumerate(steps)]
    relayed = lax.ppermute(layer, "dom", pairs)
    chunks = jnp.concatenate([own, jnp.concatenate([relayed, relayed], axis=0)], axis=1)
    lines = [[start + x for x in range(LINE)] for start in range(0, count, LINE)]
    return lax.all_to_all(chunks, "dom", 0, 0, axis_index_groups=lines)


def reduce_design(chunks, scaling):
    dom, sub = lax.axis_size("dom"), lax.axis_size("sub")
    part = OUTER * FB_DEV
    slabs = dom // part
    wide = part * sub
    groups = [[slab * wide + i for i in range(wide)] for slab in range(slabs)]
    spread = lax.all_to_all(chunks, ("dom", "sub"), 0, 0, axis_index_groups=groups)
    mine = jnp.sum(spread.astype(jnp.float32), axis=0)
    groups = [[slab * part + i for slab in range(slabs)] for i in range(part)]
    copies = jnp.broadcast_to(mine[None], (slabs,) + mine.shape)
    stacked = lax.all_to_all(copies, "dom", 0, 0, axis_index_groups=groups)
    total = jnp.sum(stacked, axis=0) * scaling
    groups = [[slab * part + i for i in range(part)] for slab in range(slabs)]
    copies = jnp.broadcast_to(total[None], (part,) + total.shape)
    gathered = lax.all_to_all(copies, "dom", 0, 0, axis_index_groups=groups)
    split = gathered.reshape(OUTER, FB_DEV, NDIR, NOBJ, gathered.shape[-1])
    return split.swapaxes(2, 3).reshape(OUTER, FB_DEV, NOBJ * NDIR, gathered.shape[-1])


def per_device(
    jac_blocks,
    block_cols,
    precond,
    right_side,
    halo_rows,
    surface_tile,
    surface_block,
    surface_count,
    surface_residual_derivative,
    lattice_bernstein_weights,
):
    slot_count = surface_tile.shape[0]
    scaling = math.sqrt(FB_DEV / (slot_count * lax.axis_size("dom")))
    cols = block_cols.T
    rows = halo_rows.T
    place = (lax.axis_index("dom") % LINE).astype(jnp.int32).reshape(1)
    indices = (surface_tile, surface_block, surface_count)
    design = (surface_residual_derivative.transpose(1, 0, 2), lattice_bernstein_weights)
    target, state, payload = first_sweep(rows, right_side, precond)
    sources = [from_behind(payload, "dom", offset) for offset in OFFSETS]
    state, rounded, own, layer, table = second_sweep(
        place, cols, rows, indices, state, payload, sources, target, precond, jac_blocks
    )
    count = OUTER * INNER
    for number in range(2, count):
        halo = exchange(own, layer)
        arrays = (table, state, rounded, halo, target, precond, jac_blocks)
        if number == count - 1:
            adjoint, chunks = sweep("last", *arrays, design + (partial,))
        elif number == INNER - 1:
            partial, state, rounded, own, layer = sweep("design", *arrays, design)
        else:
            state, rounded, own, layer = sweep("middle", *arrays)
    return (adjoint, reduce_design(chunks, scaling))


def solution(mesh):
    in_specs = (
        P(("dom", "sub"), None, None, None),
        P(("dom", "sub"), None),
        P(("dom", "sub"), None, None),
        P(("dom", "sub"), None, None),
        P(("dom", "sub"), None),
        P(("dom", "sub")),
        P(("dom", "sub")),
        P(("dom", "sub")),
        P(("dom", "sub"), None, None),
        P(("dom", "sub"), None, None),
    )
    out_specs = (P(("dom", "sub"), None, None), P(None, "sub", None, None))
    return jax.shard_map(
        per_device, mesh=mesh, in_specs=in_specs, out_specs=out_specs, check_vma=False
    )
```

time: 241 us -> 225 us (0.934)
  the two profiles are of different devices: /device:TPU:32 before, /device:TPU:2 now
where the time goes in v2:
time: 225 us
  blocking collectives  130 us (58%)
  starting transfers between devices  45.5 us (20%)
  waiting for transfers between devices  30.4 us (14%)
  Pallas kernels  16.6 us (7%)
    all_to_all x8, blocking collectives, exchange(): return lax.all_to_all(chunks, 'dom', 0, 0, axis_index_groups=lines)  81.8 us
    ppermute x8, starting transfers between devices, exchange(): relayed = lax.ppermute(layer, 'dom', pairs)  24.8 us
    ppermute x8, waiting for transfers between devices, exchange(): relayed = lax.ppermute(layer, 'dom', pairs)  23 us
    all_to_all x1, blocking collectives, reduce_design(): stacked = lax.all_to_all(copies, 'dom', 0, 0, axis_index_groups=groups)  21.4 us
    ppermute x4, starting transfers between devices, from_behind(): return lax.ppermute(value, axis, pairs)  20.7 us
    all_to_all x1, blocking collectives, reduce_design(): lax.all_to_all(chunks, ('dom', 'sub'), 0, 0, axis_index_groups=groups)  16.5 us
    pallas_call x8, Pallas kernels, sweep(): pl.pallas_call(functools.partial(sweep_kernel, kind), out_shape=shapes, i...  12.5 us
    all_to_all x1, blocking collectives, reduce_design(): gathered = lax.all_to_all(copies, 'dom', 0, 0, axis_index_groups=groups)  9.75 us
  transfers between devices with their start and end apart: 12, of which 11 were waited for; matrix products, arithmetic and copies ran while one was open for 0% of the time, Pallas kernels for 0%

profile of v2, /device:TPU:2, one launch (start us, length us, event | category | flops | bytes accessed | tf_op | source)
XLA Modules:
  0.0 224.5 jit_solution(14147663133089621953)
XLA Ops:
  0.6 1.2 first_sweep.1
  1.8 13.0 %collective-permute-start.3 = (bf16[13,48,128]{2,1,0:T(8,128)(2,1)S(1)}, bf16[13,48,128]{2,1,0:T(8,128)(2,1)S(1)}, u32[]{:S(2)}, u32[]{:S(2)}) collective-permute-start(bf16[13,48,128]{2,1,0:T(8,128)(2,1)S(1)} %get-tuple-element.42.rounded_ref), channel_id=1, source_target_pairs={{0,496},{8,504},{16,0},{24,8},{32,16},{40,24},{48,32},{56,40},{64,... | collective-permute-start | bytes 479240 | tf_op jit(solution)/shard_map/ppermute | solution.py:39
  14.8 1.9 collective-permute-start.2
  16.7 3.3 %collective-permute-start.1 = (bf16[13,48,128]{2,1,0:T(8,128)(2,1)S(1)}, bf16[13,48,128]{2,1,0:T(8,128)(2,1)S(1)}, u32[]{:S(2)}, u32[]{:S(2)}) collective-permute-start(bf16[13,48,128]{2,1,0:T(8,128)(2,1)S(1)} %get-tuple-element.42.rounded_ref), channel_id=1, source_target_pairs={{0,504},{8,0},{16,8},{24,16},{32,24},{40,32},{48,40},{56,48},{64,5... | collective-permute-start | bytes 479240 | tf_op jit(solution)/shard_map/ppermute | solution.py:39
  20.1 2.5 %collective-permute-start = (bf16[13,48,128]{2,1,0:T(8,128)(2,1)S(1)}, bf16[13,48,128]{2,1,0:T(8,128)(2,1)S(1)}, u32[]{:S(2)}, u32[]{:S(2)}) collective-permute-start(bf16[13,48,128]{2,1,0:T(8,128)(2,1)S(1)} %get-tuple-element.42.rounded_ref), channel_id=1, source_target_pairs={{0,8},{8,16},{16,24},{24,32},{32,40},{40,48},{48,56},{56,64},{64,7... | collective-permute-start | bytes 479240 | tf_op jit(solution)/shard_map/ppermute | solution.py:39
  23.3 0.0 collective-permute-done.3.from3_ref
  23.3 2.7 %collective-permute-done.2.from2_ref = bf16[13,48,128]{2,1,0:T(8,128)(2,1)S(1)} collective-permute-done((bf16[13,48,128]{2,1,0:T(8,128)(2,1)S(1)}, bf16[13,48,128]{2,1,0:T(8,128)(2,1)S(1)}, u32[]{:S(2)}, u32[]{:S(2)}) %collective-permute-start.2) | collective-permute-done | bytes 159776 | tf_op jit(solution)/shard_map/ppermute | solution.py:39
  26.0 1.6 collective-permute-done.1.from1_ref
  27.6 3.0 %collective-permute-done.from0_ref = bf16[13,48,128]{2,1,0:T(8,128)(2,1)S(1)} collective-permute-done((bf16[13,48,128]{2,1,0:T(8,128)(2,1)S(1)}, bf16[13,48,128]{2,1,0:T(8,128)(2,1)S(1)}, u32[]{:S(2)}, u32[]{:S(2)}) %collective-permute-start) | collective-permute-done | bytes 159776 | tf_op jit(solution)/shard_map/ppermute | solution.py:39
  30.6 0.0 copy-start
  30.6 0.0 copy-start.1
  30.6 2.9 %second_sweep.1 = (f32[12,48,128]{2,1,0:T(8,128)S(1)}, bf16[12,48,128]{2,1,0:T(8,128)(2,1)S(1)}, bf16[4,96,128]{2,1,0:T(8,128)(2,1)S(1)}, bf16[2,96,128]{2,1,0:T(8,128)(2,1)S(1)}, s32[104]{0:T(128)S(1)}) custom-call(s32[6,12]{1,0:T(8,128)} %bitcast.12, s32[2,4]{1,0:T(2,128)} %bitcast.14, s32[8]{0:T(128)} %tile_hbm.1, s32[8]{0:T(128)} %block_hbm.1, ...), custom_call_target="tpu_custom_call" | custom-call | tf_op jit(solution)/shard_map/second_sweep/pallas_call | solution.py:385
  33.6 1.9 collective-permute-start.4
  35.5 4.1 %collective-permute-done.4 = bf16[2,96,128]{2,1,0:T(8,128)(2,1)S(1)} collective-permute-done((bf16[2,96,128]{2,1,0:T(8,128)(2,1)S(1)}, bf16[2,96,128]{2,1,0:T(8,128)(2,1)S(1)}, u32[]{:S(2)}, u32[]{:S(2)}) %collective-permute-start.4) | collective-permute-done | bytes 49184 | tf_op jit(solution)/shard_map/ppermute | solution.py:443
  39.6 12.5 %all_to_all.55.refs_3_ = bf16[4,192,128]{2,1,0:T(8,128)(2,1)S(1)} all-to-all(bf16[4,192,128]{2,1,0:T(8,128)(2,1)S(1)} %maximum_maximum_fusion), channel_id=1, replica_groups={{0,8,16,24},{32,40,48,56},{64,72,80,88},{96,104,112,120},{128,136,144,1..., dimensions={0} | all-to-all | bytes 393216 | tf_op jit(solution)/shard_map/all_to_all | solution.py:446
  52.1 0.0 copy-done
  52.1 0.0 copy-done.1
  52.1 1.2 sweep_middle.6
  53.3 3.1 %collective-permute-start.5 = (bf16[2,96,128]{2,1,0:T(8,128)(2,1)S(1)}, bf16[2,96,128]{2,1,0:T(8,128)(2,1)S(1)}, u32[]{:S(2)}, u32[]{:S(2)}) collective-permute-start(bf16[2,96,128]{2,1,0:T(8,128)(2,1)S(1)} %get-tuple-element.52), channel_id=1, source_target_pairs={{0,480},{8,488},{16,48},{24,56},{32,0},{40,8},{48,80},{56,88},{64,... | collective-permute-start | bytes 147464 | tf_op jit(solution)/shard_map/ppermute | solution.py:443
  56.4 2.8 %collective-permute-done.5 = bf16[2,96,128]{2,1,0:T(8,128)(2,1)S(1)} collective-permute-done((bf16[2,96,128]{2,1,0:T(8,128)(2,1)S(1)}, bf16[2,96,128]{2,1,0:T(8,128)(2,1)S(1)}, u32[]{:S(2)}, u32[]{:S(2)}) %collective-permute-start.5) | collective-permute-done | bytes 49184 | tf_op jit(solution)/shard_map/ppermute | solution.py:443
  59.3 9.8 %all_to_all.56.refs_3_ = bf16[4,192,128]{2,1,0:T(8,128)(2,1)S(1)} all-to-all(bf16[4,192,128]{2,1,0:T(8,128)(2,1)S(1)} %maximum_maximum_fusion.1), channel_id=1, replica_groups={{0,8,16,24},{32,40,48,56},{64,72,80,88},{96,104,112,120},{128,136,144,1..., dimensions={0} | all-to-all | bytes 393216 | tf_op jit(solution)/shard_map/all_to_all | solution.py:446
  69.1 1.2 sweep_middle.7
  70.2 3.3 %collective-permute-start.6 = (bf16[2,96,128]{2,1,0:T(8,128)(2,1)S(1)}, bf16[2,96,128]{2,1,0:T(8,128)(2,1)S(1)}, u32[]{:S(2)}, u32[]{:S(2)}) collective-permute-start(bf16[2,96,128]{2,1,0:T(8,128)(2,1)S(1)} %get-tuple-element.56), channel_id=1, source_target_pairs={{0,480},{8,488},{16,48},{24,56},{32,0},{40,8},{48,80},{56,88},{64,... | collective-permute-start | bytes 147464 | tf_op jit(solution)/shard_map/ppermute | solution.py:443
  73.5 2.7 %collective-permute-done.6 = bf16[2,96,128]{2,1,0:T(8,128)(2,1)S(1)} collective-permute-done((bf16[2,96,128]{2,1,0:T(8,128)(2,1)S(1)}, bf16[2,96,128]{2,1,0:T(8,128)(2,1)S(1)}, u32[]{:S(2)}, u32[]{:S(2)}) %collective-permute-start.6) | collective-permute-done | bytes 49184 | tf_op jit(solution)/shard_map/ppermute | solution.py:443
  76.3 9.8 %all_to_all.57.refs_3_ = bf16[4,192,128]{2,1,0:T(8,128)(2,1)S(1)} all-to-all(bf16[4,192,128]{2,1,0:T(8,128)(2,1)S(1)} %maximum_maximum_fusion.2), channel_id=1, replica_groups={{0,8,16,24},{32,40,48,56},{64,72,80,88},{96,104,112,120},{128,136,144,1..., dimensions={0} | all-to-all | bytes 393216 | tf_op jit(solution)/shard_map/all_to_all | solution.py:446
  86.0 3.1 %sweep_design.1 = (bf16[32,24,128]{2,1,0:T(8,128)(2,1)}, f32[12,48,128]{2,1,0:T(8,128)S(1)}, bf16[12,48,128]{2,1,0:T(8,128)(2,1)S(1)}, bf16[4,96,128]{2,1,0:T(8,128)(2,1)S(1)}, bf16[2,96,128]{2,1,0:T(8,128)(2,1)S(1)}) custom-call(s32[104]{0:T(128)S(1)} %get-tuple-element.44.refs_0_, f32[12,48,128]{2,1,0:T(8,128)S(1)} %get-tuple-element.53.refs_1_, ...), custom_call_target="tpu_custom_call" | custom-call | tf_op jit(solution)/shard_map/sweep_design/pallas_call | solution.py:428
  89.1 3.4 %collective-permute-start.7 = (bf16[2,96,128]{2,1,0:T(8,128)(2,1)S(1)}, bf16[2,96,128]{2,1,0:T(8,128)(2,1)S(1)}, u32[]{:S(2)}, u32[]{:S(2)}) collective-permute-start(bf16[2,96,128]{2,1,0:T(8,128)(2,1)S(1)} %get-tuple-element.60), channel_id=1, source_target_pairs={{0,480},{8,488},{16,48},{24,56},{32,0},{40,8},{48,80},{56,88},{64,... | collective-permute-start | bytes 147464 | tf_op jit(solution)/shard_map/ppermute | solution.py:443
  92.5 2.6 %collective-permute-done.7 = bf16[2,96,128]{2,1,0:T(8,128)(2,1)S(1)} collective-permute-done((bf16[2,96,128]{2,1,0:T(8,128)(2,1)S(1)}, bf16[2,96,128]{2,1,0:T(8,128)(2,1)S(1)}, u32[]{:S(2)}, u32[]{:S(2)}) %collective-permute-start.7) | collective-permute-done | bytes 49184 | tf_op jit(solution)/shard_map/ppermute | solution.py:443
  95.1 9.8 %all_to_all.58.refs_3_ = bf16[4,192,128]{2,1,0:T(8,128)(2,1)S(1)} all-to-all(bf16[4,192,128]{2,1,0:T(8,128)(2,1)S(1)} %maximum_maximum_fusion.3), channel_id=1, replica_groups={{0,8,16,24},{32,40,48,56},{64,72,80,88},{96,104,112,120},{128,136,144,1..., dimensions={0} | all-to-all | bytes 393216 | tf_op jit(solution)/shard_map/all_to_all | solution.py:446
  104.9 1.2 sweep_middle.8
  106.0 3.5 %collective-permute-start.8 = (bf16[2,96,128]{2,1,0:T(8,128)(2,1)S(1)}, bf16[2,96,128]{2,1,0:T(8,128)(2,1)S(1)}, u32[]{:S(2)}, u32[]{:S(2)}) collective-permute-start(bf16[2,96,128]{2,1,0:T(8,128)(2,1)S(1)} %get-tuple-element.64), channel_id=1, source_target_pairs={{0,480},{8,488},{16,48},{24,56},{32,0},{40,8},{48,80},{56,88},{64,... | collective-permute-start | bytes 147464 | tf_op jit(solution)/shard_map/ppermute | solution.py:443
  109.6 2.4 %collective-permute-done.8 = bf16[2,96,128]{2,1,0:T(8,128)(2,1)S(1)} collective-permute-done((bf16[2,96,128]{2,1,0:T(8,128)(2,1)S(1)}, bf16[2,96,128]{2,1,0:T(8,128)(2,1)S(1)}, u32[]{:S(2)}, u32[]{:S(2)}) %collective-permute-start.8) | collective-permute-done | bytes 49184 | tf_op jit(solution)/shard_map/ppermute | solution.py:443
  112.1 10.7 %all_to_all.59.refs_3_ = bf16[4,192,128]{2,1,0:T(8,128)(2,1)S(1)} all-to-all(bf16[4,192,128]{2,1,0:T(8,128)(2,1)S(1)} %maximum_maximum_fusion.4), channel_id=1, replica_groups={{0,8,16,24},{32,40,48,56},{64,72,80,88},{96,104,112,120},{128,136,144,1..., dimensions={0} | all-to-all | bytes 393216 | tf_op jit(solution)/shard_map/all_to_all | solution.py:446
  122.8 1.2 sweep_middle.9
  123.9 2.8 %collective-permute-start.9 = (bf16[2,96,128]{2,1,0:T(8,128)(2,1)S(1)}, bf16[2,96,128]{2,1,0:T(8,128)(2,1)S(1)}, u32[]{:S(2)}, u32[]{:S(2)}) collective-permute-start(bf16[2,96,128]{2,1,0:T(8,128)(2,1)S(1)} %get-tuple-element.68), channel_id=1, source_target_pairs={{0,480},{8,488},{16,48},{24,56},{32,0},{40,8},{48,80},{56,88},{64,... | collective-permute-start | bytes 147464 | tf_op jit(solution)/shard_map/ppermute | solution.py:443
  126.7 3.2 %collective-permute-done.9 = bf16[2,96,128]{2,1,0:T(8,128)(2,1)S(1)} collective-permute-done((bf16[2,96,128]{2,1,0:T(8,128)(2,1)S(1)}, bf16[2,96,128]{2,1,0:T(8,128)(2,1)S(1)}, u32[]{:S(2)}, u32[]{:S(2)}) %collective-permute-start.9) | collective-permute-done | bytes 49184 | tf_op jit(solution)/shard_map/ppermute | solution.py:443
  129.9 9.8 %all_to_all.60.refs_3_ = bf16[4,192,128]{2,1,0:T(8,128)(2,1)S(1)} all-to-all(bf16[4,192,128]{2,1,0:T(8,128)(2,1)S(1)} %maximum_maximum_fusion.5), channel_id=1, replica_groups={{0,8,16,24},{32,40,48,56},{64,72,80,88},{96,104,112,120},{128,136,144,1..., dimensions={0} | all-to-all | bytes 393216 | tf_op jit(solution)/shard_map/all_to_all | solution.py:446
  139.7 1.2 sweep_middle.10
  140.9 3.3 %collective-permute-start.10 = (bf16[2,96,128]{2,1,0:T(8,128)(2,1)S(1)}, bf16[2,96,128]{2,1,0:T(8,128)(2,1)S(1)}, u32[]{:S(2)}, u32[]{:S(2)}) collective-permute-start(bf16[2,96,128]{2,1,0:T(8,128)(2,1)S(1)} %get-tuple-element.72), channel_id=1, source_target_pairs={{0,480},{8,488},{16,48},{24,56},{32,0},{40,8},{48,80},{56,88},{64,... | collective-permute-start | bytes 147464 | tf_op jit(solution)/shard_map/ppermute | solution.py:443
  144.2 2.7 %collective-permute-done.10 = bf16[2,96,128]{2,1,0:T(8,128)(2,1)S(1)} collective-permute-done((bf16[2,96,128]{2,1,0:T(8,128)(2,1)S(1)}, bf16[2,96,128]{2,1,0:T(8,128)(2,1)S(1)}, u32[]{:S(2)}, u32[]{:S(2)}) %collective-permute-start.10) | collective-permute-done | bytes 49184 | tf_op jit(solution)/shard_map/ppermute | solution.py:443
  146.9 9.8 %all_to_all.61.refs_3_ = bf16[4,192,128]{2,1,0:T(8,128)(2,1)S(1)} all-to-all(bf16[4,192,128]{2,1,0:T(8,128)(2,1)S(1)} %maximum_maximum_fusion.6), channel_id=1, replica_groups={{0,8,16,24},{32,40,48,56},{64,72,80,88},{96,104,112,120},{128,136,144,1..., dimensions={0} | all-to-all | bytes 393216 | tf_op jit(solution)/shard_map/all_to_all | solution.py:446
  156.7 1.2 sweep_middle.11
  157.8 3.4 %collective-permute-start.11 = (bf16[2,96,128]{2,1,0:T(8,128)(2,1)S(1)}, bf16[2,96,128]{2,1,0:T(8,128)(2,1)S(1)}, u32[]{:S(2)}, u32[]{:S(2)}) collective-permute-start(bf16[2,96,128]{2,1,0:T(8,128)(2,1)S(1)} %get-tuple-element.76), channel_id=1, source_target_pairs={{0,480},{8,488},{16,48},{24,56},{32,0},{40,8},{48,80},{56,88},{64,... | collective-permute-start | bytes 147464 | tf_op jit(solution)/shard_map/ppermute | solution.py:443
  161.3 2.5 %collective-permute-done.11 = bf16[2,96,128]{2,1,0:T(8,128)(2,1)S(1)} collective-permute-done((bf16[2,96,128]{2,1,0:T(8,128)(2,1)S(1)}, bf16[2,96,128]{2,1,0:T(8,128)(2,1)S(1)}, u32[]{:S(2)}, u32[]{:S(2)}) %collective-permute-start.11) | collective-permute-done | bytes 49184 | tf_op jit(solution)/shard_map/ppermute | solution.py:443
  163.8 9.8 %all_to_all.62.refs_3_ = bf16[4,192,128]{2,1,0:T(8,128)(2,1)S(1)} all-to-all(bf16[4,192,128]{2,1,0:T(8,128)(2,1)S(1)} %maximum_maximum_fusion.7), channel_id=1, replica_groups={{0,8,16,24},{32,40,48,56},{64,72,80,88},{96,104,112,120},{128,136,144,1..., dimensions={0} | all-to-all | bytes 393216 | tf_op jit(solution)/shard_map/all_to_all | solution.py:446
  173.6 2.4 %sweep_last.1 = (f32[12,48,128]{2,1,0:T(8,128)}, bf16[64,24,128]{2,1,0:T(8,128)(2,1)S(1)}) custom-call(s32[104]{0:T(128)S(1)} %get-tuple-element.44.refs_0_, f32[12,48,128]{2,1,0:T(8,128)S(1)} %get-tuple-element.73.refs_1_, bf16[12,48,128]{2,1,0:T(8,128)(2,1)S(1)} %get-tuple-element.74.refs_2_, bf16[4,192,128]{2,1,0:T(8,128)(2,1)S(1)} %all_to_all.62.refs_3_, ...), custom_call_target="tpu_custom_call" | custom-call | tf_op jit(solution)/shard_map/sweep_last/pallas_call | solution.py:428
  176.0 16.5 %all_to_all.63 = bf16[64,24,128]{2,1,0:T(8,128)(2,1)S(1)} all-to-all(bf16[64,24,128]{2,1,0:T(8,128)(2,1)S(1)} %get-tuple-element.79), channel_id=1, replica_groups={{0,1,2,3,4,5,6,7,8,9,10,11,12,13,14,15,16,17,18,19,20,21,22,23,24,25,26..., dimensions={0} | all-to-all | bytes 786432 | tf_op jit(solution)/shard_map/all_to_all | solution.py:455
  192.5 0.1 convert_reduce_fusion
  192.6 21.4 %all_to_all.64 = f32[8,24,128]{2,1,0:T(8,128)S(1)} all-to-all(f32[8,24,128]{2,1,0:T(8,128)S(1)} %broadcast_in_dim.4), channel_id=1, replica_groups={{0,64,128,192,256,320,384,448},{8,72,136,200,264,328,392,456},{16,80,14..., dimensions={0} | all-to-all | bytes 196608 | tf_op jit(solution)/shard_map/all_to_all | solution.py:459
  214.1 9.7 %all_to_all.65 = f32[8,24,128]{2,1,0:T(8,128)S(1)} all-to-all(f32[8,24,128]{2,1,0:T(8,128)S(1)} %broadcast_in_dim.5), channel_id=1, replica_groups={{0,8,16,24,32,40,48,56},{64,72,80,88,96,104,112,120},{128,136,144,152,1..., dimensions={0} | all-to-all | bytes 196608 | tf_op jit(solution)/shard_map/all_to_all | solution.py:463
  223.9 0.6 copy.15
  (13 shorter events, 0.2 us)
Async XLA Ops:
  1.8 21.4 %collective-permute-start.3 = (bf16[13,48,128]{2,1,0:T(8,128)(2,1)S(1)}, bf16[13,48,128]{2,1,0:T(8,128)(2,1)S(1)}, u32[]{:S(2)}, u32[]{:S(2)}) collective-permute-start(bf16[13,48,128]{2,1,0:T(8,128)(2,1)S(1)} %get-tuple-element.42.rounded_ref), channel_id=1, source_target_pairs={{0,496},{8,504},{16,0},{24,8},{32,16},{40,24},{48,32},{56,40},{64,... | collective-permute-start | bytes 479240 | tf_op jit(solution)/shard_map/ppermute | solution.py:39
  14.8 11.2 %collective-permute-start.2 = (bf16[13,48,128]{2,1,0:T(8,128)(2,1)S(1)}, bf16[13,48,128]{2,1,0:T(8,128)(2,1)S(1)}, u32[]{:S(2)}, u32[]{:S(2)}) collective-permute-start(bf16[13,48,128]{2,1,0:T(8,128)(2,1)S(1)} %get-tuple-element.42.rounded_ref), channel_id=1, source_target_pairs={{0,16},{8,24},{16,32},{24,40},{32,48},{40,56},{48,64},{56,72},{64,... | collective-permute-start | bytes 479240 | tf_op jit(solution)/shard_map/ppermute | solution.py:39
  16.7 10.9 %collective-permute-start.1 = (bf16[13,48,128]{2,1,0:T(8,128)(2,1)S(1)}, bf16[13,48,128]{2,1,0:T(8,128)(2,1)S(1)}, u32[]{:S(2)}, u32[]{:S(2)}) collective-permute-start(bf16[13,48,128]{2,1,0:T(8,128)(2,1)S(1)} %get-tuple-element.42.rounded_ref), channel_id=1, source_target_pairs={{0,504},{8,0},{16,8},{24,16},{32,24},{40,32},{48,40},{56,48},{64,5... | collective-permute-start | bytes 479240 | tf_op jit(solution)/shard_map/ppermute | solution.py:39
  20.1 10.5 %collective-permute-start = (bf16[13,48,128]{2,1,0:T(8,128)(2,1)S(1)}, bf16[13,48,128]{2,1,0:T(8,128)(2,1)S(1)}, u32[]{:S(2)}, u32[]{:S(2)}) collective-permute-start(bf16[13,48,128]{2,1,0:T(8,128)(2,1)S(1)} %get-tuple-element.42.rounded_ref), channel_id=1, source_target_pairs={{0,8},{8,16},{16,24},{24,32},{32,40},{40,48},{48,56},{56,64},{64,7... | collective-permute-start | bytes 479240 | tf_op jit(solution)/shard_map/ppermute | solution.py:39
  30.6 21.5 %copy-start = (bf16[12,6,128,128]{3,2,1,0:T(8,128)(2,1)S(1)}, bf16[12,6,128,128]{3,2,1,0:T(8,128)(2,1)}, u32[]{:S(2)}) copy-start(bf16[12,6,128,128]{3,2,1,0:T(8,128)(2,1)} %refs_6_.15) | copy-start | bytes 7077892
  30.6 21.5 %copy-start.1 = (f32[12,36,128]{2,1,0:T(8,128)S(1)}, f32[12,36,128]{2,1,0:T(8,128)}, u32[]{:S(2)}) copy-start(f32[12,36,128]{2,1,0:T(8,128)} %refs_5_.15) | copy-start | bytes 663556
  33.6 6.0 %collective-permute-start.4 = (bf16[2,96,128]{2,1,0:T(8,128)(2,1)S(1)}, bf16[2,96,128]{2,1,0:T(8,128)(2,1)S(1)}, u32[]{:S(2)}, u32[]{:S(2)}) collective-permute-start(bf16[2,96,128]{2,1,0:T(8,128)(2,1)S(1)} %get-tuple-element.48), channel_id=1, source_target_pairs={{0,480},{8,488},{16,48},{24,56},{32,0},{40,8},{48,80},{56,88},{64,... | collective-permute-start | bytes 147464 | tf_op jit(solution)/shard_map/ppermute | solution.py:443
  53.3 6.0 %collective-permute-start.5 = (bf16[2,96,128]{2,1,0:T(8,128)(2,1)S(1)}, bf16[2,96,128]{2,1,0:T(8,128)(2,1)S(1)}, u32[]{:S(2)}, u32[]{:S(2)}) collective-permute-start(bf16[2,96,128]{2,1,0:T(8,128)(2,1)S(1)} %get-tuple-element.52), channel_id=1, source_target_pairs={{0,480},{8,488},{16,48},{24,56},{32,0},{40,8},{48,80},{56,88},{64,... | collective-permute-start | bytes 147464 | tf_op jit(solution)/shard_map/ppermute | solution.py:443
  70.2 6.0 %collective-permute-start.6 = (bf16[2,96,128]{2,1,0:T(8,128)(2,1)S(1)}, bf16[2,96,128]{2,1,0:T(8,128)(2,1)S(1)}, u32[]{:S(2)}, u32[]{:S(2)}) collective-permute-start(bf16[2,96,128]{2,1,0:T(8,128)(2,1)S(1)} %get-tuple-element.56), channel_id=1, source_target_pairs={{0,480},{8,488},{16,48},{24,56},{32,0},{40,8},{48,80},{56,88},{64,... | collective-permute-start | bytes 147464 | tf_op jit(solution)/shard_map/ppermute | solution.py:443
  89.1 6.0 %collective-permute-start.7 = (bf16[2,96,128]{2,1,0:T(8,128)(2,1)S(1)}, bf16[2,96,128]{2,1,0:T(8,128)(2,1)S(1)}, u32[]{:S(2)}, u32[]{:S(2)}) collective-permute-start(bf16[2,96,128]{2,1,0:T(8,128)(2,1)S(1)} %get-tuple-element.60), channel_id=1, source_target_pairs={{0,480},{8,488},{16,48},{24,56},{32,0},{40,8},{48,80},{56,88},{64,... | collective-permute-start | bytes 147464 | tf_op jit(solution)/shard_map/ppermute | solution.py:443
  106.0 6.0 %collective-permute-start.8 = (bf16[2,96,128]{2,1,0:T(8,128)(2,1)S(1)}, bf16[2,96,128]{2,1,0:T(8,128)(2,1)S(1)}, u32[]{:S(2)}, u32[]{:S(2)}) collective-permute-start(bf16[2,96,128]{2,1,0:T(8,128)(2,1)S(1)} %get-tuple-element.64), channel_id=1, source_target_pairs={{0,480},{8,488},{16,48},{24,56},{32,0},{40,8},{48,80},{56,88},{64,... | collective-permute-start | bytes 147464 | tf_op jit(solution)/shard_map/ppermute | solution.py:443
  123.9 6.0 %collective-permute-start.9 = (bf16[2,96,128]{2,1,0:T(8,128)(2,1)S(1)}, bf16[2,96,128]{2,1,0:T(8,128)(2,1)S(1)}, u32[]{:S(2)}, u32[]{:S(2)}) collective-permute-start(bf16[2,96,128]{2,1,0:T(8,128)(2,1)S(1)} %get-tuple-element.68), channel_id=1, source_target_pairs={{0,480},{8,488},{16,48},{24,56},{32,0},{40,8},{48,80},{56,88},{64,... | collective-permute-start | bytes 147464 | tf_op jit(solution)/shard_map/ppermute | solution.py:443
  140.9 6.0 %collective-permute-start.10 = (bf16[2,96,128]{2,1,0:T(8,128)(2,1)S(1)}, bf16[2,96,128]{2,1,0:T(8,128)(2,1)S(1)}, u32[]{:S(2)}, u32[]{:S(2)}) collective-permute-start(bf16[2,96,128]{2,1,0:T(8,128)(2,1)S(1)} %get-tuple-element.72), channel_id=1, source_target_pairs={{0,480},{8,488},{16,48},{24,56},{32,0},{40,8},{48,80},{56,88},{64,... | collective-permute-start | bytes 147464 | tf_op jit(solution)/shard_map/ppermute | solution.py:443
  157.8 6.0 %collective-permute-start.11 = (bf16[2,96,128]{2,1,0:T(8,128)(2,1)S(1)}, bf16[2,96,128]{2,1,0:T(8,128)(2,1)S(1)}, u32[]{:S(2)}, u32[]{:S(2)}) collective-permute-start(bf16[2,96,128]{2,1,0:T(8,128)(2,1)S(1)} %get-tuple-element.76), channel_id=1, source_target_pairs={{0,480},{8,488},{16,48},{24,56},{32,0},{40,8},{48,80},{56,88},{64,... | collective-permute-start | bytes 147464 | tf_op jit(solution)/shard_map/ppermute | solution.py:443

commit v3 on v2

--- a/solution.py
+++ b/solution.py
@@ -54,23 +54,53 @@
 
 def first_kernel(
     rows_hbm,
+    cols_hbm,
+    tile_hbm,
+    block_hbm,
     target_hbm,
     mixing_hbm,
+    count_ref,
+    place_ref,
     sorted_ref,
     state_ref,
     payload_ref,
+    table_ref,
     rows_ref,
+    cols_ref,
+    tile_ref,
+    block_ref,
     target_ref,
     mixing_ref,
     sems,
 ):
-    pairs = ((target_hbm, target_ref), (mixing_hbm, mixing_ref), (rows_hbm, rows_ref))
+    pairs = (
+        (target_hbm, target_ref),
+        (mixing_hbm, mixing_ref),
+        (rows_hbm, rows_ref),
+        (cols_hbm, cols_ref),
+        (tile_hbm, tile_ref),
+        (block_hbm, block_ref),
+    )
     copies = [pltpu.make_async_copy(*pair, sems.at[i]) for i, pair in enumerate(pairs)]
     for copy in copies:
         copy.start()
-    for copy in copies:
+    for copy in copies[2:]:
         copy.wait()
-    tiles = target_ref.shape[0]
+    block_count, tiles = cols_ref.shape
+    for tile in range(tiles):
+        for b in range(block_count):
+            table_ref[COLS + tile * block_count + b] = cols_ref[b, tile]
+    slots = tile_ref.shape[0]
+    for slot in range(slots):
+        table_ref[NEEDS + slot] = tile_ref[slot]
+        table_ref[NEEDS + slots + slot] = block_ref[slot]
+    table_ref[NEEDS + 2 * slots] = count_ref[0]
+    table_ref[PLACE] = place_ref[0]
+    for k in range(len(OFFSETS)):
+        for h in range(HALO):
+            table_ref[k * HALO + h] = rows_ref[h, k]
+    for copy in copies[:2]:
+        copy.wait()
     for tile in range(tiles):
         target = jnp.concatenate(
             [target_ref[tile, pl.ds(v, NOBJ, stride=NVAR), :] for v in range(NVAR)], axis=0
@@ -128,14 +158,9 @@
 
 
 def second_kernel(
-    cols_hbm,
-    rows_hbm,
-    tile_hbm,
-    block_hbm,
     mixing_hbm,
     blocks_hbm,
-    count_ref,
-    place_ref,
+    rows_ref,
     state_ref,
     rounded_ref,
     from0_ref,
@@ -148,10 +173,6 @@
     own_ref,
     layer_ref,
     table_ref,
-    cols_ref,
-    rows_ref,
-    tile_ref,
-    block_ref,
     mixing_ref,
     blocks_ref,
     extended_ref,
@@ -159,15 +180,23 @@
     sems,
 ):
     tiles = state_ref.shape[0]
-    small = (
-        (rows_hbm, rows_ref),
-        (cols_hbm, cols_ref),
-        (tile_hbm, tile_ref),
-        (block_hbm, block_ref),
-    )
     number = iter(range(sems.shape[0]))
-    first = [pltpu.make_async_copy(*pair, sems.at[next(number)]) for pair in small]
-    large = [pltpu.make_async_copy(mixing_hbm, mixing_ref, sems.at[next(number)])]
+    sources = (from0_ref, from1_ref, from2_ref, from3_ref)
+    copies = []
+    for k, source_ref in enumerate(sources):
+        copies.append(
+            pltpu.make_async_copy(source_ref.at[tiles], told_ref.at[k], sems.at[next(number)])
+        )
+        for h in range(HALO):
+            entry = k * HALO + h
+            copies.append(
+                pltpu.make_async_copy(
+                    source_ref.at[rows_ref[entry]],
+                    extended_ref.at[tiles + entry],
+                    sems.at[next(number)],
+                )
+            )
+    large = pltpu.make_async_copy(mixing_hbm, mixing_ref, sems.at[next(number)])
     parts = []
     for start in range(0, tiles, PART):
         span = pl.ds(start, PART)
@@ -176,39 +205,12 @@
                 blocks_hbm.at[span], blocks_ref.at[span], sems.at[next(number)]
             )
         )
-    for copy in first + large + parts:
+    for copy in parts + [large] + copies:
         copy.start()
     for tile in range(tiles):
         extended_ref[tile] = rounded_ref[tile]
-    for copy in first:
-        copy.wait()
-    sources = (from0_ref, from1_ref, from2_ref, from3_ref)
-    copies = []
-    for k, source_ref in enumerate(sources):
-        for h in range(HALO):
-            copies.append(
-                pltpu.make_async_copy(
-                    source_ref.at[rows_ref[h, k]],
-                    extended_ref.at[tiles + k * HALO + h],
-                    sems.at[next(number)],
-                )
-            )
-        copies.append(
-            pltpu.make_async_copy(source_ref.at[tiles], told_ref.at[k], sems.at[next(number)])
-        )
-    for copy in copies:
-        copy.start()
-    block_count = blocks_ref.shape[1]
-    for tile in range(tiles):
-        for b in range(block_count):
-            table_ref[COLS + tile * block_count + b] = cols_ref[b, tile]
-    slots = tile_ref.shape[0]
-    for slot in range(slots):
-        table_ref[NEEDS + slot] = tile_ref[slot]
-        table_ref[NEEDS + slots + slot] = block_ref[slot]
-    table_ref[NEEDS + 2 * slots] = count_ref[0]
-    place = place_ref[0]
-    table_ref[PLACE] = place
+    for entry in range(NEEDS, table_ref.shape[0]):
+        table_ref[entry] = rows_ref[entry]
     for copy in copies:
         copy.wait()
     needs = [None] * NEEDS
@@ -221,8 +223,7 @@
             needs[entry] = jnp.max(jnp.where(row == entry, named, 0.0)).astype(jnp.int32)
     for entry, need in enumerate(needs):
         table_ref[entry] = need
-    for copy in large:
-        copy.wait()
+    large.wait()
 
     def before(tile):
         if tile % PART == 0:
@@ -233,9 +234,9 @@
         new_rounded_ref[tile] = state.astype(jnp.bfloat16)
 
     update_tiles(
-        table_ref, state_ref, extended_ref, target_ref, mixing_ref, blocks_ref, store, before
-    )
-    pack(place, needs, new_rounded_ref, own_ref, layer_ref)
+        rows_ref, state_ref, extended_ref, target_ref, mixing_ref, blocks_ref, store, before
+    )
+    pack(rows_ref[PLACE], needs, new_rounded_ref, own_ref, layer_ref)
 
 
 def design_sum(table_ref, state_ref, derivative_ref, weights_ref, sum_ref):
@@ -269,6 +270,27 @@
         sum_ref[chunk] = sum_ref[chunk] + (halves[:rows] + halves[rows:])
 
 
+def design_kernel(
+    table_ref,
+    state_ref,
+    derivative_hbm,
+    weights_hbm,
+    partial_ref,
+    derivative_ref,
+    weights_ref,
+    sum_ref,
+    sems,
+):
+    pairs = ((derivative_hbm, derivative_ref), (weights_hbm, weights_ref))
+    copies = [pltpu.make_async_copy(*pair, sems.at[i]) for i, pair in enumerate(pairs)]
+    for copy in copies:
+        copy.start()
+    for copy in copies:
+        copy.wait()
+    design_sum(table_ref, state_ref, derivative_ref, weights_ref, sum_ref)
+    partial_ref[...] = sum_ref[...].astype(jnp.bfloat16)
+
+
 def sweep_kernel(kind, *refs):
     table_ref, state_ref, rounded_ref, halo_ref, target_ref, mixing_ref, blocks_ref = refs[:7]
     refs = list(refs[7:])
@@ -288,8 +310,6 @@
         copies.append(
             pltpu.make_async_copy(earlier_hbm, chunks_ref.at[pl.ds(0, half)], sems.at[2])
         )
-    elif kind == "design":
-        partial_hbm, new_ref, new_rounded_ref, own_ref, layer_ref, partial_ref = refs
     else:
         new_ref, new_rounded_ref, own_ref, layer_ref = refs
     for copy in copies:
@@ -324,10 +344,6 @@
         for copy in copies:
             copy.wait()
         design_sum(table_ref, new_ref, derivative_ref, weights_ref, sum_ref)
-    if kind == "design":
-        partial_ref[...] = sum_ref[...].astype(jnp.bfloat16)
-        written = pltpu.make_async_copy(partial_ref, partial_hbm, sems.at[2])
-        written.start()
     if kind == "last":
         chunks_ref[pl.ds(half, half)] = sum_ref[...].astype(jnp.bfloat16)
     else:
@@ -341,23 +357,27 @@
     return pltpu.with_memory_space_constraint(value, HBM)
 
 
-def first_sweep(rows, target, mixing):
+def in_smem(value):
+    return pltpu.with_memory_space_constraint(value, SMEM)
+
+
+def first_sweep(place, rows, cols, indices, target, mixing):
     shape = jax.ShapeDtypeStruct(target.shape, jnp.float32)
     payload = jax.ShapeDtypeStruct((target.shape[0] + 1,) + target.shape[1:], jnp.bfloat16)
+    table = SMEM((COLS + cols.size,), jnp.int32)
+    small = (rows, cols) + indices[:2]
+    large = (target, mixing)
     return pl.pallas_call(
         first_kernel,
-        out_shape=(shape, shape, payload),
-        in_specs=specs(HBM, HBM, HBM),
-        out_specs=tuple(specs(VMEM, VMEM, VMEM)),
-        scratch_shapes=[
-            pltpu.SMEM(rows.shape, rows.dtype),
-            pltpu.VMEM(target.shape, target.dtype),
-            pltpu.VMEM(mixing.shape, mixing.dtype),
-            pltpu.SemaphoreType.DMA((3,)),
-        ],
+        out_shape=(shape, shape, payload, table),
+        in_specs=specs(*[HBM] * 6, SMEM, SMEM),
+        out_specs=tuple(specs(VMEM, VMEM, VMEM, SMEM)),
+        scratch_shapes=[pltpu.SMEM(value.shape, value.dtype) for value in small]
+        + [pltpu.VMEM(value.shape, value.dtype) for value in large]
+        + [pltpu.SemaphoreType.DMA((6,))],
         compiler_params=GRANT,
         name="first_sweep",
-    )(in_hbm(rows), in_hbm(target), in_hbm(mixing))
+    )(*[in_hbm(value) for value in small + large], indices[2], place)
 
 
 def sweep_shapes(state):
@@ -374,20 +394,16 @@
     return pltpu.VMEM((state.shape[0] + NEEDS,) + state.shape[1:], jnp.bfloat16)
 
 
-def second_sweep(place, cols, rows, indices, state, payload, sources, target, mixing, blocks):
-    table = jax.ShapeDtypeStruct((COLS + cols.size,), jnp.int32)
-    small = (cols, rows) + indices[:2]
-    kept = [in_hbm(value) for value in small + (mixing, blocks)]
-    own = [pltpu.SMEM(value.shape, value.dtype) for value in small]
-    own += [pltpu.VMEM(value.shape, value.dtype) for value in (mixing, blocks)]
+def second_sweep(table, state, payload, sources, target, mixing, blocks):
+    kept = (mixing, blocks)
     tiles = state.shape[0]
-    copies = len(own) - 1 + tiles // PART + NEEDS + len(OFFSETS)
+    copies = 1 + tiles // PART + NEEDS + len(OFFSETS)
     return pl.pallas_call(
         second_kernel,
-        out_shape=sweep_shapes(state) + (table,),
-        in_specs=specs(*[HBM] * 6, SMEM, SMEM, VMEM, VMEM, *[pl.ANY] * 4, VMEM),
+        out_shape=sweep_shapes(state) + (SMEM(table.shape, table.dtype),),
+        in_specs=specs(HBM, HBM, SMEM, VMEM, VMEM, *[pl.ANY] * 4, VMEM),
         out_specs=tuple(specs(VMEM, VMEM, VMEM, VMEM, SMEM)),
-        scratch_shapes=own
+        scratch_shapes=[pltpu.VMEM(value.shape, value.dtype) for value in kept]
         + [
             extended_scratch(state),
             pltpu.VMEM((len(OFFSETS),) + state.shape[1:], jnp.bfloat16),
@@ -395,7 +411,7 @@
         ],
         compiler_params=GRANT,
         name="second_sweep",
-    )(*kept, indices[2], place, state, payload, *sources, target)
+    )(*[in_hbm(value) for value in kept], in_smem(table), state, payload, *sources, target)
 
 
 def sweep(kind, table, state, rounded, halo, target, mixing, blocks, design=()):
@@ -421,10 +437,6 @@
         out_specs = specs(HBM, VMEM)
         full = pltpu.VMEM(state.shape, jnp.float32)
         scratch = [full, full] + scratch + extra
-    elif kind == "design":
-        shapes = (HBM(sums, jnp.bfloat16),) + shapes
-        out_specs = specs(HBM) + out_specs
-        scratch = [pltpu.VMEM(sums, jnp.bfloat16)] + scratch + extra
     return pl.pallas_call(
         functools.partial(sweep_kernel, kind),
         out_shape=shapes,
@@ -433,17 +445,37 @@
         scratch_shapes=scratch,
         compiler_params=GRANT,
         name="sweep_" + kind,
-    )(table, state, rounded, halo, target, mixing, blocks, *design)
-
-
-def exchange(own, layer):
+    )(in_smem(table), state, rounded, halo, target, mixing, blocks, *design)
+
+
+def design_partial(table, state, derivative, weights):
+    sums = (FB_DEV * lax.axis_size("sub"), NOBJ * NDIR, weights.shape[1])
+    return pl.pallas_call(
+        design_kernel,
+        out_shape=HBM(sums, jnp.bfloat16),
+        in_specs=specs(SMEM, VMEM, HBM, HBM),
+        out_specs=pl.BlockSpec(memory_space=VMEM),
+        scratch_shapes=[
+            pltpu.VMEM(derivative.shape, derivative.dtype),
+            pltpu.VMEM(weights.shape, weights.dtype),
+            pltpu.VMEM(sums, jnp.float32),
+            pltpu.SemaphoreType.DMA((2,)),
+        ],
+        compiler_params=GRANT,
+        name="design_partial",
+    )(in_smem(table), state, in_hbm(derivative), in_hbm(weights))
+
+
+def exchange(own, layer, beside=None):
     count = lax.axis_size("dom")
     steps = [LINE if source % LINE >= 2 else -LINE for source in range(count)]
     pairs = [(source, (source + step) % count) for source, step in enumerate(steps)]
     relayed = lax.ppermute(layer, "dom", pairs)
+    if beside is not None:
+        relayed, beside = lax.optimization_barrier((relayed, beside))
     chunks = jnp.concatenate([own, jnp.concatenate([relayed, relayed], axis=0)], axis=1)
     lines = [[start + x for x in range(LINE)] for start in range(0, count, LINE)]
-    return lax.all_to_all(chunks, "dom", 0, 0, axis_index_groups=lines)
+    return lax.all_to_all(chunks, "dom", 0, 0, axis_index_groups=lines), beside
 
 
 def reduce_design(chunks, scaling):
@@ -484,21 +516,26 @@
     place = (lax.axis_index("dom") % LINE).astype(jnp.int32).reshape(1)
     indices = (surface_tile, surface_block, surface_count)
     design = (surface_residual_derivative.transpose(1, 0, 2), lattice_bernstein_weights)
-    target, state, payload = first_sweep(rows, right_side, precond)
+    target, state, payload, table = first_sweep(
+        place, rows, cols, indices, right_side, precond
+    )
     sources = [from_behind(payload, "dom", offset) for offset in OFFSETS]
     state, rounded, own, layer, table = second_sweep(
-        place, cols, rows, indices, state, payload, sources, target, precond, jac_blocks
+        table, state, payload, sources, target, precond, jac_blocks
     )
     count = OUTER * INNER
     for number in range(2, count):
-        halo = exchange(own, layer)
+        beside = partial if number == INNER else None
+        halo, beside = exchange(own, layer, beside)
+        if beside is not None:
+            partial = beside
         arrays = (table, state, rounded, halo, target, precond, jac_blocks)
         if number == count - 1:
             adjoint, chunks = sweep("last", *arrays, design + (partial,))
-        elif number == INNER - 1:
-            partial, state, rounded, own, layer = sweep("design", *arrays, design)
         else:
             state, rounded, own, layer = sweep("middle", *arrays)
+        if number == INNER - 1:
+            partial = design_partial(table, state, *design)
     return (adjoint, reduce_design(chunks, scaling))
 
 

time: 225 us -> 220 us (0.978)
  Pallas kernels: 16.6 us -> 12.5 us
    pallas_call x8, Pallas kernels: 12.5 us -> 6.29 us  [sweep(): pl.pallas_call(functools.partial(sweep_kernel, kind), out_shape=shapes, i...]
    pallas_call x2 -> x3, Pallas kernels: 4.12 us -> 6.2 us  [the longest x1 2.96 us: second_sweep(): pl.pallas_call(second_kernel, out_shape=sweep_shapes(state) + (SMEM(table...]
  transfers between devices with their start and end apart: 12 -> 12, of which waited for: 11 -> 11; matrix products, arithmetic and copies ran while one was open for 0% -> 0% of each run, Pallas kernels for 0% -> 1%
where the time goes in v3:
time: 220 us; the launch traced here: 219 us
  blocking collectives  130 us (59%)
  starting transfers between devices  45.3 us (21%)
  waiting for transfers between devices  29.2 us (13%)
  Pallas kernels  12.5 us (6%)
    all_to_all x8, blocking collectives, exchange(): lax.all_to_all(chunks, 'dom', 0, 0, axis_index_groups=lines)  81.9 us
    ppermute x8, starting transfers between devices, exchange(): relayed = lax.ppermute(layer, 'dom', pairs)  24.6 us
    all_to_all x1, blocking collectives, reduce_design(): stacked = lax.all_to_all(copies, 'dom', 0, 0, axis_index_groups=groups)  21.6 us
    ppermute x8, waiting for transfers between devices, exchange(): relayed = lax.ppermute(layer, 'dom', pairs)  21.2 us
    ppermute x4, starting transfers between devices, from_behind(): return lax.ppermute(value, axis, pairs)  20.7 us
    all_to_all x1, blocking collectives, reduce_design(): lax.all_to_all(chunks, ('dom', 'sub'), 0, 0, axis_index_groups=groups)  16.4 us
    all_to_all x1, blocking collectives, reduce_design(): gathered = lax.all_to_all(copies, 'dom', 0, 0, axis_index_groups=groups)  9.75 us
    ppermute x4, waiting for transfers between devices, from_behind(): return lax.ppermute(value, axis, pairs)  8.02 us
  transfers between devices with their start and end apart: 12, of which 11 were waited for; matrix products, arithmetic and copies ran while one was open for 0% of the time, Pallas kernels for 1%

profile of v3, /device:TPU:2, one launch (start us, length us, event | category | flops | bytes accessed | tf_op | source)
XLA Modules:
  0.0 219.2 jit_solution(16068402914081150212)
XLA Ops:
  1.3 1.2 first_sweep.1
  2.5 13.0 %collective-permute-start.3 = (bf16[13,48,128]{2,1,0:T(8,128)(2,1)S(1)}, bf16[13,48,128]{2,1,0:T(8,128)(2,1)S(1)}, u32[]{:S(2)}, u32[]{:S(2)}) collective-permute-start(bf16[13,48,128]{2,1,0:T(8,128)(2,1)S(1)} %get-tuple-element.45.rounded_ref), channel_id=1, source_target_pairs={{0,496},{8,504},{16,0},{24,8},{32,16},{40,24},{48,32},{56,40},{64,... | collective-permute-start | bytes 479240 | tf_op jit(solution)/shard_map/ppermute | solution.py:39
  15.5 1.9 collective-permute-start.2
  17.4 3.3 %collective-permute-start.1 = (bf16[13,48,128]{2,1,0:T(8,128)(2,1)S(1)}, bf16[13,48,128]{2,1,0:T(8,128)(2,1)S(1)}, u32[]{:S(2)}, u32[]{:S(2)}) collective-permute-start(bf16[13,48,128]{2,1,0:T(8,128)(2,1)S(1)} %get-tuple-element.45.rounded_ref), channel_id=1, source_target_pairs={{0,504},{8,0},{16,8},{24,16},{32,24},{40,32},{48,40},{56,48},{64,5... | collective-permute-start | bytes 479240 | tf_op jit(solution)/shard_map/ppermute | solution.py:39
  20.8 2.5 %collective-permute-start = (bf16[13,48,128]{2,1,0:T(8,128)(2,1)S(1)}, bf16[13,48,128]{2,1,0:T(8,128)(2,1)S(1)}, u32[]{:S(2)}, u32[]{:S(2)}) collective-permute-start(bf16[13,48,128]{2,1,0:T(8,128)(2,1)S(1)} %get-tuple-element.45.rounded_ref), channel_id=1, source_target_pairs={{0,8},{8,16},{16,24},{24,32},{32,40},{40,48},{48,56},{56,64},{64,7... | collective-permute-start | bytes 479240 | tf_op jit(solution)/shard_map/ppermute | solution.py:39
  23.3 0.0 collective-permute-done.3.from3_ref
  23.3 3.4 %collective-permute-done.2.from2_ref = bf16[13,48,128]{2,1,0:T(8,128)(2,1)S(1)} collective-permute-done((bf16[13,48,128]{2,1,0:T(8,128)(2,1)S(1)}, bf16[13,48,128]{2,1,0:T(8,128)(2,1)S(1)}, u32[]{:S(2)}, u32[]{:S(2)}) %collective-permute-start.2) | collective-permute-done | bytes 159776 | tf_op jit(solution)/shard_map/ppermute | solution.py:39
  26.7 1.6 collective-permute-done.1.from1_ref
  28.3 3.0 %collective-permute-done.from0_ref = bf16[13,48,128]{2,1,0:T(8,128)(2,1)S(1)} collective-permute-done((bf16[13,48,128]{2,1,0:T(8,128)(2,1)S(1)}, bf16[13,48,128]{2,1,0:T(8,128)(2,1)S(1)}, u32[]{:S(2)}, u32[]{:S(2)}) %collective-permute-start) | collective-permute-done | bytes 159776 | tf_op jit(solution)/shard_map/ppermute | solution.py:39
  31.3 0.0 copy-start
  31.3 0.0 copy-start.1
  31.3 3.0 %second_sweep.1 = (f32[12,48,128]{2,1,0:T(8,128)S(1)}, bf16[12,48,128]{2,1,0:T(8,128)(2,1)S(1)}, bf16[4,96,128]{2,1,0:T(8,128)(2,1)S(1)}, bf16[2,96,128]{2,1,0:T(8,128)(2,1)S(1)}, s32[104]{0:T(128)S(4)}) custom-call(f32[12,36,128]{2,1,0:T(8,128)} %refs_5_.15, bf16[12,6,128,128]{3,2,1,0:T(8,128)(2,1)} %refs_6_.15, s32[104]{0:T(128)S(4)} %get-tuple-element.43.rows_ref, ...), custom_call_target="tpu_custom_call" | custom-call | tf_op jit(solution)/shard_map/second_sweep/pallas_call | solution.py:401
  34.3 1.9 collective-permute-start.4
  36.2 4.1 %collective-permute-done.4 = bf16[2,96,128]{2,1,0:T(8,128)(2,1)S(1)} collective-permute-done((bf16[2,96,128]{2,1,0:T(8,128)(2,1)S(1)}, bf16[2,96,128]{2,1,0:T(8,128)(2,1)S(1)}, u32[]{:S(2)}, u32[]{:S(2)}) %collective-permute-start.4) | collective-permute-done | bytes 49184 | tf_op jit(solution)/shard_map/ppermute | solution.py:473
  40.3 12.6 %all_to_all.55.refs_3_ = bf16[4,192,128]{2,1,0:T(8,128)(2,1)S(1)} all-to-all(bf16[4,192,128]{2,1,0:T(8,128)(2,1)S(1)} %maximum_maximum_fusion), channel_id=1, replica_groups={{0,8,16,24},{32,40,48,56},{64,72,80,88},{96,104,112,120},{128,136,144,1..., dimensions={0} | all-to-all | bytes 393216 | tf_op jit(solution)/shard_map/all_to_all | solution.py:478
  52.8 0.0 copy-done
  52.8 0.0 copy-done.1
  52.8 0.6 sweep_middle.7
  53.5 3.1 %collective-permute-start.5 = (bf16[2,96,128]{2,1,0:T(8,128)(2,1)S(1)}, bf16[2,96,128]{2,1,0:T(8,128)(2,1)S(1)}, u32[]{:S(2)}, u32[]{:S(2)}) collective-permute-start(bf16[2,96,128]{2,1,0:T(8,128)(2,1)S(1)} %get-tuple-element.55), channel_id=1, source_target_pairs={{0,480},{8,488},{16,48},{24,56},{32,0},{40,8},{48,80},{56,88},{64,... | collective-permute-start | bytes 147464 | tf_op jit(solution)/shard_map/ppermute | solution.py:473
  56.6 2.8 %collective-permute-done.5 = bf16[2,96,128]{2,1,0:T(8,128)(2,1)S(1)} collective-permute-done((bf16[2,96,128]{2,1,0:T(8,128)(2,1)S(1)}, bf16[2,96,128]{2,1,0:T(8,128)(2,1)S(1)}, u32[]{:S(2)}, u32[]{:S(2)}) %collective-permute-start.5) | collective-permute-done | bytes 49184 | tf_op jit(solution)/shard_map/ppermute | solution.py:473
  59.5 9.8 %all_to_all.56.refs_3_ = bf16[4,192,128]{2,1,0:T(8,128)(2,1)S(1)} all-to-all(bf16[4,192,128]{2,1,0:T(8,128)(2,1)S(1)} %maximum_maximum_fusion.1), channel_id=1, replica_groups={{0,8,16,24},{32,40,48,56},{64,72,80,88},{96,104,112,120},{128,136,144,1..., dimensions={0} | all-to-all | bytes 393216 | tf_op jit(solution)/shard_map/all_to_all | solution.py:478
  69.3 0.6 sweep_middle.8
  69.9 3.3 %collective-permute-start.6 = (bf16[2,96,128]{2,1,0:T(8,128)(2,1)S(1)}, bf16[2,96,128]{2,1,0:T(8,128)(2,1)S(1)}, u32[]{:S(2)}, u32[]{:S(2)}) collective-permute-start(bf16[2,96,128]{2,1,0:T(8,128)(2,1)S(1)} %get-tuple-element.59), channel_id=1, source_target_pairs={{0,480},{8,488},{16,48},{24,56},{32,0},{40,8},{48,80},{56,88},{64,... | collective-permute-start | bytes 147464 | tf_op jit(solution)/shard_map/ppermute | solution.py:473
  73.2 2.7 %collective-permute-done.6 = bf16[2,96,128]{2,1,0:T(8,128)(2,1)S(1)} collective-permute-done((bf16[2,96,128]{2,1,0:T(8,128)(2,1)S(1)}, bf16[2,96,128]{2,1,0:T(8,128)(2,1)S(1)}, u32[]{:S(2)}, u32[]{:S(2)}) %collective-permute-start.6) | collective-permute-done | bytes 49184 | tf_op jit(solution)/shard_map/ppermute | solution.py:473
  75.9 9.8 %all_to_all.57.refs_3_ = bf16[4,192,128]{2,1,0:T(8,128)(2,1)S(1)} all-to-all(bf16[4,192,128]{2,1,0:T(8,128)(2,1)S(1)} %maximum_maximum_fusion.2), channel_id=1, replica_groups={{0,8,16,24},{32,40,48,56},{64,72,80,88},{96,104,112,120},{128,136,144,1..., dimensions={0} | all-to-all | bytes 393216 | tf_op jit(solution)/shard_map/all_to_all | solution.py:478
  85.7 0.6 sweep_middle.9
  86.3 3.4 %collective-permute-start.7 = (bf16[2,96,128]{2,1,0:T(8,128)(2,1)S(1)}, bf16[2,96,128]{2,1,0:T(8,128)(2,1)S(1)}, u32[]{:S(2)}, u32[]{:S(2)}) collective-permute-start(bf16[2,96,128]{2,1,0:T(8,128)(2,1)S(1)} %get-tuple-element.63), channel_id=1, source_target_pairs={{0,480},{8,488},{16,48},{24,56},{32,0},{40,8},{48,80},{56,88},{64,... | collective-permute-start | bytes 147464 | tf_op jit(solution)/shard_map/ppermute | solution.py:473
  89.7 2.0 design_partial.1.refs_9_
  91.8 0.6 collective-permute-done.7
  92.3 9.8 %all_to_all.58.refs_3_ = bf16[4,192,128]{2,1,0:T(8,128)(2,1)S(1)} all-to-all(bf16[4,192,128]{2,1,0:T(8,128)(2,1)S(1)} %maximum_maximum_fusion.3), channel_id=1, replica_groups={{0,8,16,24},{32,40,48,56},{64,72,80,88},{96,104,112,120},{128,136,144,1..., dimensions={0} | all-to-all | bytes 393216 | tf_op jit(solution)/shard_map/all_to_all | solution.py:478
  102.1 0.6 sweep_middle.10
  102.8 3.5 %collective-permute-start.8 = (bf16[2,96,128]{2,1,0:T(8,128)(2,1)S(1)}, bf16[2,96,128]{2,1,0:T(8,128)(2,1)S(1)}, u32[]{:S(2)}, u32[]{:S(2)}) collective-permute-start(bf16[2,96,128]{2,1,0:T(8,128)(2,1)S(1)} %get-tuple-element.68), channel_id=1, source_target_pairs={{0,480},{8,488},{16,48},{24,56},{32,0},{40,8},{48,80},{56,88},{64,... | collective-permute-start | bytes 147464 | tf_op jit(solution)/shard_map/ppermute | solution.py:473
  106.3 2.5 %collective-permute-done.8 = bf16[2,96,128]{2,1,0:T(8,128)(2,1)S(1)} collective-permute-done((bf16[2,96,128]{2,1,0:T(8,128)(2,1)S(1)}, bf16[2,96,128]{2,1,0:T(8,128)(2,1)S(1)}, u32[]{:S(2)}, u32[]{:S(2)}) %collective-permute-start.8) | collective-permute-done | bytes 49184 | tf_op jit(solution)/shard_map/ppermute | solution.py:473
  108.8 10.7 %all_to_all.59.refs_3_ = bf16[4,192,128]{2,1,0:T(8,128)(2,1)S(1)} all-to-all(bf16[4,192,128]{2,1,0:T(8,128)(2,1)S(1)} %maximum_maximum_fusion.4), channel_id=1, replica_groups={{0,8,16,24},{32,40,48,56},{64,72,80,88},{96,104,112,120},{128,136,144,1..., dimensions={0} | all-to-all | bytes 393216 | tf_op jit(solution)/shard_map/all_to_all | solution.py:478
  119.5 0.6 sweep_middle.11
  120.1 2.7 %collective-permute-start.9 = (bf16[2,96,128]{2,1,0:T(8,128)(2,1)S(1)}, bf16[2,96,128]{2,1,0:T(8,128)(2,1)S(1)}, u32[]{:S(2)}, u32[]{:S(2)}) collective-permute-start(bf16[2,96,128]{2,1,0:T(8,128)(2,1)S(1)} %get-tuple-element.72), channel_id=1, source_target_pairs={{0,480},{8,488},{16,48},{24,56},{32,0},{40,8},{48,80},{56,88},{64,... | collective-permute-start | bytes 147464 | tf_op jit(solution)/shard_map/ppermute | solution.py:473
  122.8 3.3 %collective-permute-done.9 = bf16[2,96,128]{2,1,0:T(8,128)(2,1)S(1)} collective-permute-done((bf16[2,96,128]{2,1,0:T(8,128)(2,1)S(1)}, bf16[2,96,128]{2,1,0:T(8,128)(2,1)S(1)}, u32[]{:S(2)}, u32[]{:S(2)}) %collective-permute-start.9) | collective-permute-done | bytes 49184 | tf_op jit(solution)/shard_map/ppermute | solution.py:473
  126.1 9.8 %all_to_all.60.refs_3_ = bf16[4,192,128]{2,1,0:T(8,128)(2,1)S(1)} all-to-all(bf16[4,192,128]{2,1,0:T(8,128)(2,1)S(1)} %maximum_maximum_fusion.5), channel_id=1, replica_groups={{0,8,16,24},{32,40,48,56},{64,72,80,88},{96,104,112,120},{128,136,144,1..., dimensions={0} | all-to-all | bytes 393216 | tf_op jit(solution)/shard_map/all_to_all | solution.py:478
  135.9 0.6 sweep_middle.12
  136.5 3.3 %collective-permute-start.10 = (bf16[2,96,128]{2,1,0:T(8,128)(2,1)S(1)}, bf16[2,96,128]{2,1,0:T(8,128)(2,1)S(1)}, u32[]{:S(2)}, u32[]{:S(2)}) collective-permute-start(bf16[2,96,128]{2,1,0:T(8,128)(2,1)S(1)} %get-tuple-element.76), channel_id=1, source_target_pairs={{0,480},{8,488},{16,48},{24,56},{32,0},{40,8},{48,80},{56,88},{64,... | collective-permute-start | bytes 147464 | tf_op jit(solution)/shard_map/ppermute | solution.py:473
  139.8 2.7 %collective-permute-done.10 = bf16[2,96,128]{2,1,0:T(8,128)(2,1)S(1)} collective-permute-done((bf16[2,96,128]{2,1,0:T(8,128)(2,1)S(1)}, bf16[2,96,128]{2,1,0:T(8,128)(2,1)S(1)}, u32[]{:S(2)}, u32[]{:S(2)}) %collective-permute-start.10) | collective-permute-done | bytes 49184 | tf_op jit(solution)/shard_map/ppermute | solution.py:473
  142.6 9.8 %all_to_all.61.refs_3_ = bf16[4,192,128]{2,1,0:T(8,128)(2,1)S(1)} all-to-all(bf16[4,192,128]{2,1,0:T(8,128)(2,1)S(1)} %maximum_maximum_fusion.6), channel_id=1, replica_groups={{0,8,16,24},{32,40,48,56},{64,72,80,88},{96,104,112,120},{128,136,144,1..., dimensions={0} | all-to-all | bytes 393216 | tf_op jit(solution)/shard_map/all_to_all | solution.py:478
  152.3 0.6 sweep_middle.13
  153.0 3.4 %collective-permute-start.11 = (bf16[2,96,128]{2,1,0:T(8,128)(2,1)S(1)}, bf16[2,96,128]{2,1,0:T(8,128)(2,1)S(1)}, u32[]{:S(2)}, u32[]{:S(2)}) collective-permute-start(bf16[2,96,128]{2,1,0:T(8,128)(2,1)S(1)} %get-tuple-element.80), channel_id=1, source_target_pairs={{0,480},{8,488},{16,48},{24,56},{32,0},{40,8},{48,80},{56,88},{64,... | collective-permute-start | bytes 147464 | tf_op jit(solution)/shard_map/ppermute | solution.py:473
  156.4 2.6 %collective-permute-done.11 = bf16[2,96,128]{2,1,0:T(8,128)(2,1)S(1)} collective-permute-done((bf16[2,96,128]{2,1,0:T(8,128)(2,1)S(1)}, bf16[2,96,128]{2,1,0:T(8,128)(2,1)S(1)}, u32[]{:S(2)}, u32[]{:S(2)}) %collective-permute-start.11) | collective-permute-done | bytes 49184 | tf_op jit(solution)/shard_map/ppermute | solution.py:473
  159.0 9.8 %all_to_all.62.refs_3_ = bf16[4,192,128]{2,1,0:T(8,128)(2,1)S(1)} all-to-all(bf16[4,192,128]{2,1,0:T(8,128)(2,1)S(1)} %maximum_maximum_fusion.7), channel_id=1, replica_groups={{0,8,16,24},{32,40,48,56},{64,72,80,88},{96,104,112,120},{128,136,144,1..., dimensions={0} | all-to-all | bytes 393216 | tf_op jit(solution)/shard_map/all_to_all | solution.py:478
  168.8 1.8 sweep_last.1
  170.6 16.4 %all_to_all.63 = bf16[64,24,128]{2,1,0:T(8,128)(2,1)S(1)} all-to-all(bf16[64,24,128]{2,1,0:T(8,128)(2,1)S(1)} %get-tuple-element.83), channel_id=1, replica_groups={{0,1,2,3,4,5,6,7,8,9,10,11,12,13,14,15,16,17,18,19,20,21,22,23,24,25,26..., dimensions={0} | all-to-all | bytes 786432 | tf_op jit(solution)/shard_map/all_to_all | solution.py:487
  187.0 0.1 convert_reduce_fusion
  187.1 21.6 %all_to_all.64 = f32[8,24,128]{2,1,0:T(8,128)S(1)} all-to-all(f32[8,24,128]{2,1,0:T(8,128)S(1)} %broadcast_in_dim.4), channel_id=1, replica_groups={{0,64,128,192,256,320,384,448},{8,72,136,200,264,328,392,456},{16,80,14..., dimensions={0} | all-to-all | bytes 196608 | tf_op jit(solution)/shard_map/all_to_all | solution.py:491
  208.8 9.7 %all_to_all.65 = f32[8,24,128]{2,1,0:T(8,128)S(1)} all-to-all(f32[8,24,128]{2,1,0:T(8,128)S(1)} %broadcast_in_dim.5), channel_id=1, replica_groups={{0,8,16,24,32,40,48,56},{64,72,80,88,96,104,112,120},{128,136,144,152,1..., dimensions={0} | all-to-all | bytes 196608 | tf_op jit(solution)/shard_map/all_to_all | solution.py:495
  218.6 0.6 copy.15
  (13 shorter events, 0.2 us)
Async XLA Ops:
  2.5 20.8 %collective-permute-start.3 = (bf16[13,48,128]{2,1,0:T(8,128)(2,1)S(1)}, bf16[13,48,128]{2,1,0:T(8,128)(2,1)S(1)}, u32[]{:S(2)}, u32[]{:S(2)}) collective-permute-start(bf16[13,48,128]{2,1,0:T(8,128)(2,1)S(1)} %get-tuple-element.45.rounded_ref), channel_id=1, source_target_pairs={{0,496},{8,504},{16,0},{24,8},{32,16},{40,24},{48,32},{56,40},{64,... | collective-permute-start | bytes 479240 | tf_op jit(solution)/shard_map/ppermute | solution.py:39
  15.5 11.2 %collective-permute-start.2 = (bf16[13,48,128]{2,1,0:T(8,128)(2,1)S(1)}, bf16[13,48,128]{2,1,0:T(8,128)(2,1)S(1)}, u32[]{:S(2)}, u32[]{:S(2)}) collective-permute-start(bf16[13,48,128]{2,1,0:T(8,128)(2,1)S(1)} %get-tuple-element.45.rounded_ref), channel_id=1, source_target_pairs={{0,16},{8,24},{16,32},{24,40},{32,48},{40,56},{48,64},{56,72},{64,... | collective-permute-start | bytes 479240 | tf_op jit(solution)/shard_map/ppermute | solution.py:39
  17.4 10.9 %collective-permute-start.1 = (bf16[13,48,128]{2,1,0:T(8,128)(2,1)S(1)}, bf16[13,48,128]{2,1,0:T(8,128)(2,1)S(1)}, u32[]{:S(2)}, u32[]{:S(2)}) collective-permute-start(bf16[13,48,128]{2,1,0:T(8,128)(2,1)S(1)} %get-tuple-element.45.rounded_ref), channel_id=1, source_target_pairs={{0,504},{8,0},{16,8},{24,16},{32,24},{40,32},{48,40},{56,48},{64,5... | collective-permute-start | bytes 479240 | tf_op jit(solution)/shard_map/ppermute | solution.py:39
  20.8 10.5 %collective-permute-start = (bf16[13,48,128]{2,1,0:T(8,128)(2,1)S(1)}, bf16[13,48,128]{2,1,0:T(8,128)(2,1)S(1)}, u32[]{:S(2)}, u32[]{:S(2)}) collective-permute-start(bf16[13,48,128]{2,1,0:T(8,128)(2,1)S(1)} %get-tuple-element.45.rounded_ref), channel_id=1, source_target_pairs={{0,8},{8,16},{16,24},{24,32},{32,40},{40,48},{48,56},{56,64},{64,7... | collective-permute-start | bytes 479240 | tf_op jit(solution)/shard_map/ppermute | solution.py:39
  31.3 21.5 %copy-start = (bf16[12,6,128,128]{3,2,1,0:T(8,128)(2,1)S(1)}, bf16[12,6,128,128]{3,2,1,0:T(8,128)(2,1)}, u32[]{:S(2)}) copy-start(bf16[12,6,128,128]{3,2,1,0:T(8,128)(2,1)} %refs_6_.15) | copy-start | bytes 7077892
  31.3 21.5 %copy-start.1 = (f32[12,36,128]{2,1,0:T(8,128)S(1)}, f32[12,36,128]{2,1,0:T(8,128)}, u32[]{:S(2)}) copy-start(f32[12,36,128]{2,1,0:T(8,128)} %refs_5_.15) | copy-start | bytes 663556
  34.3 6.0 %collective-permute-start.4 = (bf16[2,96,128]{2,1,0:T(8,128)(2,1)S(1)}, bf16[2,96,128]{2,1,0:T(8,128)(2,1)S(1)}, u32[]{:S(2)}, u32[]{:S(2)}) collective-permute-start(bf16[2,96,128]{2,1,0:T(8,128)(2,1)S(1)} %get-tuple-element.51), channel_id=1, source_target_pairs={{0,480},{8,488},{16,48},{24,56},{32,0},{40,8},{48,80},{56,88},{64,... | collective-permute-start | bytes 147464 | tf_op jit(solution)/shard_map/ppermute | solution.py:473
  53.5 6.0 %collective-permute-start.5 = (bf16[2,96,128]{2,1,0:T(8,128)(2,1)S(1)}, bf16[2,96,128]{2,1,0:T(8,128)(2,1)S(1)}, u32[]{:S(2)}, u32[]{:S(2)}) collective-permute-start(bf16[2,96,128]{2,1,0:T(8,128)(2,1)S(1)} %get-tuple-element.55), channel_id=1, source_target_pairs={{0,480},{8,488},{16,48},{24,56},{32,0},{40,8},{48,80},{56,88},{64,... | collective-permute-start | bytes 147464 | tf_op jit(solution)/shard_map/ppermute | solution.py:473
  69.9 6.0 %collective-permute-start.6 = (bf16[2,96,128]{2,1,0:T(8,128)(2,1)S(1)}, bf16[2,96,128]{2,1,0:T(8,128)(2,1)S(1)}, u32[]{:S(2)}, u32[]{:S(2)}) collective-permute-start(bf16[2,96,128]{2,1,0:T(8,128)(2,1)S(1)} %get-tuple-element.59), channel_id=1, source_target_pairs={{0,480},{8,488},{16,48},{24,56},{32,0},{40,8},{48,80},{56,88},{64,... | collective-permute-start | bytes 147464 | tf_op jit(solution)/shard_map/ppermute | solution.py:473
  86.3 6.0 %collective-permute-start.7 = (bf16[2,96,128]{2,1,0:T(8,128)(2,1)S(1)}, bf16[2,96,128]{2,1,0:T(8,128)(2,1)S(1)}, u32[]{:S(2)}, u32[]{:S(2)}) collective-permute-start(bf16[2,96,128]{2,1,0:T(8,128)(2,1)S(1)} %get-tuple-element.63), channel_id=1, source_target_pairs={{0,480},{8,488},{16,48},{24,56},{32,0},{40,8},{48,80},{56,88},{64,... | collective-permute-start | bytes 147464 | tf_op jit(solution)/shard_map/ppermute | solution.py:473
  102.8 6.0 %collective-permute-start.8 = (bf16[2,96,128]{2,1,0:T(8,128)(2,1)S(1)}, bf16[2,96,128]{2,1,0:T(8,128)(2,1)S(1)}, u32[]{:S(2)}, u32[]{:S(2)}) collective-permute-start(bf16[2,96,128]{2,1,0:T(8,128)(2,1)S(1)} %get-tuple-element.68), channel_id=1, source_target_pairs={{0,480},{8,488},{16,48},{24,56},{32,0},{40,8},{48,80},{56,88},{64,... | collective-permute-start | bytes 147464 | tf_op jit(solution)/shard_map/ppermute | solution.py:473
  120.1 6.0 %collective-permute-start.9 = (bf16[2,96,128]{2,1,0:T(8,128)(2,1)S(1)}, bf16[2,96,128]{2,1,0:T(8,128)(2,1)S(1)}, u32[]{:S(2)}, u32[]{:S(2)}) collective-permute-start(bf16[2,96,128]{2,1,0:T(8,128)(2,1)S(1)} %get-tuple-element.72), channel_id=1, source_target_pairs={{0,480},{8,488},{16,48},{24,56},{32,0},{40,8},{48,80},{56,88},{64,... | collective-permute-start | bytes 147464 | tf_op jit(solution)/shard_map/ppermute | solution.py:473
  136.5 6.0 %collective-permute-start.10 = (bf16[2,96,128]{2,1,0:T(8,128)(2,1)S(1)}, bf16[2,96,128]{2,1,0:T(8,128)(2,1)S(1)}, u32[]{:S(2)}, u32[]{:S(2)}) collective-permute-start(bf16[2,96,128]{2,1,0:T(8,128)(2,1)S(1)} %get-tuple-element.76), channel_id=1, source_target_pairs={{0,480},{8,488},{16,48},{24,56},{32,0},{40,8},{48,80},{56,88},{64,... | collective-permute-start | bytes 147464 | tf_op jit(solution)/shard_map/ppermute | solution.py:473
  153.0 6.0 %collective-permute-start.11 = (bf16[2,96,128]{2,1,0:T(8,128)(2,1)S(1)}, bf16[2,96,128]{2,1,0:T(8,128)(2,1)S(1)}, u32[]{:S(2)}, u32[]{:S(2)}) collective-permute-start(bf16[2,96,128]{2,1,0:T(8,128)(2,1)S(1)} %get-tuple-element.80), channel_id=1, source_target_pairs={{0,480},{8,488},{16,48},{24,56},{32,0},{40,8},{48,80},{56,88},{64,... | collective-permute-start | bytes 147464 | tf_op jit(solution)/shard_map/ppermute | solution.py:473

commit v4 on v3

--- a/solution.py
+++ b/solution.py
@@ -185,7 +185,9 @@
     copies = []
     for k, source_ref in enumerate(sources):
         copies.append(
-            pltpu.make_async_copy(source_ref.at[tiles], told_ref.at[k], sems.at[next(number)])
+            pltpu.make_async_copy(
+                source_ref.at[tiles, pl.ds(0, 16)], told_ref.at[k], sems.at[next(number)]
+            )
         )
         for h in range(HALO):
             entry = k * HALO + h
@@ -205,7 +207,7 @@
                 blocks_hbm.at[span], blocks_ref.at[span], sems.at[next(number)]
             )
         )
-    for copy in parts + [large] + copies:
+    for copy in copies + [large] + parts:
         copy.start()
     for tile in range(tiles):
         extended_ref[tile] = rounded_ref[tile]
@@ -215,7 +217,7 @@
         copy.wait()
     needs = [None] * NEEDS
     for k in range(len(sources)):
-        named = told_ref[k].astype(jnp.float32)
+        named = told_ref[k].astype(jnp.float32)[:NEEDS]
         row = lax.broadcasted_iota(jnp.int32, named.shape, 0)
         told = OFFSETS.index(-OFFSETS[k])
         for h in range(HALO):
@@ -406,7 +408,7 @@
         scratch_shapes=[pltpu.VMEM(value.shape, value.dtype) for value in kept]
         + [
             extended_scratch(state),
-            pltpu.VMEM((len(OFFSETS),) + state.shape[1:], jnp.bfloat16),
+            pltpu.VMEM((len(OFFSETS), 16, state.shape[2]), jnp.bfloat16),
             pltpu.SemaphoreType.DMA((copies,)),
         ],
         compiler_params=GRANT,

time: 220 us -> 220 us (level)
  no operation moved by 1% of the time
where the time goes in v4:
time: 220 us; the launch traced here: 219 us
  blocking collectives  130 us (59%)
  starting transfers between devices  45.4 us (21%)
  waiting for transfers between devices  29.2 us (13%)
  Pallas kernels  12.1 us (6%)
    all_to_all x8, blocking collectives, exchange(): lax.all_to_all(chunks, 'dom', 0, 0, axis_index_groups=lines)  81.9 us
    ppermute x8, starting transfers between devices, exchange(): relayed = lax.ppermute(layer, 'dom', pairs)  24.6 us
    all_to_all x1, blocking collectives, reduce_design(): stacked = lax.all_to_all(copies, 'dom', 0, 0, axis_index_groups=groups)  21.6 us
    ppermute x8, waiting for transfers between devices, exchange(): relayed = lax.ppermute(layer, 'dom', pairs)  21.2 us
    ppermute x4, starting transfers between devices, from_behind(): return lax.ppermute(value, axis, pairs)  20.7 us
    all_to_all x1, blocking collectives, reduce_design(): lax.all_to_all(chunks, ('dom', 'sub'), 0, 0, axis_index_groups=groups)  16.4 us
    all_to_all x1, blocking collectives, reduce_design(): gathered = lax.all_to_all(copies, 'dom', 0, 0, axis_index_groups=groups)  9.75 us
    ppermute x4, waiting for transfers between devices, from_behind(): return lax.ppermute(value, axis, pairs)  8.02 us
  transfers between devices with their start and end apart: 12, of which 11 were waited for; matrix products, arithmetic and copies ran while one was open for 0% of the time, Pallas kernels for 1%

profile of v4, /device:TPU:2, one launch (start us, length us, event | category | flops | bytes accessed | tf_op | source)
XLA Modules:
  0.0 218.8 jit_solution(18109344501179351923)
XLA Ops:
  1.3 1.2 first_sweep.1
  2.5 13.0 %collective-permute-start.3 = (bf16[13,48,128]{2,1,0:T(8,128)(2,1)S(1)}, bf16[13,48,128]{2,1,0:T(8,128)(2,1)S(1)}, u32[]{:S(2)}, u32[]{:S(2)}) collective-permute-start(bf16[13,48,128]{2,1,0:T(8,128)(2,1)S(1)} %get-tuple-element.45.rounded_ref), channel_id=1, source_target_pairs={{0,496},{8,504},{16,0},{24,8},{32,16},{40,24},{48,32},{56,40},{64,... | collective-permute-start | bytes 479240 | tf_op jit(solution)/shard_map/ppermute | solution.py:39
  15.5 1.9 collective-permute-start.2
  17.4 3.3 %collective-permute-start.1 = (bf16[13,48,128]{2,1,0:T(8,128)(2,1)S(1)}, bf16[13,48,128]{2,1,0:T(8,128)(2,1)S(1)}, u32[]{:S(2)}, u32[]{:S(2)}) collective-permute-start(bf16[13,48,128]{2,1,0:T(8,128)(2,1)S(1)} %get-tuple-element.45.rounded_ref), channel_id=1, source_target_pairs={{0,504},{8,0},{16,8},{24,16},{32,24},{40,32},{48,40},{56,48},{64,5... | collective-permute-start | bytes 479240 | tf_op jit(solution)/shard_map/ppermute | solution.py:39
  20.8 2.5 %collective-permute-start = (bf16[13,48,128]{2,1,0:T(8,128)(2,1)S(1)}, bf16[13,48,128]{2,1,0:T(8,128)(2,1)S(1)}, u32[]{:S(2)}, u32[]{:S(2)}) collective-permute-start(bf16[13,48,128]{2,1,0:T(8,128)(2,1)S(1)} %get-tuple-element.45.rounded_ref), channel_id=1, source_target_pairs={{0,8},{8,16},{16,24},{24,32},{32,40},{40,48},{48,56},{56,64},{64,7... | collective-permute-start | bytes 479240 | tf_op jit(solution)/shard_map/ppermute | solution.py:39
  23.3 0.0 collective-permute-done.3.from3_ref
  23.3 3.4 %collective-permute-done.2.from2_ref = bf16[13,48,128]{2,1,0:T(8,128)(2,1)S(1)} collective-permute-done((bf16[13,48,128]{2,1,0:T(8,128)(2,1)S(1)}, bf16[13,48,128]{2,1,0:T(8,128)(2,1)S(1)}, u32[]{:S(2)}, u32[]{:S(2)}) %collective-permute-start.2) | collective-permute-done | bytes 159776 | tf_op jit(solution)/shard_map/ppermute | solution.py:39
  26.7 1.6 collective-permute-done.1.from1_ref
  28.3 3.0 %collective-permute-done.from0_ref = bf16[13,48,128]{2,1,0:T(8,128)(2,1)S(1)} collective-permute-done((bf16[13,48,128]{2,1,0:T(8,128)(2,1)S(1)}, bf16[13,48,128]{2,1,0:T(8,128)(2,1)S(1)}, u32[]{:S(2)}, u32[]{:S(2)}) %collective-permute-start) | collective-permute-done | bytes 159776 | tf_op jit(solution)/shard_map/ppermute | solution.py:39
  31.3 0.0 copy-start
  31.3 0.0 copy-start.1
  31.3 2.6 %second_sweep.1 = (f32[12,48,128]{2,1,0:T(8,128)S(1)}, bf16[12,48,128]{2,1,0:T(8,128)(2,1)S(1)}, bf16[4,96,128]{2,1,0:T(8,128)(2,1)S(1)}, bf16[2,96,128]{2,1,0:T(8,128)(2,1)S(1)}, s32[104]{0:T(128)S(4)}) custom-call(f32[12,36,128]{2,1,0:T(8,128)} %refs_5_.15, bf16[12,6,128,128]{3,2,1,0:T(8,128)(2,1)} %refs_6_.15, s32[104]{0:T(128)S(4)} %get-tuple-element.43.rows_ref, ...), custom_call_target="tpu_custom_call" | custom-call | tf_op jit(solution)/shard_map/second_sweep/pallas_call | solution.py:403
  33.9 1.9 collective-permute-start.4
  35.9 4.1 %collective-permute-done.4 = bf16[2,96,128]{2,1,0:T(8,128)(2,1)S(1)} collective-permute-done((bf16[2,96,128]{2,1,0:T(8,128)(2,1)S(1)}, bf16[2,96,128]{2,1,0:T(8,128)(2,1)S(1)}, u32[]{:S(2)}, u32[]{:S(2)}) %collective-permute-start.4) | collective-permute-done | bytes 49184 | tf_op jit(solution)/shard_map/ppermute | solution.py:475
  39.9 12.6 %all_to_all.55.refs_3_ = bf16[4,192,128]{2,1,0:T(8,128)(2,1)S(1)} all-to-all(bf16[4,192,128]{2,1,0:T(8,128)(2,1)S(1)} %maximum_maximum_fusion), channel_id=1, replica_groups={{0,8,16,24},{32,40,48,56},{64,72,80,88},{96,104,112,120},{128,136,144,1..., dimensions={0} | all-to-all | bytes 393216 | tf_op jit(solution)/shard_map/all_to_all | solution.py:480
  52.5 0.0 copy-done
  52.5 0.0 copy-done.1
  52.5 0.6 sweep_middle.7
  53.1 3.1 %collective-permute-start.5 = (bf16[2,96,128]{2,1,0:T(8,128)(2,1)S(1)}, bf16[2,96,128]{2,1,0:T(8,128)(2,1)S(1)}, u32[]{:S(2)}, u32[]{:S(2)}) collective-permute-start(bf16[2,96,128]{2,1,0:T(8,128)(2,1)S(1)} %get-tuple-element.55), channel_id=1, source_target_pairs={{0,480},{8,488},{16,48},{24,56},{32,0},{40,8},{48,80},{56,88},{64,... | collective-permute-start | bytes 147464 | tf_op jit(solution)/shard_map/ppermute | solution.py:475
  56.3 2.8 %collective-permute-done.5 = bf16[2,96,128]{2,1,0:T(8,128)(2,1)S(1)} collective-permute-done((bf16[2,96,128]{2,1,0:T(8,128)(2,1)S(1)}, bf16[2,96,128]{2,1,0:T(8,128)(2,1)S(1)}, u32[]{:S(2)}, u32[]{:S(2)}) %collective-permute-start.5) | collective-permute-done | bytes 49184 | tf_op jit(solution)/shard_map/ppermute | solution.py:475
  59.2 9.8 %all_to_all.56.refs_3_ = bf16[4,192,128]{2,1,0:T(8,128)(2,1)S(1)} all-to-all(bf16[4,192,128]{2,1,0:T(8,128)(2,1)S(1)} %maximum_maximum_fusion.1), channel_id=1, replica_groups={{0,8,16,24},{32,40,48,56},{64,72,80,88},{96,104,112,120},{128,136,144,1..., dimensions={0} | all-to-all | bytes 393216 | tf_op jit(solution)/shard_map/all_to_all | solution.py:480
  68.9 0.6 sweep_middle.8
  69.6 3.3 %collective-permute-start.6 = (bf16[2,96,128]{2,1,0:T(8,128)(2,1)S(1)}, bf16[2,96,128]{2,1,0:T(8,128)(2,1)S(1)}, u32[]{:S(2)}, u32[]{:S(2)}) collective-permute-start(bf16[2,96,128]{2,1,0:T(8,128)(2,1)S(1)} %get-tuple-element.59), channel_id=1, source_target_pairs={{0,480},{8,488},{16,48},{24,56},{32,0},{40,8},{48,80},{56,88},{64,... | collective-permute-start | bytes 147464 | tf_op jit(solution)/shard_map/ppermute | solution.py:475
  72.8 2.7 %collective-permute-done.6 = bf16[2,96,128]{2,1,0:T(8,128)(2,1)S(1)} collective-permute-done((bf16[2,96,128]{2,1,0:T(8,128)(2,1)S(1)}, bf16[2,96,128]{2,1,0:T(8,128)(2,1)S(1)}, u32[]{:S(2)}, u32[]{:S(2)}) %collective-permute-start.6) | collective-permute-done | bytes 49184 | tf_op jit(solution)/shard_map/ppermute | solution.py:475
  75.6 9.8 %all_to_all.57.refs_3_ = bf16[4,192,128]{2,1,0:T(8,128)(2,1)S(1)} all-to-all(bf16[4,192,128]{2,1,0:T(8,128)(2,1)S(1)} %maximum_maximum_fusion.2), channel_id=1, replica_groups={{0,8,16,24},{32,40,48,56},{64,72,80,88},{96,104,112,120},{128,136,144,1..., dimensions={0} | all-to-all | bytes 393216 | tf_op jit(solution)/shard_map/all_to_all | solution.py:480
  85.4 0.6 sweep_middle.9
  86.0 3.4 %collective-permute-start.7 = (bf16[2,96,128]{2,1,0:T(8,128)(2,1)S(1)}, bf16[2,96,128]{2,1,0:T(8,128)(2,1)S(1)}, u32[]{:S(2)}, u32[]{:S(2)}) collective-permute-start(bf16[2,96,128]{2,1,0:T(8,128)(2,1)S(1)} %get-tuple-element.63), channel_id=1, source_target_pairs={{0,480},{8,488},{16,48},{24,56},{32,0},{40,8},{48,80},{56,88},{64,... | collective-permute-start | bytes 147464 | tf_op jit(solution)/shard_map/ppermute | solution.py:475
  89.4 2.0 design_partial.1.refs_9_
  91.4 0.6 collective-permute-done.7
  92.0 9.8 %all_to_all.58.refs_3_ = bf16[4,192,128]{2,1,0:T(8,128)(2,1)S(1)} all-to-all(bf16[4,192,128]{2,1,0:T(8,128)(2,1)S(1)} %maximum_maximum_fusion.3), channel_id=1, replica_groups={{0,8,16,24},{32,40,48,56},{64,72,80,88},{96,104,112,120},{128,136,144,1..., dimensions={0} | all-to-all | bytes 393216 | tf_op jit(solution)/shard_map/all_to_all | solution.py:480
  101.8 0.6 sweep_middle.10
  102.4 3.5 %collective-permute-start.8 = (bf16[2,96,128]{2,1,0:T(8,128)(2,1)S(1)}, bf16[2,96,128]{2,1,0:T(8,128)(2,1)S(1)}, u32[]{:S(2)}, u32[]{:S(2)}) collective-permute-start(bf16[2,96,128]{2,1,0:T(8,128)(2,1)S(1)} %get-tuple-element.68), channel_id=1, source_target_pairs={{0,480},{8,488},{16,48},{24,56},{32,0},{40,8},{48,80},{56,88},{64,... | collective-permute-start | bytes 147464 | tf_op jit(solution)/shard_map/ppermute | solution.py:475
  106.0 2.5 %collective-permute-done.8 = bf16[2,96,128]{2,1,0:T(8,128)(2,1)S(1)} collective-permute-done((bf16[2,96,128]{2,1,0:T(8,128)(2,1)S(1)}, bf16[2,96,128]{2,1,0:T(8,128)(2,1)S(1)}, u32[]{:S(2)}, u32[]{:S(2)}) %collective-permute-start.8) | collective-permute-done | bytes 49184 | tf_op jit(solution)/shard_map/ppermute | solution.py:475
  108.5 10.7 %all_to_all.59.refs_3_ = bf16[4,192,128]{2,1,0:T(8,128)(2,1)S(1)} all-to-all(bf16[4,192,128]{2,1,0:T(8,128)(2,1)S(1)} %maximum_maximum_fusion.4), channel_id=1, replica_groups={{0,8,16,24},{32,40,48,56},{64,72,80,88},{96,104,112,120},{128,136,144,1..., dimensions={0} | all-to-all | bytes 393216 | tf_op jit(solution)/shard_map/all_to_all | solution.py:480
  119.1 0.6 sweep_middle.11
  119.8 2.7 %collective-permute-start.9 = (bf16[2,96,128]{2,1,0:T(8,128)(2,1)S(1)}, bf16[2,96,128]{2,1,0:T(8,128)(2,1)S(1)}, u32[]{:S(2)}, u32[]{:S(2)}) collective-permute-start(bf16[2,96,128]{2,1,0:T(8,128)(2,1)S(1)} %get-tuple-element.72), channel_id=1, source_target_pairs={{0,480},{8,488},{16,48},{24,56},{32,0},{40,8},{48,80},{56,88},{64,... | collective-permute-start | bytes 147464 | tf_op jit(solution)/shard_map/ppermute | solution.py:475
  122.5 3.3 %collective-permute-done.9 = bf16[2,96,128]{2,1,0:T(8,128)(2,1)S(1)} collective-permute-done((bf16[2,96,128]{2,1,0:T(8,128)(2,1)S(1)}, bf16[2,96,128]{2,1,0:T(8,128)(2,1)S(1)}, u32[]{:S(2)}, u32[]{:S(2)}) %collective-permute-start.9) | collective-permute-done | bytes 49184 | tf_op jit(solution)/shard_map/ppermute | solution.py:475
  125.8 9.8 %all_to_all.60.refs_3_ = bf16[4,192,128]{2,1,0:T(8,128)(2,1)S(1)} all-to-all(bf16[4,192,128]{2,1,0:T(8,128)(2,1)S(1)} %maximum_maximum_fusion.5), channel_id=1, replica_groups={{0,8,16,24},{32,40,48,56},{64,72,80,88},{96,104,112,120},{128,136,144,1..., dimensions={0} | all-to-all | bytes 393216 | tf_op jit(solution)/shard_map/all_to_all | solution.py:480
  135.6 0.6 sweep_middle.12
  136.2 3.3 %collective-permute-start.10 = (bf16[2,96,128]{2,1,0:T(8,128)(2,1)S(1)}, bf16[2,96,128]{2,1,0:T(8,128)(2,1)S(1)}, u32[]{:S(2)}, u32[]{:S(2)}) collective-permute-start(bf16[2,96,128]{2,1,0:T(8,128)(2,1)S(1)} %get-tuple-element.76), channel_id=1, source_target_pairs={{0,480},{8,488},{16,48},{24,56},{32,0},{40,8},{48,80},{56,88},{64,... | collective-permute-start | bytes 147464 | tf_op jit(solution)/shard_map/ppermute | solution.py:475
  139.5 2.7 %collective-permute-done.10 = bf16[2,96,128]{2,1,0:T(8,128)(2,1)S(1)} collective-permute-done((bf16[2,96,128]{2,1,0:T(8,128)(2,1)S(1)}, bf16[2,96,128]{2,1,0:T(8,128)(2,1)S(1)}, u32[]{:S(2)}, u32[]{:S(2)}) %collective-permute-start.10) | collective-permute-done | bytes 49184 | tf_op jit(solution)/shard_map/ppermute | solution.py:475
  142.2 9.8 %all_to_all.61.refs_3_ = bf16[4,192,128]{2,1,0:T(8,128)(2,1)S(1)} all-to-all(bf16[4,192,128]{2,1,0:T(8,128)(2,1)S(1)} %maximum_maximum_fusion.6), channel_id=1, replica_groups={{0,8,16,24},{32,40,48,56},{64,72,80,88},{96,104,112,120},{128,136,144,1..., dimensions={0} | all-to-all | bytes 393216 | tf_op jit(solution)/shard_map/all_to_all | solution.py:480
  152.0 0.6 sweep_middle.13
  152.7 3.4 %collective-permute-start.11 = (bf16[2,96,128]{2,1,0:T(8,128)(2,1)S(1)}, bf16[2,96,128]{2,1,0:T(8,128)(2,1)S(1)}, u32[]{:S(2)}, u32[]{:S(2)}) collective-permute-start(bf16[2,96,128]{2,1,0:T(8,128)(2,1)S(1)} %get-tuple-element.80), channel_id=1, source_target_pairs={{0,480},{8,488},{16,48},{24,56},{32,0},{40,8},{48,80},{56,88},{64,... | collective-permute-start | bytes 147464 | tf_op jit(solution)/shard_map/ppermute | solution.py:475
  156.1 2.6 %collective-permute-done.11 = bf16[2,96,128]{2,1,0:T(8,128)(2,1)S(1)} collective-permute-done((bf16[2,96,128]{2,1,0:T(8,128)(2,1)S(1)}, bf16[2,96,128]{2,1,0:T(8,128)(2,1)S(1)}, u32[]{:S(2)}, u32[]{:S(2)}) %collective-permute-start.11) | collective-permute-done | bytes 49184 | tf_op jit(solution)/shard_map/ppermute | solution.py:475
  158.7 9.8 %all_to_all.62.refs_3_ = bf16[4,192,128]{2,1,0:T(8,128)(2,1)S(1)} all-to-all(bf16[4,192,128]{2,1,0:T(8,128)(2,1)S(1)} %maximum_maximum_fusion.7), channel_id=1, replica_groups={{0,8,16,24},{32,40,48,56},{64,72,80,88},{96,104,112,120},{128,136,144,1..., dimensions={0} | all-to-all | bytes 393216 | tf_op jit(solution)/shard_map/all_to_all | solution.py:480
  168.4 1.8 sweep_last.1
  170.3 16.4 %all_to_all.63 = bf16[64,24,128]{2,1,0:T(8,128)(2,1)S(1)} all-to-all(bf16[64,24,128]{2,1,0:T(8,128)(2,1)S(1)} %get-tuple-element.83), channel_id=1, replica_groups={{0,1,2,3,4,5,6,7,8,9,10,11,12,13,14,15,16,17,18,19,20,21,22,23,24,25,26..., dimensions={0} | all-to-all | bytes 786432 | tf_op jit(solution)/shard_map/all_to_all | solution.py:489
  186.7 0.1 convert_reduce_fusion
  186.8 21.6 %all_to_all.64 = f32[8,24,128]{2,1,0:T(8,128)S(1)} all-to-all(f32[8,24,128]{2,1,0:T(8,128)S(1)} %broadcast_in_dim.4), channel_id=1, replica_groups={{0,64,128,192,256,320,384,448},{8,72,136,200,264,328,392,456},{16,80,14..., dimensions={0} | all-to-all | bytes 196608 | tf_op jit(solution)/shard_map/all_to_all | solution.py:493
  208.4 9.7 %all_to_all.65 = f32[8,24,128]{2,1,0:T(8,128)S(1)} all-to-all(f32[8,24,128]{2,1,0:T(8,128)S(1)} %broadcast_in_dim.5), channel_id=1, replica_groups={{0,8,16,24,32,40,48,56},{64,72,80,88,96,104,112,120},{128,136,144,152,1..., dimensions={0} | all-to-all | bytes 196608 | tf_op jit(solution)/shard_map/all_to_all | solution.py:497
  218.2 0.6 copy.15
  (13 shorter events, 0.2 us)
Async XLA Ops:
  2.5 20.8 %collective-permute-start.3 = (bf16[13,48,128]{2,1,0:T(8,128)(2,1)S(1)}, bf16[13,48,128]{2,1,0:T(8,128)(2,1)S(1)}, u32[]{:S(2)}, u32[]{:S(2)}) collective-permute-start(bf16[13,48,128]{2,1,0:T(8,128)(2,1)S(1)} %get-tuple-element.45.rounded_ref), channel_id=1, source_target_pairs={{0,496},{8,504},{16,0},{24,8},{32,16},{40,24},{48,32},{56,40},{64,... | collective-permute-start | bytes 479240 | tf_op jit(solution)/shard_map/ppermute | solution.py:39
  15.5 11.2 %collective-permute-start.2 = (bf16[13,48,128]{2,1,0:T(8,128)(2,1)S(1)}, bf16[13,48,128]{2,1,0:T(8,128)(2,1)S(1)}, u32[]{:S(2)}, u32[]{:S(2)}) collective-permute-start(bf16[13,48,128]{2,1,0:T(8,128)(2,1)S(1)} %get-tuple-element.45.rounded_ref), channel_id=1, source_target_pairs={{0,16},{8,24},{16,32},{24,40},{32,48},{40,56},{48,64},{56,72},{64,... | collective-permute-start | bytes 479240 | tf_op jit(solution)/shard_map/ppermute | solution.py:39
  17.4 10.9 %collective-permute-start.1 = (bf16[13,48,128]{2,1,0:T(8,128)(2,1)S(1)}, bf16[13,48,128]{2,1,0:T(8,128)(2,1)S(1)}, u32[]{:S(2)}, u32[]{:S(2)}) collective-permute-start(bf16[13,48,128]{2,1,0:T(8,128)(2,1)S(1)} %get-tuple-element.45.rounded_ref), channel_id=1, source_target_pairs={{0,504},{8,0},{16,8},{24,16},{32,24},{40,32},{48,40},{56,48},{64,5... | collective-permute-start | bytes 479240 | tf_op jit(solution)/shard_map/ppermute | solution.py:39
  20.8 10.5 %collective-permute-start = (bf16[13,48,128]{2,1,0:T(8,128)(2,1)S(1)}, bf16[13,48,128]{2,1,0:T(8,128)(2,1)S(1)}, u32[]{:S(2)}, u32[]{:S(2)}) collective-permute-start(bf16[13,48,128]{2,1,0:T(8,128)(2,1)S(1)} %get-tuple-element.45.rounded_ref), channel_id=1, source_target_pairs={{0,8},{8,16},{16,24},{24,32},{32,40},{40,48},{48,56},{56,64},{64,7... | collective-permute-start | bytes 479240 | tf_op jit(solution)/shard_map/ppermute | solution.py:39
  31.3 21.2 %copy-start = (bf16[12,6,128,128]{3,2,1,0:T(8,128)(2,1)S(1)}, bf16[12,6,128,128]{3,2,1,0:T(8,128)(2,1)}, u32[]{:S(2)}) copy-start(bf16[12,6,128,128]{3,2,1,0:T(8,128)(2,1)} %refs_6_.15) | copy-start | bytes 7077892
  31.3 21.2 %copy-start.1 = (f32[12,36,128]{2,1,0:T(8,128)S(1)}, f32[12,36,128]{2,1,0:T(8,128)}, u32[]{:S(2)}) copy-start(f32[12,36,128]{2,1,0:T(8,128)} %refs_5_.15) | copy-start | bytes 663556
  33.9 6.0 %collective-permute-start.4 = (bf16[2,96,128]{2,1,0:T(8,128)(2,1)S(1)}, bf16[2,96,128]{2,1,0:T(8,128)(2,1)S(1)}, u32[]{:S(2)}, u32[]{:S(2)}) collective-permute-start(bf16[2,96,128]{2,1,0:T(8,128)(2,1)S(1)} %get-tuple-element.51), channel_id=1, source_target_pairs={{0,480},{8,488},{16,48},{24,56},{32,0},{40,8},{48,80},{56,88},{64,... | collective-permute-start | bytes 147464 | tf_op jit(solution)/shard_map/ppermute | solution.py:475
  53.1 6.0 %collective-permute-start.5 = (bf16[2,96,128]{2,1,0:T(8,128)(2,1)S(1)}, bf16[2,96,128]{2,1,0:T(8,128)(2,1)S(1)}, u32[]{:S(2)}, u32[]{:S(2)}) collective-permute-start(bf16[2,96,128]{2,1,0:T(8,128)(2,1)S(1)} %get-tuple-element.55), channel_id=1, source_target_pairs={{0,480},{8,488},{16,48},{24,56},{32,0},{40,8},{48,80},{56,88},{64,... | collective-permute-start | bytes 147464 | tf_op jit(solution)/shard_map/ppermute | solution.py:475
  69.6 6.0 %collective-permute-start.6 = (bf16[2,96,128]{2,1,0:T(8,128)(2,1)S(1)}, bf16[2,96,128]{2,1,0:T(8,128)(2,1)S(1)}, u32[]{:S(2)}, u32[]{:S(2)}) collective-permute-start(bf16[2,96,128]{2,1,0:T(8,128)(2,1)S(1)} %get-tuple-element.59), channel_id=1, source_target_pairs={{0,480},{8,488},{16,48},{24,56},{32,0},{40,8},{48,80},{56,88},{64,... | collective-permute-start | bytes 147464 | tf_op jit(solution)/shard_map/ppermute | solution.py:475
  86.0 6.0 %collective-permute-start.7 = (bf16[2,96,128]{2,1,0:T(8,128)(2,1)S(1)}, bf16[2,96,128]{2,1,0:T(8,128)(2,1)S(1)}, u32[]{:S(2)}, u32[]{:S(2)}) collective-permute-start(bf16[2,96,128]{2,1,0:T(8,128)(2,1)S(1)} %get-tuple-element.63), channel_id=1, source_target_pairs={{0,480},{8,488},{16,48},{24,56},{32,0},{40,8},{48,80},{56,88},{64,... | collective-permute-start | bytes 147464 | tf_op jit(solution)/shard_map/ppermute | solution.py:475
  102.4 6.0 %collective-permute-start.8 = (bf16[2,96,128]{2,1,0:T(8,128)(2,1)S(1)}, bf16[2,96,128]{2,1,0:T(8,128)(2,1)S(1)}, u32[]{:S(2)}, u32[]{:S(2)}) collective-permute-start(bf16[2,96,128]{2,1,0:T(8,128)(2,1)S(1)} %get-tuple-element.68), channel_id=1, source_target_pairs={{0,480},{8,488},{16,48},{24,56},{32,0},{40,8},{48,80},{56,88},{64,... | collective-permute-start | bytes 147464 | tf_op jit(solution)/shard_map/ppermute | solution.py:475
  119.8 6.0 %collective-permute-start.9 = (bf16[2,96,128]{2,1,0:T(8,128)(2,1)S(1)}, bf16[2,96,128]{2,1,0:T(8,128)(2,1)S(1)}, u32[]{:S(2)}, u32[]{:S(2)}) collective-permute-start(bf16[2,96,128]{2,1,0:T(8,128)(2,1)S(1)} %get-tuple-element.72), channel_id=1, source_target_pairs={{0,480},{8,488},{16,48},{24,56},{32,0},{40,8},{48,80},{56,88},{64,... | collective-permute-start | bytes 147464 | tf_op jit(solution)/shard_map/ppermute | solution.py:475
  136.2 6.0 %collective-permute-start.10 = (bf16[2,96,128]{2,1,0:T(8,128)(2,1)S(1)}, bf16[2,96,128]{2,1,0:T(8,128)(2,1)S(1)}, u32[]{:S(2)}, u32[]{:S(2)}) collective-permute-start(bf16[2,96,128]{2,1,0:T(8,128)(2,1)S(1)} %get-tuple-element.76), channel_id=1, source_target_pairs={{0,480},{8,488},{16,48},{24,56},{32,0},{40,8},{48,80},{56,88},{64,... | collective-permute-start | bytes 147464 | tf_op jit(solution)/shard_map/ppermute | solution.py:475
  152.7 6.0 %collective-permute-start.11 = (bf16[2,96,128]{2,1,0:T(8,128)(2,1)S(1)}, bf16[2,96,128]{2,1,0:T(8,128)(2,1)S(1)}, u32[]{:S(2)}, u32[]{:S(2)}) collective-permute-start(bf16[2,96,128]{2,1,0:T(8,128)(2,1)S(1)} %get-tuple-element.80), channel_id=1, source_target_pairs={{0,480},{8,488},{16,48},{24,56},{32,0},{40,8},{48,80},{56,88},{64,... | collective-permute-start | bytes 147464 | tf_op jit(solution)/shard_map/ppermute | solution.py:475
